TPU v7x, 32 devices: a whole 2x2x4 slice. The times are simulated.
32 devices in a mesh: section: 2 (over x), dp: 16 (over z, y, core).
Axes of the slice: x: 2, y: 2, z: 4, core: 2. Of those that a mesh axis runs over, the one named last changes fastest.
Arguments:
- states_in: bfloat16 [3072, 1536], P('dp'), may hold values from -6 to 6
- out_grad: bfloat16 [3072, 1536], P('dp'), may hold values from -6 to 6
- counts: int32 [32], P('dp'), may hold values from 24 to 96
- segments: int32 [32, 96], P('dp'), may hold values from 0 to 3, never falling along the last dimension, each value on 1 to 48 neighbouring positions
- mixing: float32 [2, 2, 2], P('section'), may hold values from -2.5 to 2.5
- correction: float32 [2, 2], P('section'), may hold values from 0.5 to 1.5
- gain_attn: float32 [2, 768], P('section'), may hold values from 0.1 to 1.9
- w_query: bfloat16 [2, 768, 768], P('section'), may hold values from -0.3125 to 0.3125
- w_key: bfloat16 [2, 768, 768], P('section'), may hold values from -0.3125 to 0.3125
- w_value: bfloat16 [2, 768, 768], P('section'), may hold values from -0.21875 to 0.21875
- w_attn_out: bfloat16 [2, 768, 768], P('section'), may hold values from -0.4375 to 0.4375
- gain_ffn: float32 [2, 768], P('section'), may hold values from 0.1 to 1.9
- w_gate: bfloat16 [2, 768, 3072], P('section'), may hold values from -0.21875 to 0.21875
- w_up: bfloat16 [2, 768, 3072], P('section'), may hold values from -0.21875 to 0.21875
- w_down: bfloat16 [2, 3072, 768], P('section'), may hold values from -0.15625 to 0.15625
Outputs:
- states: bfloat16 [2, 3072, 1536], P('section', 'dp')
- state_grads: bfloat16 [2, 3072, 1536], P('section', 'dp')
- grad_mixing: float32 [2, 2, 2], P('section')
- grad_correction: float32 [2, 2], P('section')
- grad_gain_attn: float32 [2, 768], P('section', 'dp')
- grad_query: float32 [2, 768, 768], P('section', 'dp')
- grad_key: float32 [2, 768, 768], P('section', 'dp')
- grad_value: float32 [2, 768, 768], P('section', 'dp')
- grad_attn_out: float32 [2, 768, 768], P('section', 'dp')
- grad_gain_ffn: float32 [2, 768], P('section', 'dp')
- grad_gate: float32 [2, 768, 3072], P('section', 'dp')
- grad_up: float32 [2, 768, 3072], P('section', 'dp')
- grad_down: float32 [2, 3072, 768], P('section', 'dp')
Inputs may be any that keep to these rules, and one draw needn't show every extreme that they name: Positions below counts of a row hold real tokens, the rest is padding. `segments`: document numbers never fall along a row.
All inputs are finite; a program needn't handle non-finite values.
Results may differ from a plain program's by a relative error of at most 0.03.
The roundings to bfloat16 on the way count: a program that leaves them out, or rounds other values in their place, can miss the bound.
Values may be sent and summed in bfloat16 or wider, within the bound.
No kernel may reach another device: no remote copies, remote signals or barrier semaphores. Data moves between devices by JAX's collectives and lax.ppermute only.
A program may use at most 256 MiB of HBM per device.

v0:
```python
import functools

import jax
import jax.numpy as jnp
from jax import lax
from jax.experimental import pallas as pl
from jax.experimental.pallas import tpu as pltpu
from jax.sharding import PartitionSpec as P

HEAD_DIM = 64
PAIR = 2 * HEAD_DIM
EPSILON = 1e-06
MASKED = -1e30
SCALE = HEAD_DIM ** (-0.5)
GELU_A = 0.7978845608028654
GELU_B = 0.044715
EXTRA = 16
SCOPED = 12
bfloat = jnp.bfloat16
floating = jnp.float32

VMEM = pl.BlockSpec(memory_space=pltpu.VMEM)
SMEM = pl.BlockSpec(memory_space=pltpu.SMEM)
ANY = pl.BlockSpec(memory_space=pltpu.MemorySpace.HBM)


def dot(a, b):
    return jnp.dot(a, b, preferred_element_type=floating)


def dot_t(a, b):
    return lax.dot_general(a, b, (((1,), (1,)), ((), ())), preferred_element_type=floating)


def t_dot(a, b):
    return lax.dot_general(a, b, (((0,), (0,)), ((), ())), preferred_element_type=floating)


def params(mebibytes):
    return pltpu.CompilerParams(vmem_limit_bytes=mebibytes * 1024 * 1024)


def cost(flops, moved):
    return pl.CostEstimate(flops=flops // 1000, bytes_accessed=moved // 1000, transcendentals=0)


def scalar_rows(values, rows, width):
    lane = lax.broadcasted_iota(jnp.int32, (rows, width), 1)
    row = lax.broadcasted_iota(jnp.int32, (rows, width), 0)
    whole = jnp.zeros((rows, width), floating)
    for place, value in enumerate(values):
        whole = jnp.where(lane == place, value, whole)
    high = whole.astype(bfloat).astype(floating)
    middle = (whole - high).astype(bfloat).astype(floating)
    low = whole - high - middle
    part = jnp.where(row == 0, high, jnp.where(row == 1, middle, jnp.where(row == 2, low, 0.0)))
    return part.astype(bfloat)


def spread(value):
    high = value.astype(bfloat).astype(floating)
    middle = (value - high).astype(bfloat).astype(floating)
    low = value - high - middle
    top = jnp.concatenate([high, middle], axis=1)
    bottom = jnp.concatenate([low, jnp.zeros_like(low)], axis=1)
    return jnp.concatenate([top, bottom], axis=0).astype(bfloat)


def gathered_parts(block):
    block = block.astype(floating)
    width = block.shape[1] // 2
    return block[:8, :width] + block[:8, width:] + block[8:, :width]


def read_scalars(block, count):
    lane = lax.broadcasted_iota(jnp.int32, block.shape, 1)
    return [jnp.sum(jnp.where(lane == place, block, 0.0)) for place in range(count)]


def rms_scale(values):
    return lax.rsqrt(jnp.mean(values * values, axis=-1, keepdims=True) + EPSILON)


def lane_mask(length):
    return lax.broadcasted_iota(jnp.int32, (length, PAIR), 1) < HEAD_DIM


def stack_heads(block, first):
    zero = jnp.zeros_like(block)
    return jnp.concatenate([jnp.where(first, block, zero), jnp.where(first, zero, block)], axis=0)


def gelu_wave(gate):
    return jnp.tanh(GELU_A * (gate + GELU_B * gate * gate * gate))


def relative(blocks, index):
    low = (index & 1) == 1
    high = (index >> 1) == 1
    once = [jnp.where(low, blocks[place ^ 1], blocks[place]) for place in range(4)]
    return [jnp.where(high, once[place ^ 2], once[place]) for place in range(4)]


def attention(q_ref, k_ref, v_ref, seg_ref, att_ref, p_ref):
    length = seg_ref.shape[1]
    rows = q_ref.shape[0] // length
    pairs = q_ref.shape[1] // PAIR
    first = lane_mask(length)
    later = lax.broadcasted_iota(jnp.int32, (length, length), 0)
    earlier = lax.broadcasted_iota(jnp.int32, (length, length), 1)
    for row in range(rows):
        documents = jnp.broadcast_to(seg_ref[row : row + 1, :], (length, length)).astype(floating)
        allowed = (earlier <= later) & (documents == documents.T)
        allowed = jnp.concatenate([allowed, allowed], axis=0)
        span = slice(row * length, (row + 1) * length)
        for pair in range(pairs):
            heads = slice(pair * PAIR, (pair + 1) * PAIR)
            stacked = stack_heads(q_ref[span, heads], first)
            scores = jnp.where(allowed, dot_t(stacked, k_ref[span, heads]) * SCALE, MASKED)
            powers = jnp.exp(scores - jnp.max(scores, axis=-1, keepdims=True))
            probs = powers / jnp.sum(powers, axis=-1, keepdims=True)
            if p_ref is not None:
                p_ref[row * pairs + pair] = probs
            mixed = dot(probs.astype(bfloat), v_ref[span, heads])
            att_ref[span, heads] = jnp.where(first, mixed[:length], mixed[length:]).astype(bfloat)


def in_hbm(value):
    return pltpu.with_memory_space_constraint(value, pltpu.MemorySpace.HBM)


def forward_lite_kernel(x_any, seg_any, mix_any, cor_any, ga_any, gf_any, wq, wk, wv, wo, wg, wu, wd,
                        out_ref, wq_s, wk_s, wv_s, wo_s, wg_s, wu_s, wd_s,
                        x_in, seg_ref, mix_ref, cor_ref, ga_ref, gf_ref, q_ref, k_ref, v_ref, act_ref,
                        nrm_ref, att_ref, nf_ref, acc, sem, small_sem):
    tokens, width = act_ref.shape
    chunk = width
    pieces = wg.shape[2] // chunk
    small = [
        pltpu.make_async_copy(source, target, small_sem.at[place])
        for place, (source, target) in enumerate(
            ((x_any, x_in), (mix_any, mix_ref), (ga_any, ga_ref), (seg_any, seg_ref), (gf_any, gf_ref), (cor_any, cor_ref))
        )
    ]
    pairs = [(wq, wq_s), (wk, wk_s), (wv, wv_s), (wo, wo_s)]
    queue = [pltpu.make_async_copy(source, target, sem.at[place]) for place, (source, target) in enumerate(pairs)]

    def group(piece):
        span = pl.ds(pl.multiple_of(piece * chunk, chunk), chunk)
        places = ((wg, wg_s, (slice(None), slice(None), span)), (wu, wu_s, (slice(None), slice(None), span)),
                  (wd, wd_s, (slice(None), span, slice(None))))
        return [
            pltpu.make_async_copy(source.at[where], target.at[where], sem.at[4 + 3 * piece + place])
            for place, (source, target, where) in enumerate(places)
        ]

    def start_group(piece):
        for copy in group(piece):
            copy.start()

    for copy in small + queue:
        copy.start()
    start_group(0)
    for copy in small:
        copy.wait()
    section = lax.axis_index("section")
    mix = [[mix_ref[0, i, j] for j in range(2)] for i in range(2)]
    cor = [cor_ref[0, i] for i in range(2)]
    xa = x_in[:, :width].astype(floating)
    xb = x_in[:, width:].astype(floating)
    own_a = jnp.where(section == 0, mix[0][0], mix[1][0])
    own_b = jnp.where(section == 0, mix[0][1], mix[1][1])
    active = jnp.where(section == 0, xa, xb) + (own_a * xa + own_b * xb)
    act_ref[...] = active
    nrm_ref[...] = (active * rms_scale(active) * ga_ref[...]).astype(bfloat)
    for copy, weight, target in zip(queue, (wq_s, wk_s, wv_s), (q_ref, k_ref, v_ref)):
        copy.wait()
        target[...] = dot(nrm_ref[...], weight[0]).astype(bfloat)
    start_group(1)
    attention(q_ref, k_ref, v_ref, seg_ref, att_ref, None)
    for piece in range(2, pieces):
        start_group(piece)
    queue[3].wait()
    middle = act_ref[...] + dot(att_ref[...], wo_s[0])
    acc[...] = middle - act_ref[...]
    nf_ref[...] = (middle * rms_scale(middle) * gf_ref[...]).astype(bfloat)

    def one_piece(piece, carry):
        span = pl.ds(pl.multiple_of(piece * chunk, chunk), chunk)
        waits = group(piece)
        waits[0].wait()
        gate = dot(nf_ref[...], wg_s[0, :, span])
        waits[1].wait()
        upward = dot(nf_ref[...], wu_s[0, :, span])
        hidden = (0.5 * gate * (1.0 + gelu_wave(gate)) * upward).astype(bfloat)
        waits[2].wait()
        acc[...] += dot(hidden, wd_s[0, span, :])
        return carry

    lax.fori_loop(0, pieces, one_piece, 0)
    out_ref[:tokens, :] = acc[...].astype(bfloat)
    out_ref[tokens:, :] = scalar_rows(mix[0] + mix[1] + cor, EXTRA, width)


def forward_lite(x_in, segments, mixing, correction, gain_attn, gain_ffn, weights):
    tokens = x_in.shape[0]
    width = gain_attn.shape[1]
    size = sum(weight.size for weight in weights)
    narrow = pltpu.VMEM((tokens, width), bfloat)
    wide = pltpu.VMEM((tokens, width), floating)
    args = (x_in, segments, mixing, correction, gain_attn, gain_ffn) + weights
    scratch = [
        pltpu.VMEM(x_in.shape, bfloat), pltpu.VMEM(segments.shape, jnp.int32), pltpu.SMEM(mixing.shape, floating),
        pltpu.SMEM(correction.shape, floating), pltpu.VMEM(gain_attn.shape, floating), pltpu.VMEM(gain_ffn.shape, floating),
        narrow, narrow, narrow, wide, narrow, narrow, narrow, wide,
    ]
    scratch += [pltpu.SemaphoreType.DMA((4 + 3 * (weights[4].shape[2] // width),)), pltpu.SemaphoreType.DMA((6,))]
    return pl.pallas_call(
        forward_lite_kernel,
        out_shape=[jax.ShapeDtypeStruct((tokens + EXTRA, width), bfloat)]
        + [jax.ShapeDtypeStruct(weight.shape, bfloat) for weight in weights],
        in_specs=[ANY] * len(args),
        out_specs=[VMEM] * 8,
        scratch_shapes=scratch,
        compiler_params=params(SCOPED),
        cost_estimate=cost(2 * tokens * size, 2 * size),
        name="forward_lite",
    )(*[in_hbm(one) for one in args])


def forward_kernel(fast, x_in, message, seg_ref, mix_ref, cor_ref, ga_ref, gf_ref, wq, wk, wv, wo, wg, wu, wd,
                   x_ref, out_ref, q_ref, k_ref, v_ref, p_ref, act_ref, mid_ref, one_ref, two_ref, chg_ref, *refs):
    kept = refs[:4]
    nf_ref = refs[-4]
    nrm_ref, att_ref, acc = refs[-3:]
    tokens, width = act_ref.shape
    chunk = width
    pieces = wg.shape[2] // chunk
    section = lax.axis_index("section")
    quarter = lax.axis_index("dp") & 3
    mix = [[mix_ref[0, i, j] for j in range(2)] for i in range(2)]
    cor = [cor_ref[0, i] for i in range(2)]
    xa = x_in[:, :width].astype(floating)
    xb = x_in[:, width:].astype(floating)
    got = read_scalars(message[tokens : tokens + EXTRA, :PAIR].astype(floating), 6)
    moved = message[:tokens, :].astype(floating)
    sent_a = (xa + (got[0] * xa + got[1] * xb) + got[4] * moved).astype(bfloat)
    sent_b = (xb + (got[2] * xa + got[3] * xb) + got[5] * moved).astype(bfloat)
    x_ref[:, :width] = jnp.where(section == 0, x_in[:, :width], sent_a)
    x_ref[:, width:] = jnp.where(section == 0, x_in[:, width:], sent_b)
    xa = x_ref[:, :width].astype(floating)
    xb = x_ref[:, width:].astype(floating)
    own_a = jnp.where(section == 0, mix[0][0], mix[1][0])
    own_b = jnp.where(section == 0, mix[0][1], mix[1][1])
    active = jnp.where(section == 0, xa, xb) + (own_a * xa + own_b * xb)
    act_ref[...] = active
    nrm_ref[...] = (active * rms_scale(active) * ga_ref[...]).astype(bfloat)
    for weight, target in zip((wq, wk, wv), (q_ref, k_ref, v_ref)):
        target[...] = dot(nrm_ref[...], weight[0]).astype(bfloat)

    def keep_quarters(values, base):
        share = width // 16
        for far in range(4):
            blocks = [values[:, (4 * far + near) * share : (4 * far + near + 1) * share] for near in range(4)]
            for slot, block in enumerate(relative(blocks, quarter)):
                target, start = (kept[slot], width + base) if slot < 3 else (refs[4], base)
                target[:, start + far * share : start + (far + 1) * share] = block

    attention(q_ref, k_ref, v_ref, seg_ref, att_ref, p_ref)
    middle = act_ref[...] + dot(att_ref[...], wo[0])
    mid_ref[...] = middle
    nf_ref[...] = (middle * rms_scale(middle) * gf_ref[...]).astype(bfloat)
    if fast:
        keep_quarters(att_ref[...], 0)
        keep_quarters(nrm_ref[...], width // 4)
        for slot in (1, 2):
            kept[slot][:, width + width // 2 :] = nf_ref[...]
    else:
        kept[1][...] = nrm_ref[...]
        kept[2][...] = att_ref[...]
    for piece in range(pieces):
        span = slice(piece * chunk, (piece + 1) * chunk)
        gate = dot(nf_ref[...], wg[0, :, span])
        upward = dot(nf_ref[...], wu[0, :, span])
        wave = gelu_wave(gate)
        half = 0.5 * (1.0 + wave)
        value = gate * half
        hidden = (value * upward).astype(bfloat)
        slope = half + 0.5 * gate * (1.0 - wave * wave) * (GELU_A * (1.0 + 3.0 * GELU_B * gate * gate))
        one_ref[piece] = upward * slope
        two_ref[piece] = value
        if fast:
            share = chunk // 4
            blocks = [hidden[:, near * share : (near + 1) * share] for near in range(4)]
            for slot, block in enumerate(relative(blocks, quarter)):
                kept[slot][:, piece * share : (piece + 1) * share] = block
        else:
            kept[0][:, span] = hidden
        down = dot(hidden, wd[0, span, :])
        if piece == 0:
            acc[...] = down
        else:
            acc[...] += down
    change = mid_ref[...] + acc[...] - act_ref[...]
    chg_ref[...] = change
    xa = x_ref[:, :width].astype(floating)
    xb = x_ref[:, width:].astype(floating)
    out_ref[0, :, :width] = (xa + (mix[0][0] * xa + mix[0][1] * xb) + cor[0] * change).astype(bfloat)
    out_ref[0, :, width:] = (xb + (mix[1][0] * xa + mix[1][1] * xb) + cor[1] * change).astype(bfloat)


def forward(fast, x_in, message, segments, mixing, correction, gain_attn, gain_ffn, weights):
    tokens = x_in.shape[0]
    length = segments.shape[1]
    width = gain_attn.shape[1]
    hidden_width = weights[4].shape[2]
    size = sum(weight.size for weight in weights)
    shape = jax.ShapeDtypeStruct
    narrow = ((tokens, width), bfloat)
    wide = ((tokens, width), floating)
    probs = ((tokens // length * (width // PAIR), 2 * length, length), floating)
    if fast:
        short, long = (((tokens, columns), bfloat) for columns in (width + width // 2, 2 * width + width // 2))
        kept = [short, long, long, narrow, ((tokens, width // 2), bfloat), narrow]
    else:
        kept = [((tokens, hidden_width), bfloat), narrow, narrow, narrow]
    ffn = ((hidden_width // width, tokens, width), floating)
    outs = [((tokens, 2 * width), bfloat), ((1, tokens, 2 * width), bfloat), narrow, narrow, narrow, probs, wide, wide,
            ffn, ffn, wide] + kept
    return pl.pallas_call(
        lambda *refs: forward_kernel(fast, *refs),
        out_shape=[shape(*one) for one in outs],
        in_specs=[VMEM, VMEM, VMEM, SMEM, SMEM, VMEM, VMEM] + [VMEM] * 7,
        out_specs=[VMEM] * len(outs),
        scratch_shapes=[pltpu.VMEM(*narrow)] * 2 + [pltpu.VMEM(*wide)],
        compiler_params=params(SCOPED),
        cost_estimate=cost(2 * tokens * size, 2 * size),
        name="forward_full",
    )(x_in, message, segments, mixing, correction, gain_attn, gain_ffn, *weights)


def start_rows(message, grad_ref, counts_ref, cor_ref, g_ref, low_ref):
    tokens, width = low_ref.shape
    rows = counts_ref.shape[0]
    length = tokens // rows
    section = lax.axis_index("section")
    if message is not None:
        got = read_scalars(message[tokens : tokens + EXTRA, :PAIR].astype(floating), 4)
    place = lax.broadcasted_iota(jnp.int32, (length, width), 0)
    for row in range(rows):
        span = slice(row * length, (row + 1) * length)
        valid = place < counts_ref[row]
        own_a = jnp.where(valid, grad_ref[span, :width].astype(floating), 0.0)
        own_b = jnp.where(valid, grad_ref[span, width:].astype(floating), 0.0)
        if message is not None:
            later_b = own_b + message[span, :].astype(floating)
            far_a = own_a + (got[0] * own_a + got[2] * later_b)
            far_b = later_b + (got[1] * own_a + got[3] * later_b)
            own_a = jnp.where(section == 0, far_a, own_a).astype(bfloat).astype(floating)
            own_b = jnp.where(section == 0, far_b, own_b).astype(bfloat).astype(floating)
        g_ref[span, :width] = own_a.astype(bfloat)
        g_ref[span, width:] = own_b.astype(bfloat)
        low_ref[span, :] = (cor_ref[0, 0] * own_a + cor_ref[0, 1] * own_b).astype(bfloat)


def start(message, out_grad, counts, correction, before):
    tokens = out_grad.shape[0]
    width = message.shape[1]
    shape = jax.ShapeDtypeStruct
    return pl.pallas_call(
        lambda *refs: start_rows(*refs[:4], *refs[-2:]),
        out_shape=[shape((tokens, 2 * width), bfloat), shape((tokens, width), bfloat)],
        in_specs=[VMEM, VMEM, SMEM, SMEM] + [ANY] * len(before),
        out_specs=[VMEM, VMEM],
        compiler_params=params(SCOPED),
        cost_estimate=cost(tokens * width * 20, tokens * width * 12),
        name="backward_start",
    )(message, out_grad, counts, correction, *before)


def norm_backward(values, gain, grad_normed, with_gain):
    inverse = rms_scale(values)
    grad_gain = jnp.sum(grad_normed * values * inverse, axis=0, keepdims=True) if with_gain else None
    weighted = grad_normed * gain
    grad_values = inverse * weighted - values * inverse**3 * jnp.mean(weighted * values, axis=-1, keepdims=True)
    return grad_gain, grad_values


def ffn_steps(low_ref, one, two, wg, wu, wd, acc, emit):
    width = wd.shape[2]
    quarter = lax.axis_index("dp") & 3
    for step in range(4):
        piece = (3 - step) ^ quarter
        span = pl.ds(pl.multiple_of(piece * width, width), width)
        grad_hidden = dot_t(low_ref[...], wd[0, span, :])
        dgate = (grad_hidden * one[piece]).astype(bfloat)
        dup = (grad_hidden * two[piece]).astype(bfloat)
        emit(3 - step, dgate, dup)
        total = dot_t(dgate, wg[0, :, span]) + dot_t(dup, wu[0, :, span])
        if step == 0:
            acc[...] = total
        else:
            acc[...] += total


def ffn_kernel(g_in, low_ref, cor_ref, gf_ref, mid_ref, one, two, wg, wu, wd, *refs):
    slots = refs[-12:-4]
    dmid_ref, datt_ref, gain_ref, acc = refs[-4:]
    width = gf_ref.shape[1]

    def emit(slot, dgate, dup):
        slots[slot][...] = dgate
        slots[4 + slot][...] = dup

    ffn_steps(low_ref, one, two, wg, wu, wd, acc, emit)
    grad_gain, grad_values = norm_backward(mid_ref[...], gf_ref[...], acc[...], True)
    block = cor_ref[0, 0] * g_in[:, :width].astype(floating) + cor_ref[0, 1] * g_in[:, width:].astype(floating)
    grad_middle = block + grad_values
    dmid_ref[...] = grad_middle
    datt_ref[...] = grad_middle.astype(bfloat)
    gain_ref[...] = grad_gain


def ffn_backward(g_in, low, correction, gain_ffn, middle, one, two, before, weights):
    tokens = g_in.shape[0]
    width = gain_ffn.shape[1]
    shape = jax.ShapeDtypeStruct
    return pl.pallas_call(
        ffn_kernel,
        out_shape=[shape((tokens, width), bfloat)] * 8
        + [shape((tokens, width), floating), shape((tokens, width), bfloat), shape((1, width), floating)],
        in_specs=[VMEM, VMEM, SMEM] + [VMEM] * 7 + [ANY] * len(before),
        out_specs=[VMEM] * 11,
        scratch_shapes=[pltpu.VMEM((tokens, width), floating)],
        compiler_params=params(SCOPED),
        cost_estimate=cost(2 * tokens * 3 * weights[4].size, 2 * 3 * weights[4].size),
        name="backward_ffn",
    )(g_in, low, correction, gain_ffn, middle, one, two, *weights[4:], *before)


def attn_steps(q_ref, k_ref, v_ref, p_ref, do_ref, parts):
    tokens, width = do_ref.shape
    length = p_ref.shape[2]
    rows = tokens // length
    pairs = width // PAIR
    first = lane_mask(length)
    for row in range(rows):
        span = slice(row * length, (row + 1) * length)
        for pair in range(pairs):
            heads = slice(pair * PAIR, (pair + 1) * PAIR)
            probs = p_ref[row * pairs + pair]
            grad_out = stack_heads(do_ref[span, heads], first)
            grad_value = t_dot(probs.astype(bfloat), grad_out)
            grad_probs = dot_t(grad_out, v_ref[span, heads])
            carried = jnp.sum(probs * grad_probs, axis=-1, keepdims=True)
            grad_scores = (probs * (grad_probs - carried)).astype(bfloat)
            grad_query = dot(grad_scores, k_ref[span, heads])
            grad_query = jnp.where(first, grad_query[:length], grad_query[length:])
            grad_key = t_dot(grad_scores, stack_heads(q_ref[span, heads], first))
            for (part, base), value in zip(parts, (grad_query * SCALE, grad_key * SCALE, grad_value)):
                part[span, base + pair * PAIR : base + (pair + 1) * PAIR] = value.astype(bfloat)


def normed_grad(parts, rows, width, wq, wk, wv):
    return sum(dot_t(part[:rows, base : base + width], weight[0]) for (part, base), weight in zip(parts, (wq, wk, wv)))


def attn_kernel(datt_ref, q_ref, k_ref, v_ref, p_ref, gfg_ref, ga_ref, x_ref, g_in, dmid_ref, act_ref, chg_ref, mix_ref, cor_ref,
                wq, wk, wv, wo, before,
                grad_ref, right_ref, small_ref, do_ref):
    tokens, width = datt_ref.shape
    right_ref[:tokens, :width] = datt_ref[...]
    do_ref[...] = dot_t(datt_ref[...], wo[0]).astype(bfloat)
    parts = (right_ref, width), (right_ref, 2 * width), (right_ref, 3 * width)
    attn_steps(q_ref, k_ref, v_ref, p_ref, do_ref, parts)
    grad_normed = normed_grad(parts, tokens, width, wq, wk, wv)
    grad_gain, grad_values = norm_backward(act_ref[...], ga_ref[...], grad_normed, True)
    section = lax.axis_index("section")
    mix = [[mix_ref[0, i, j] for j in range(2)] for i in range(2)]
    cor = [cor_ref[0, i] for i in range(2)]
    out_a = g_in[:, :width].astype(floating)
    out_b = g_in[:, width:].astype(floating)
    grad_active = dmid_ref[...] + grad_values - (cor[0] * out_a + cor[1] * out_b)
    pred_a = out_a + jnp.where(section == 0, grad_active, 0.0)
    pred_b = out_b + jnp.where(section == 0, 0.0, grad_active)
    grad_ref[0, :, :width] = (pred_a + (mix[0][0] * pred_a + mix[1][0] * pred_b)).astype(bfloat)
    grad_ref[0, :, width:] = (pred_b + (mix[0][1] * pred_a + mix[1][1] * pred_b)).astype(bfloat)
    xa = x_ref[:, :width].astype(floating)
    xb = x_ref[:, width:].astype(floating)
    small_ref[0:1, :] = grad_gain
    small_ref[1:2, :] = gfg_ref[...]
    place = 2
    for pred in (pred_a, pred_b):
        for state in (xa, xb):
            small_ref[place : place + 1, :] = jnp.sum(pred * state, axis=0, keepdims=True)
            place += 1
    for out in (out_a, out_b):
        small_ref[place : place + 1, :] = jnp.sum(out * chg_ref[...], axis=0, keepdims=True)
        place += 1
    right_ref[tokens:, : 2 * width] = spread(small_ref[...])
    right_ref[tokens:, 2 * width :] = jnp.zeros((right_ref.shape[0] - tokens, 2 * width), bfloat)


def attn_backward(x, g_in, grad_middle, grad_att, active, change, queries, key_rows, value_rows, probs, ffn_gain, gain_attn,
                  mixing, correction, before, weights):
    tokens, width = active.shape
    shape = jax.ShapeDtypeStruct
    return pl.pallas_call(
        attn_kernel,
        out_shape=[
            shape((1, tokens, 2 * width), bfloat), shape((tokens + EXTRA, 4 * width), bfloat), shape((8, width), floating),
        ],
        in_specs=[VMEM] * 12 + [SMEM] * 2 + [VMEM] * 4 + [ANY],
        out_specs=[VMEM] * 3,
        scratch_shapes=[pltpu.VMEM((tokens, width), bfloat)],
        compiler_params=params(SCOPED),
        cost_estimate=cost(2 * tokens * 5 * weights[0].size, 2 * 4 * weights[0].size),
        name="backward_attn",
    )(grad_att, queries, key_rows, value_rows, probs, ffn_gain, gain_attn, x, g_in, grad_middle, active, change,
      mixing, correction, *weights[:4], before)


def relay_kernel(grad_in, counts_ref, cor_ref, mix_ref, gf_ref, ga_ref, one, two, mid_ref, q_ref, k_ref, v_ref, p_ref, act_ref,
                 wq, wk, wv, wo, wg, wu, wd,
                 msg_ref,
                 acc, g_in, low_ref, do_ref, dqkv_ref):
    tokens, width = low_ref.shape
    start_rows(None, grad_in, counts_ref, cor_ref, g_in, low_ref)
    acc[...] = jnp.zeros_like(acc)

    def one_piece(piece, carry):
        span = pl.ds(pl.multiple_of(piece * width, width), width)
        grad_hidden = dot_t(low_ref[...], wd[0, span, :])
        dgate = (grad_hidden * one[piece]).astype(bfloat)
        dup = (grad_hidden * two[piece]).astype(bfloat)
        acc[...] += dot_t(dgate, wg[0, :, span]) + dot_t(dup, wu[0, :, span])
        return carry

    lax.fori_loop(0, one.shape[0], one_piece, 0)
    grad_values = norm_backward(mid_ref[...], gf_ref[...], acc[...], False)[1]
    cor = [cor_ref[0, i] for i in range(2)]
    block = cor[0] * g_in[:, :width].astype(floating) + cor[1] * g_in[:, width:].astype(floating)
    acc[...] = block + grad_values
    do_ref[...] = dot_t(acc[...].astype(bfloat), wo[0]).astype(bfloat)
    parts = (dqkv_ref, 0), (dqkv_ref, width), (dqkv_ref, 2 * width)
    attn_steps(q_ref, k_ref, v_ref, p_ref, do_ref, parts)
    grad_normed = normed_grad(parts, tokens, width, wq, wk, wv)
    grad_values = norm_backward(act_ref[...], ga_ref[...], grad_normed, False)[1]
    block = cor[0] * g_in[:, :width].astype(floating) + cor[1] * g_in[:, width:].astype(floating)
    msg_ref[:tokens, :] = (acc[...] + grad_values - block).astype(bfloat)
    mix = [[mix_ref[0, i, j] for j in range(2)] for i in range(2)]
    msg_ref[tokens:, :] = scalar_rows(mix[0] + mix[1], EXTRA, width)


def relay_backward(out_grad, counts, correction, mixing, gain_ffn, gain_attn, one, two, middle, queries, key_rows, value_rows,
                   probs, active, weights):
    tokens, width = active.shape
    shape = jax.ShapeDtypeStruct
    narrow = pltpu.VMEM((tokens, width), bfloat)
    wide = pltpu.VMEM((tokens, width), floating)
    size = sum(weight.size for weight in weights)
    return pl.pallas_call(
        relay_kernel,
        out_shape=shape((tokens + EXTRA, width), bfloat),
        in_specs=[VMEM, SMEM, SMEM, SMEM] + [VMEM] * 17,
        out_specs=VMEM,
        scratch_shapes=[wide, pltpu.VMEM((tokens, 2 * width), bfloat), narrow, narrow, pltpu.VMEM((tokens, 3 * width), bfloat)],
        compiler_params=params(SCOPED),
        cost_estimate=cost(2 * tokens * size, 2 * size),
        name="backward_relay",
    )(out_grad, counts, correction, mixing, gain_ffn, gain_attn, one, two, middle, queries, key_rows, value_rows, probs, active,
      *weights)


def quarter_kernel(base, products, block, refs):
    count = 4
    lefts = refs[:count]
    rights = refs[count : 2 * count]
    send_ref, keep_ref = refs[-2:]
    quarter_parts(base, products, block, lefts, rights, send_ref, keep_ref)


def quarter_parts(base, products, block, lefts, rights, send_ref, keep_ref):
    tokens = lefts[0].shape[0]
    tail = lefts[0].shape[1] - lefts[-1].shape[1]
    index = lax.axis_index("dp")
    near = (index >> 2) & 1
    far = (index >> 3) & 1
    for left_at, left_wide, right_at, right_wide in products:
        columns = slice(right_at, right_at + right_wide)
        total = 0.0
        for left, right in zip(lefts, rights):
            at = left_at if left.shape[1] > left_at else left_at - tail
            total = total + t_dot(left[:, at : at + left_wide], right[:tokens, columns])
        span = slice(right_at - base, right_at - base + right_wide)
        for place in range(4):
            part = total[place * block : (place + 1) * block, :]
            slot = (place >> 1) ^ far
            mine = (place & 1) == near

            @pl.when(mine)
            def _():
                keep_ref[slot, :, span] = part

            @pl.when(jnp.logical_not(mine))
            def _():
                send_ref[slot, :, span] = part.astype(bfloat)


def attn_product_kernel(halves, block, refs):
    lefts, rights = refs[:4], refs[4:8]
    first_send, first_keep, small_ref, second_send, second_keep, stage = refs[-6:]
    tokens = lefts[0].shape[0]
    wide = first_keep.shape[2]
    quarter_parts(0, halves[0], block, lefts, rights, stage, first_keep)
    first_send[:block, :] = stage[0]
    first_send[block : 2 * block, :] = stage[1]
    small = sum(gathered_parts(right[tokens:, :wide]) for right in rights)
    small_ref[...] = small
    first_send[2 * block :, :] = spread(small)
    quarter_parts(wide, halves[1], block, lefts, rights, second_send, second_keep)


def attn_product(lefts, rights, halves, block, before):
    wide = rights[0].shape[1] // 2
    shape = jax.ShapeDtypeStruct
    send, keep = shape((2, block, wide), bfloat), shape((2, block, wide), floating)
    return pl.pallas_call(
        lambda *refs: attn_product_kernel(halves, block, refs),
        out_shape=[shape((2 * block + EXTRA, wide), bfloat), keep, shape((8, wide // 2), floating), send, keep],
        in_specs=[VMEM] * 8 + [ANY] * len(before),
        out_specs=[VMEM] * 5,
        scratch_shapes=[pltpu.VMEM(send.shape, bfloat)],
        compiler_params=params(SCOPED),
        cost_estimate=cost(wide, wide),
        name="product_attn",
    )(*lefts, *rights, *before)


def first_sum_kernel(keep_ref, came_ref, small_ref, held_ref, passed_ref, sums_ref):
    block = held_ref.shape[0]
    held_ref[...] = keep_ref[0] + came_ref[:block, :].astype(floating)
    passed_ref[:block, :] = (keep_ref[1] + came_ref[block : 2 * block, :].astype(floating)).astype(bfloat)
    small = small_ref[...] + gathered_parts(came_ref[2 * block :, :])
    sums_ref[...] = small
    passed_ref[block:, :] = spread(small)


def first_sum(keep, came, small):
    _, block, wide = keep.shape
    shape = jax.ShapeDtypeStruct
    return pl.pallas_call(
        first_sum_kernel,
        out_shape=[shape((block, wide), floating), shape((block + EXTRA, wide), bfloat), shape(small.shape, floating)],
        in_specs=[VMEM] * 3,
        out_specs=[VMEM] * 3,
        compiler_params=params(SCOPED),
        cost_estimate=cost(wide, wide),
        name="first_sum",
    )(keep, came, small)


def first_end_kernel(held_ref, came_ref, small_ref, left_ref, right_ref, sums_ref):
    block, wide = held_ref.shape
    left_ref[0] = held_ref[:, : wide // 2] + came_ref[:block, : wide // 2].astype(floating)
    right_ref[0] = held_ref[:, wide // 2 :] + came_ref[:block, wide // 2 :].astype(floating)
    sums_ref[...] = small_ref[...] + gathered_parts(came_ref[block:, :])


def first_end(held, came, small):
    block, wide = held.shape
    shape = jax.ShapeDtypeStruct
    return pl.pallas_call(
        first_end_kernel,
        out_shape=[shape((1, block, wide // 2), floating)] * 2 + [shape(small.shape, floating)],
        in_specs=[VMEM] * 3,
        out_specs=[VMEM] * 3,
        compiler_params=params(SCOPED),
        cost_estimate=cost(wide, wide),
        name="first_end",
    )(held, came, small)


def quarter_product(lefts, rights, products, block, before, name):
    base = products[0][2]
    wide = sum(one[3] for one in products)
    shape = jax.ShapeDtypeStruct
    flops = sum(2 * 4 * lefts[0].shape[0] * one[1] * one[3] for one in products)
    return pl.pallas_call(
        lambda *refs: quarter_kernel(base, products, block, refs),
        out_shape=[shape((2, block, wide), bfloat), shape((2, block, wide), floating)],
        in_specs=[VMEM] * 8 + [ANY] * len(before),
        out_specs=[VMEM, VMEM],
        compiler_params=params(SCOPED),
        cost_estimate=cost(flops, 12 * block * wide),
        name=name,
    )(*lefts, *rights, *before)


def assemble_kernel(own, one, two, three, gate_ref, up_ref):
    quarter = lax.axis_index("dp") & 3
    width = own.shape[1] // 2
    for slot, piece in enumerate((own, one, two, three)):
        span = pl.ds(pl.multiple_of((slot ^ quarter) * width, width), width)
        gate_ref[0, :, span] = piece[:, :width].astype(floating)
        up_ref[0, :, span] = piece[:, width:].astype(floating)


def assemble(pieces):
    share, double = pieces[0].shape
    shape = jax.ShapeDtypeStruct((1, share, 2 * double), floating)
    return pl.pallas_call(
        assemble_kernel,
        out_shape=[shape, shape],
        in_specs=[VMEM] * 4,
        out_specs=[VMEM] * 2,
        compiler_params=params(SCOPED),
        cost_estimate=cost(share * double * 4, share * double * 24),
        name="assemble",
    )(*pieces)


def exchange(value, flips):
    count = lax.axis_size("dp")
    return lax.ppermute(value, "dp", [(source, source ^ flips) for source in range(count)])


def relative_rows(matrix, order, index):
    bits = len(order)
    block = matrix.shape[0] >> bits
    split = matrix.reshape((2,) * bits + (block, matrix.shape[1]))
    axes = [bits - 1 - bit for bit in order]
    split = jnp.transpose(split, axes + [bits, bits + 1])
    for axis, bit in enumerate(order):
        split = jnp.where((index >> bit) & 1 == 1, jnp.flip(split, axis), split)
    return split.reshape(matrix.shape)


def scatter_sum(left, right, order):
    total = left.shape[0]
    arrived = []
    for step in range(len(order) + 1):
        low = total >> (step + 1) if step < len(order) else 0
        high = total >> step
        part = dot(left[low:high], right)
        for other in arrived:
            part = part + other[low:high].astype(floating)
        if step == len(order):
            return part
        arrived.append(exchange(part.astype(bfloat), 1 << order[step]))


def halving_grads(kept, low, slots, right, index, count):
    width = low.shape[1]
    order = list(range(count.bit_length() - 1))
    hidden, normed, attended, normed_ffn = (relative_rows(one.T, order, index) for one in kept)
    quarter = index & 3
    places = jnp.arange(4) ^ quarter
    dgate = jnp.concatenate(list(jnp.stack(slots[:4])[places]), axis=1)
    dup = jnp.concatenate(list(jnp.stack(slots[4:])[places]), axis=1)
    grad_down = scatter_sum(hidden, low, order)
    grad_gate = scatter_sum(normed_ffn, dgate, order)
    grad_up = scatter_sum(normed_ffn, dup, order)
    grad_out = scatter_sum(attended, right[:, :width], order)
    grad_qkv = scatter_sum(normed, right[:, width:], order)
    grads = [grad_down, grad_gate, grad_up, grad_out] + [grad_qkv[:, place * width : (place + 1) * width] for place in range(3)]
    return [one[None] for one in grads]


def after(values, *earlier):
    return lax.optimization_barrier((values, earlier))[0]


def gather_start(value):
    return [value, exchange(value, 1), exchange(value, 2)]


def gather_end(pieces, *earlier):
    return pieces + [exchange(after(pieces[2], *earlier), 1)]


def swapped(pieces):
    return [pieces[0]] + [exchange(pieces[flips], flips) for flips in (1, 2, 3)]


def sum_once(pair, *earlier):
    send, keep = pair
    arrived = after(exchange(send, 4), *earlier)
    return keep[0] + arrived[0].astype(floating), (keep[1] + arrived[1].astype(floating)).astype(bfloat)


def sum_twice(held, passed, *earlier):
    return held + after(exchange(passed, 8), *earlier).astype(floating)


def sum_over(value, bits):
    for bit in range(bits):
        value = value + exchange(value, 1 << bit)
    return value


def quarter_grads(normed_ffn, kept, nearby, slots, right, down_pair, index):
    width = normed_ffn[0].shape[1]
    share = width // 16
    block = 4 * share
    whole = [(0, width, 0, width)]
    gates = swapped(slots[:4])
    ups, nearby = after((slots[4:], nearby), right)
    ups, nearby = swapped(list(ups)), exchange(nearby, 3)
    down_sums = sum_once(down_pair, right)
    gate_pair = quarter_product(normed_ffn, gates, whole, block, [right, down_sums[1]], "product_gate")
    grad_down = sum_twice(*down_sums)
    rights = gather_start(after(right, gate_pair[0], grad_down, ups[1:], nearby))
    gate_sums = sum_once(gate_pair)
    up_pair = quarter_product(normed_ffn, ups, whole, block, [gate_sums[1], grad_down], "product_up")
    up_sums = sum_once(up_pair)
    gate_tile = sum_twice(*gate_sums).astype(bfloat)
    rights = gather_end(rights, up_sums[1], gate_tile)
    halves = (
        [(width, block, 0, width), (width + block, block, width, width)], [(width + block, block, 2 * width, 2 * width)])
    before = [up_sums[1], gate_tile]
    first_send, first_keep, small, *second_pair = attn_product(kept[:3] + [nearby], rights, halves, share, before)
    held, first_passed, small = first_sum(first_keep, exchange(first_send, 4), small)
    up_tile = sum_twice(*up_sums, first_passed).astype(bfloat)
    quarter = index & 3
    gate_tile = after(gate_tile, first_passed)
    pieces = [
        jnp.concatenate(
            [lax.dynamic_slice_in_dim(tile, (slot ^ quarter) * share, share, axis=0) for tile in (gate_tile, up_tile)], axis=1)
        for slot in range(4)
    ]
    pieces = swapped(pieces)
    grad_out, grad_query, small = first_end(held, exchange(first_passed, 8), small)
    second_sums = sum_once(second_pair, first_passed)
    grad_gate, grad_up = assemble(list(after(pieces, second_sums[1], small)))
    held, passed = second_sums
    passed = exchange(passed, 8)
    grads = [grad_down[None], grad_gate, grad_up, grad_out, grad_query]
    for span in (slice(0, width), slice(width, 2 * width)):
        grads.append((held[:, span] + passed[:, span].astype(floating))[None])
    return grads, small


def local(states_in, out_grad, counts, segments, mixing, correction, gain_attn, w_query, w_key, w_value, w_attn_out, gain_ffn,
          w_gate, w_up, w_down):
    weights = (w_query, w_key, w_value, w_attn_out, w_gate, w_up, w_down)
    width = gain_attn.shape[1]
    index = lax.axis_index("dp")
    count = lax.axis_size("dp")
    fast = count == 16
    message, *weights = forward_lite(states_in, segments, mixing, correction, gain_attn, gain_ffn, weights)
    message = lax.ppermute(message, "section", [(0, 1), (1, 0)])
    (x, states, queries, key_rows, value_rows, probs, active, middle, one, two, change, *kept) = forward(
        fast, states_in, message, segments, mixing, correction, gain_attn, gain_ffn, weights)
    before = []
    if fast:
        kept, nearby, normed_ffn = swapped(kept[:4]), kept[4], kept[5]
        before = kept[1:]
    message = relay_backward(out_grad, counts, correction, mixing, gain_ffn, gain_attn, one, two, middle, queries, key_rows,
                             value_rows, probs, active, weights)
    message = lax.ppermute(message, "section", [(0, 1), (1, 0)])
    g_in, low = start(message, out_grad, counts, correction, [])
    *slots, grad_middle, grad_att, ffn_gain = ffn_backward(g_in, low, correction, gain_ffn, middle, one, two, before, weights)
    before = slots[0]
    if fast:
        lows = gather_end(gather_start(low), before)
        beside, across = (one[:, width + width // 2 :] for one in kept[1:3])
        normed_ffn = gather_end([normed_ffn, beside, across], before)
        down_pair = quarter_product(kept, lows, [(0, width, 0, width)], width // 4, [before], "product_down")
        before = down_pair[0]
    state_grads, right, small = attn_backward(x, g_in, grad_middle, grad_att, active, change, queries, key_rows, value_rows, probs,
                                              ffn_gain, gain_attn, mixing, correction, before, weights)
    if fast:
        grads, small = quarter_grads(normed_ffn, kept, nearby, slots, right, down_pair, index)
    else:
        grads = halving_grads(kept, low, slots, right[: low.shape[0]], index, count)
        small = sum_over(small, count.bit_length() - 1)
    grad_down, grad_gate, grad_up, grad_out, grad_query, grad_key, grad_value = grads
    share = width // count
    gains = lax.dynamic_slice(small, (0, index * share), (2, share))
    sums = jnp.sum(small[2:], axis=1)
    return (
        states,
        state_grads,
        sums[:4].reshape(1, 2, 2),
        sums[4:].reshape(1, 2),
        gains[0:1],
        grad_query,
        grad_key,
        grad_value,
        grad_out,
        gains[1:2],
        grad_gate,
        grad_up,
        grad_down,
    )


def solution(mesh):
    rows = P("dp", None)
    matrix = P("section", None, None)
    vector = P("section", None)
    share = P("section", "dp", None)
    gain_share = P("section", "dp")
    in_specs = (rows, rows, P("dp"), rows, matrix, vector, vector, matrix, matrix, matrix, matrix, vector, matrix, matrix, matrix)
    out_specs = (share, share, matrix, vector, gain_share, share, share, share, share, gain_share, share, share, share)
    return jax.shard_map(local, mesh=mesh, in_specs=in_specs, out_specs=out_specs, check_vma=False)
```

profile of v0, /device:TPU:0, one launch (start us, length us, event | category | flops | bytes accessed | tf_op | source)
XLA Modules:
  0.0 187.0 jit_solution(13043422690999418899)
XLA Ops:
  0.7 11.9 %forward_lite.1 = (bf16[208,768]{1,0:T(8,128)(2,1)S(1)}, bf16[1,768,768]{2,1,0:T(8,128)(2,1)S(1)}, bf16[1,768,768]{2,1,0:T(8,128)(2,1)S(1)}, bf16[1,768,768]{2,1...) custom-call(bf16[192,1536]{1,0:T(8,128)(2,1)} %refs_0_.1, ...), custom_call_target="tpu_custom_call" | custom-call | flops 3623878 | bytes 18874 | tf_op jit(solution)/shard_map/forward_lite/pallas_call | solution.py:218
  12.6 3.0 %collective-permute-start = (bf16[208,768]{1,0:T(8,128)(2,1)S(1)}, bf16[208,768]{1,0:T(8,128)(2,1)S(1)}, u32[]{:S(2)}, u32[]{:S(2)}) collective-permute-start(bf16[208,768]{1,0:T(8,128)(2,1)S(1)} %get-tuple-element.89), channel_id=1, source_target_pairs={{0,16},{16,0},{1,17},{17,1},{2,18},{18,2},{3,19},{19,3},{4,20},{20... | collective-permute-start | bytes 958472 | tf_op jit(solution)/shard_map/ppermute | solution.py:852
  15.6 7.5 %collective-permute-done.refs_1_ = bf16[208,768]{1,0:T(8,128)(2,1)S(1)} collective-permute-done((bf16[208,768]{1,0:T(8,128)(2,1)S(1)}, bf16[208,768]{1,0:T(8,128)(2,1)S(1)}, u32[]{:S(2)}, u32[]{:S(2)}) %collective-permute-start) | collective-permute-done | bytes 319520 | tf_op jit(solution)/shard_map/ppermute | solution.py:852
  23.2 9.0 %forward_full.1 = (bf16[192,1536]{1,0:T(8,128)(2,1)S(1)}, bf16[1,192,1536]{2,1,0:T(8,128)(2,1)}, bf16[192,768]{1,0:T(8,128)(2,1)S(1)}, bf16[192,768]{1,0:T(8,128...) custom-call(bf16[192,1536]{1,0:T(8,128)(2,1)S(1)} %copy-done.1, ...), custom_call_target="tpu_custom_call" | custom-call | flops 3623878 | bytes 18874 | tf_op jit(solution)/shard_map/forward_full/pallas_call | solution.py:330
  32.2 1.8 collective-permute-start.3
  34.0 12.7 %backward_relay.1 = bf16[208,768]{1,0:T(8,128)(2,1)S(1)} custom-call(bf16[192,1536]{1,0:T(8,128)(2,1)S(1)} %copy-done.2, s32[2]{0:T(128)S(1)} %copy-done.8, f32[1,2]{1,0:T(1,128)S(1)} %copy-done.5, f32[1,2,2]{2,1,0:T(2,128)S(1)} %copy-done.6, f32[1,768]{1,0:T(1,128)S(1)} %copy-done.3, f32[1,768]{1,0:T(1,128)S(1)} %copy-done.4, ...), custom_call_target="tpu_custom_call" | custom-call | flops 3623878 | bytes 18874 | tf_op jit(solution)/shard_map/backward_relay/pallas_call | solution.py:562
  46.7 1.6 collective-permute-start.1
  48.3 8.1 %collective-permute-done.1.refs_0_ = bf16[208,768]{1,0:T(8,128)(2,1)S(1)} collective-permute-done((bf16[208,768]{1,0:T(8,128)(2,1)S(1)}, bf16[208,768]{1,0:T(8,128)(2,1)S(1)}, u32[]{:S(2)}, u32[]{:S(2)}) %collective-permute-start.1) | collective-permute-done | bytes 319520 | tf_op jit(solution)/shard_map/ppermute | solution.py:861
  56.4 1.4 backward_start.1
  58.2 5.3 %backward_ffn.1 = (bf16[192,768]{1,0:T(8,128)(2,1)S(1)}, bf16[192,768]{1,0:T(8,128)(2,1)S(1)}, bf16[192,768]{1,0:T(8,128)(2,1)S(1)}, bf16[192,768]{1,0:T(8,128)(...) custom-call(bf16[192,1536]{1,0:T(8,128)(2,1)S(1)} %get-tuple-element, ...), custom_call_target="tpu_custom_call" | custom-call | flops 2717908 | bytes 14155 | tf_op jit(solution)/shard_map/backward_ffn/pallas_call | solution.py:428
  63.5 2.7 %collective-permute-done.6.refs_6_ = bf16[192,768]{1,0:T(8,128)(2,1)S(1)} collective-permute-done((bf16[192,768]{1,0:T(8,128)(2,1)S(1)}, bf16[192,768]{1,0:T(8,128)(2,1)S(1)}, u32[]{:S(2)}, u32[]{:S(2)}) %collective-permute-start.6) | collective-permute-done | bytes 294944 | tf_op jit(solution)/shard_map/ppermute | solution.py:725
  66.2 1.6 collective-permute-done.7.refs_7_
  67.8 1.9 product_down.1
  69.6 1.6 collective-permute-start.13
  71.9 0.5 collective-permute-start.11
  72.4 0.9 collective-permute-start.12
  73.3 7.9 %backward_attn.1 = (bf16[1,192,1536]{2,1,0:T(8,128)(2,1)}, bf16[208,3072]{1,0:T(8,128)(2,1)S(1)}, f32[8,768]{1,0:T(8,128)}) custom-call(bf16[192,768]{1,0:T(8,128)(2,1)S(1)} %get-tuple-element.111.datt_ref, bf16[192,768]{1,0:T(8,128)(2,1)S(1)} %get-tuple-element.101.q_ref, bf16[192,768]{1,0:T(8,128)(2,1)S(1)} %get-tuple-element.102.k_ref, ...), custom_call_target="tpu_custom_call" | custom-call | flops 1132462 | bytes 4718 | tf_op jit(solution)/shard_map/backward_attn/pallas_call | solution.py:508
  81.2 3.8 %collective-permute-done.13 = bf16[2,192,768]{2,1,0:T(8,128)(2,1)S(1)} collective-permute-done((bf16[2,192,768]{2,1,0:T(8,128)(2,1)S(1)}, bf16[2,192,768]{2,1,0:T(8,128)(2,1)S(1)}, u32[]{:S(2)}, u32[]{:S(2)}) %collective-permute-start.13) | collective-permute-done | bytes 589856 | tf_op jit(solution)/shard_map/ppermute | solution.py:725
  85.1 2.7 %collective-permute-start.14 = (bf16[192,768]{1,0:T(8,128)(2,1)S(1)}, bf16[192,768]{1,0:T(8,128)(2,1)S(1)}, u32[]{:S(2)}, u32[]{:S(2)}) collective-permute-start(bf16[192,768]{1,0:T(8,128)(2,1)S(1)} %fusion.2.refs_9_), channel_id=1, source_target_pairs={{0,8},{1,9},{2,10},{3,11},{4,12},{5,13},{6,14},{7,15},{8,0},{9,1},... | collective-permute-start | bytes 884744 | tf_op jit(solution)/shard_map/ppermute | solution.py:725
  87.8 1.6 product_gate.1
  89.5 1.6 collective-permute-start.20
  91.6 1.4 collective-permute-start.17
  93.0 7.8 %collective-permute-done.14 = bf16[192,768]{1,0:T(8,128)(2,1)S(1)} collective-permute-done((bf16[192,768]{1,0:T(8,128)(2,1)S(1)}, bf16[192,768]{1,0:T(8,128)(2,1)S(1)}, u32[]{:S(2)}, u32[]{:S(2)}) %collective-permute-start.14) | collective-permute-done | bytes 294944 | tf_op jit(solution)/shard_map/ppermute | solution.py:725
  100.8 8.8 %collective-permute-done.8.refs_3_ = bf16[192,384]{1,0:T(8,128)(2,1)S(1)} collective-permute-done((bf16[192,384]{1,0:T(8,128)(2,1)S(1)}, bf16[192,384]{1,0:T(8,128)(2,1)S(1)}, u32[]{:S(2)}, u32[]{:S(2)}) %collective-permute-start.8) | collective-permute-done | bytes 147488 | tf_op jit(solution)/shard_map/ppermute | solution.py:725
  109.6 0.6 collective-permute-start.19
  110.3 1.6 product_up.1
  111.9 0.5 collective-permute-start.21
  112.4 2.5 %collective-permute-start.22 = (bf16[192,768]{1,0:T(8,128)(2,1)S(1)}, bf16[192,768]{1,0:T(8,128)(2,1)S(1)}, u32[]{:S(2)}, u32[]{:S(2)}) collective-permute-start(bf16[192,768]{1,0:T(8,128)(2,1)S(1)} %fusion.3.refs_8_), channel_id=1, source_target_pairs={{0,8},{1,9},{2,10},{3,11},{4,12},{5,13},{6,14},{7,15},{8,0},{9,1},... | collective-permute-start | bytes 884744 | tf_op jit(solution)/shard_map/ppermute | solution.py:725
  114.9 16.5 %collective-permute-done.22 = bf16[192,768]{1,0:T(8,128)(2,1)S(1)} collective-permute-done((bf16[192,768]{1,0:T(8,128)(2,1)S(1)}, bf16[192,768]{1,0:T(8,128)(2,1)S(1)}, u32[]{:S(2)}, u32[]{:S(2)}) %collective-permute-start.22) | collective-permute-done | bytes 294944 | tf_op jit(solution)/shard_map/ppermute | solution.py:725
  131.5 1.9 %collective-permute-done.21 = bf16[2,192,768]{2,1,0:T(8,128)(2,1)S(1)} collective-permute-done((bf16[2,192,768]{2,1,0:T(8,128)(2,1)S(1)}, bf16[2,192,768]{2,1,0:T(8,128)(2,1)S(1)}, u32[]{:S(2)}, u32[]{:S(2)}) %collective-permute-start.21) | collective-permute-done | bytes 589856 | tf_op jit(solution)/shard_map/ppermute | solution.py:725
  133.5 6.4 %collective-permute-done.19.refs_6_ = bf16[208,3072]{1,0:T(8,128)(2,1)S(1)} collective-permute-done((bf16[208,3072]{1,0:T(8,128)(2,1)S(1)}, bf16[208,3072]{1,0:T(8,128)(2,1)S(1)}, u32[]{:S(2)}, u32[]{:S(2)}) %collective-permute-start.19) | collective-permute-done | bytes 1277984 | tf_op jit(solution)/shard_map/ppermute | solution.py:725
  139.9 3.0 %collective-permute-done.23.refs_7_ = bf16[208,3072]{1,0:T(8,128)(2,1)S(1)} collective-permute-done((bf16[208,3072]{1,0:T(8,128)(2,1)S(1)}, bf16[208,3072]{1,0:T(8,128)(2,1)S(1)}, u32[]{:S(2)}, u32[]{:S(2)}) %collective-permute-start.23) | collective-permute-done | bytes 1277984 | tf_op jit(solution)/shard_map/ppermute | solution.py:725
  142.9 4.1 %product_attn.1 = (bf16[112,1536]{1,0:T(8,128)(2,1)}, f32[2,48,1536]{2,1,0:T(8,128)S(1)}, f32[8,768]{1,0:T(8,128)S(1)}, bf16[2,48,1536]{2,1,0:T(8,128)(2,1)}, f32[2,48,1536]{2,1,0:T(8,128)S(1)}) custom-call(bf16[192,1152]{1,0:T(8,128)(2,1)S(1)} %get-tuple-element.116.refs_0_, bf16[192,1920]{1,0:T(8,128)(2,1)S(1)} %collective-permute-done.2.refs_0_.refs_1_, ...), custom_call_target="tpu_custom_call" | custom-call | flops 1 | bytes 1 | tf_op jit(solution)/shard_map/product_attn/pallas_call | solution.py:628
  147.5 1.3 collective-permute-start.28
  148.8 0.5 collective-permute-start.26
  149.3 15.2 %collective-permute-done.24.came_ref = bf16[112,1536]{1,0:T(8,128)(2,1)} collective-permute-done((bf16[112,1536]{1,0:T(8,128)(2,1)}, bf16[112,1536]{1,0:T(8,128)(2,1)}, u32[]{:S(2)}, u32[]{:S(2)}) %collective-permute-start.24) | collective-permute-done | bytes 344096 | tf_op jit(solution)/shard_map/ppermute | solution.py:725
  164.5 1.0 first_sum.1
  165.7 1.1 fusion
  166.9 0.6 collective-permute-start.30
  167.5 1.4 collective-permute-start.29
  168.9 3.2 %collective-permute-done.26 = bf16[2,48,1536]{2,1,0:T(8,128)(2,1)S(1)} collective-permute-done((bf16[2,48,1536]{2,1,0:T(8,128)(2,1)}, bf16[2,48,1536]{2,1,0:T(8,128)(2,1)S(1)}, u32[]{:S(2)}, u32[]{:S(2)}) %collective-permute-start.26) | collective-permute-done | bytes 294944 | tf_op jit(solution)/shard_map/ppermute | solution.py:725
  172.6 9.8 %collective-permute-done.27 = bf16[48,1536]{1,0:T(8,128)(2,1)S(1)} collective-permute-done((bf16[48,1536]{1,0:T(8,128)(2,1)S(1)}, bf16[48,1536]{1,0:T(8,128)(2,1)S(1)}, u32[]{:S(2)}, u32[]{:S(2)}) %collective-permute-start.27) | collective-permute-done | bytes 147488 | tf_op jit(solution)/shard_map/ppermute | solution.py:725
  182.4 0.7 fusion.6
  183.2 0.7 first_end.1
  184.1 0.5 fusion.8
  184.7 0.6 slice_bitcast_fusion
  185.2 0.6 reshape.52
  185.9 1.1 assemble.1
  (70 shorter events, 3.4 us)
Async XLA Ops:
  0.6 22.5 %copy-start.1 = (bf16[192,1536]{1,0:T(8,128)(2,1)S(1)}, bf16[192,1536]{1,0:T(8,128)(2,1)}, u32[]{:S(2)}) copy-start(bf16[192,1536]{1,0:T(8,128)(2,1)} %refs_0_.1) | copy-start | bytes 1769476
  0.7 22.5 %copy-start.7 = (s32[2,96]{1,0:T(2,128)S(1)}, s32[2,96]{1,0:T(2,128)}, u32[]{:S(2)}) copy-start(s32[2,96]{1,0:T(2,128)} %refs_2_.2) | copy-start | bytes 2308
  0.7 22.4 %copy-start.6 = (f32[1,2,2]{2,1,0:T(2,128)S(1)}, f32[1,2,2]{2,1,0:T(2,128)}, u32[]{:S(2)}) copy-start(f32[1,2,2]{2,1,0:T(2,128)} %mix_ref.3) | copy-start | bytes 52
  0.7 22.4 %copy-start.5 = (f32[1,2]{1,0:T(1,128)S(1)}, f32[1,2]{1,0:T(1,128)}, u32[]{:S(2)}) copy-start(f32[1,2]{1,0:T(1,128)} %cor_ref.5) | copy-start | bytes 28
  0.7 22.4 %copy-start.4 = (f32[1,768]{1,0:T(1,128)S(1)}, f32[1,768]{1,0:T(1,128)}, u32[]{:S(2)}) copy-start(f32[1,768]{1,0:T(1,128)} %ga_ref.3) | copy-start | bytes 9220
  0.7 22.4 %copy-start.3 = (f32[1,768]{1,0:T(1,128)S(1)}, f32[1,768]{1,0:T(1,128)}, u32[]{:S(2)}) copy-start(f32[1,768]{1,0:T(1,128)} %gf_ref.3) | copy-start | bytes 9220
  12.6 10.5 %collective-permute-start = (bf16[208,768]{1,0:T(8,128)(2,1)S(1)}, bf16[208,768]{1,0:T(8,128)(2,1)S(1)}, u32[]{:S(2)}, u32[]{:S(2)}) collective-permute-start(bf16[208,768]{1,0:T(8,128)(2,1)S(1)} %get-tuple-element.89), channel_id=1, source_target_pairs={{0,16},{16,0},{1,17},{17,1},{2,18},{18,2},{3,19},{19,3},{4,20},{20... | collective-permute-start | bytes 958472 | tf_op jit(solution)/shard_map/ppermute | solution.py:852
  23.1 10.8 %copy-start.2 = (bf16[192,1536]{1,0:T(8,128)(2,1)S(1)}, bf16[192,1536]{1,0:T(8,128)(2,1)}, u32[]{:S(2)}) copy-start(bf16[192,1536]{1,0:T(8,128)(2,1)} %refs_1_.1) | copy-start | bytes 1769476
  23.2 10.8 %copy-start.8 = (s32[2]{0:T(128)S(1)}, s32[2]{0:T(128)}, u32[]{:S(2)}) copy-start(s32[2]{0:T(128)} %refs_2_.3) | copy-start | bytes 28
  32.2 26.0 %collective-permute-start.2 = (bf16[192,1920]{1,0:T(8,128)(2,1)S(1)}, bf16[192,1920]{1,0:T(8,128)(2,1)S(1)}, u32[]{:S(2)}, u32[]{:S(2)}) collective-permute-start(bf16[192,1920]{1,0:T(8,128)(2,1)S(1)} %get-tuple-element.108), channel_id=1, source_target_pairs={{0,1},{1,0},{2,3},{3,2},{4,5},{5,4},{6,7},{7,6},{8,9},{9,8},{10,11... | collective-permute-start | bytes 2211848 | tf_op jit(solution)/shard_map/ppermute | solution.py:725
  32.2 26.0 %collective-permute-start.3 = (bf16[192,1920]{1,0:T(8,128)(2,1)S(1)}, bf16[192,1920]{1,0:T(8,128)(2,1)S(1)}, u32[]{:S(2)}, u32[]{:S(2)}) collective-permute-start(bf16[192,1920]{1,0:T(8,128)(2,1)S(1)} %get-tuple-element.109), channel_id=1, source_target_pairs={{0,2},{1,3},{2,0},{3,1},{4,6},{5,7},{6,4},{7,5},{8,10},{9,11},{10,... | collective-permute-start | bytes 2211848 | tf_op jit(solution)/shard_map/ppermute | solution.py:725
  46.7 9.7 %collective-permute-start.1 = (bf16[208,768]{1,0:T(8,128)(2,1)S(1)}, bf16[208,768]{1,0:T(8,128)(2,1)S(1)}, u32[]{:S(2)}, u32[]{:S(2)}) collective-permute-start(bf16[208,768]{1,0:T(8,128)(2,1)S(1)} %backward_relay.1), channel_id=1, source_target_pairs={{0,16},{16,0},{1,17},{17,1},{2,18},{18,2},{3,19},{19,3},{4,20},{20... | collective-permute-start | bytes 958472 | tf_op jit(solution)/shard_map/ppermute | solution.py:861
  48.2 9.9 %collective-permute-start.4 = (bf16[192,768]{1,0:T(8,128)(2,1)S(1)}, bf16[192,768]{1,0:T(8,128)(2,1)S(1)}, u32[]{:S(2)}, u32[]{:S(2)}) collective-permute-start(bf16[192,768]{1,0:T(8,128)(2,1)S(1)} %get-tuple-element.110), channel_id=1, source_target_pairs={{0,3},{1,2},{2,1},{3,0},{4,7},{5,6},{6,5},{7,4},{8,11},{9,10},{10,... | collective-permute-start | bytes 884744 | tf_op jit(solution)/shard_map/ppermute | solution.py:725
  57.8 8.4 %collective-permute-start.6 = (bf16[192,768]{1,0:T(8,128)(2,1)S(1)}, bf16[192,768]{1,0:T(8,128)(2,1)S(1)}, u32[]{:S(2)}, u32[]{:S(2)}) collective-permute-start(bf16[192,768]{1,0:T(8,128)(2,1)S(1)} %get-tuple-element.107.low_ref.refs_4_), channel_id=1, source_target_pairs={{0,2},{1,3},{2,0},{3,1},{4,6},{5,7},{6,4},{7,5},{8,10},{9,11},{10,... | collective-permute-start | bytes 884744 | tf_op jit(solution)/shard_map/ppermute | solution.py:725
  58.2 8.0 %collective-permute-start.5 = (bf16[192,768]{1,0:T(8,128)(2,1)S(1)}, bf16[192,768]{1,0:T(8,128)(2,1)S(1)}, u32[]{:S(2)}, u32[]{:S(2)}) collective-permute-start(bf16[192,768]{1,0:T(8,128)(2,1)S(1)} %get-tuple-element.107.low_ref.refs_4_), channel_id=1, source_target_pairs={{0,1},{1,0},{2,3},{3,2},{4,5},{5,4},{6,7},{7,6},{8,9},{9,8},{10,11... | collective-permute-start | bytes 884744 | tf_op jit(solution)/shard_map/ppermute | solution.py:725
  66.2 1.6 collective-permute-start.7
  69.6 15.4 %collective-permute-start.13 = (bf16[2,192,768]{2,1,0:T(8,128)(2,1)S(1)}, bf16[2,192,768]{2,1,0:T(8,128)(2,1)S(1)}, u32[]{:S(2)}, u32[]{:S(2)}) collective-permute-start(bf16[2,192,768]{2,1,0:T(8,128)(2,1)S(1)} %get-tuple-element.119.before), channel_id=1, source_target_pairs={{0,4},{1,5},{2,6},{3,7},{4,0},{5,1},{6,2},{7,3},{8,12},{9,13},{10,... | collective-permute-start | bytes 1769480 | tf_op jit(solution)/shard_map/ppermute | solution.py:725
  71.3 16.5 %collective-permute-start.9 = (bf16[192,768]{1,0:T(8,128)(2,1)S(1)}, bf16[192,768]{1,0:T(8,128)(2,1)S(1)}, u32[]{:S(2)}, u32[]{:S(2)}) collective-permute-start(bf16[192,768]{1,0:T(8,128)(2,1)S(1)} %slice.109.refs_2_), channel_id=1, source_target_pairs={{0,1},{1,0},{2,3},{3,2},{4,5},{5,4},{6,7},{7,6},{8,9},{9,8},{10,11... | collective-permute-start | bytes 884744 | tf_op jit(solution)/shard_map/ppermute | solution.py:725
  71.4 16.4 %collective-permute-start.10 = (bf16[192,768]{1,0:T(8,128)(2,1)S(1)}, bf16[192,768]{1,0:T(8,128)(2,1)S(1)}, u32[]{:S(2)}, u32[]{:S(2)}) collective-permute-start(bf16[192,768]{1,0:T(8,128)(2,1)S(1)} %get-tuple-element.130), channel_id=1, source_target_pairs={{0,1},{1,0},{2,3},{3,2},{4,5},{5,4},{6,7},{7,6},{8,9},{9,8},{10,11... | collective-permute-start | bytes 884744 | tf_op jit(solution)/shard_map/ppermute | solution.py:725
  71.9 15.9 %collective-permute-start.11 = (bf16[192,768]{1,0:T(8,128)(2,1)S(1)}, bf16[192,768]{1,0:T(8,128)(2,1)S(1)}, u32[]{:S(2)}, u32[]{:S(2)}) collective-permute-start(bf16[192,768]{1,0:T(8,128)(2,1)S(1)} %get-tuple-element.131), channel_id=1, source_target_pairs={{0,2},{1,3},{2,0},{3,1},{4,6},{5,7},{6,4},{7,5},{8,10},{9,11},{10,... | collective-permute-start | bytes 884744 | tf_op jit(solution)/shard_map/ppermute | solution.py:725
  72.4 15.4 %collective-permute-start.12 = (bf16[192,768]{1,0:T(8,128)(2,1)S(1)}, bf16[192,768]{1,0:T(8,128)(2,1)S(1)}, u32[]{:S(2)}, u32[]{:S(2)}) collective-permute-start(bf16[192,768]{1,0:T(8,128)(2,1)S(1)} %get-tuple-element.132), channel_id=1, source_target_pairs={{0,3},{1,2},{2,1},{3,0},{4,7},{5,6},{6,5},{7,4},{8,11},{9,10},{10,... | collective-permute-start | bytes 884744 | tf_op jit(solution)/shard_map/ppermute | solution.py:725
  85.1 15.6 %collective-permute-start.14 = (bf16[192,768]{1,0:T(8,128)(2,1)S(1)}, bf16[192,768]{1,0:T(8,128)(2,1)S(1)}, u32[]{:S(2)}, u32[]{:S(2)}) collective-permute-start(bf16[192,768]{1,0:T(8,128)(2,1)S(1)} %fusion.2.refs_9_), channel_id=1, source_target_pairs={{0,8},{1,9},{2,10},{3,11},{4,12},{5,13},{6,14},{7,15},{8,0},{9,1},... | collective-permute-start | bytes 884744 | tf_op jit(solution)/shard_map/ppermute | solution.py:725
  89.5 20.8 %collective-permute-start.20 = (bf16[2,192,768]{2,1,0:T(8,128)(2,1)S(1)}, bf16[2,192,768]{2,1,0:T(8,128)(2,1)S(1)}, u32[]{:S(2)}, u32[]{:S(2)}) collective-permute-start(bf16[2,192,768]{2,1,0:T(8,128)(2,1)S(1)} %get-tuple-element.135), channel_id=1, source_target_pairs={{0,4},{1,5},{2,6},{3,7},{4,0},{5,1},{6,2},{7,3},{8,12},{9,13},{10,... | collective-permute-start | bytes 1769480 | tf_op jit(solution)/shard_map/ppermute | solution.py:725
  91.1 18.5 %collective-permute-start.15 = (bf16[192,768]{1,0:T(8,128)(2,1)S(1)}, bf16[192,768]{1,0:T(8,128)(2,1)S(1)}, u32[]{:S(2)}, u32[]{:S(2)}) collective-permute-start(bf16[192,768]{1,0:T(8,128)(2,1)S(1)} %get-tuple-element.136), channel_id=1, source_target_pairs={{0,1},{1,0},{2,3},{3,2},{4,5},{5,4},{6,7},{7,6},{8,9},{9,8},{10,11... | collective-permute-start | bytes 884744 | tf_op jit(solution)/shard_map/ppermute | solution.py:725
  91.1 18.5 %collective-permute-start.16 = (bf16[192,768]{1,0:T(8,128)(2,1)S(1)}, bf16[192,768]{1,0:T(8,128)(2,1)S(1)}, u32[]{:S(2)}, u32[]{:S(2)}) collective-permute-start(bf16[192,768]{1,0:T(8,128)(2,1)S(1)} %get-tuple-element.137), channel_id=1, source_target_pairs={{0,2},{1,3},{2,0},{3,1},{4,6},{5,7},{6,4},{7,5},{8,10},{9,11},{10,... | collective-permute-start | bytes 884744 | tf_op jit(solution)/shard_map/ppermute | solution.py:725
  91.6 18.0 %collective-permute-start.17 = (bf16[192,768]{1,0:T(8,128)(2,1)S(1)}, bf16[192,768]{1,0:T(8,128)(2,1)S(1)}, u32[]{:S(2)}, u32[]{:S(2)}) collective-permute-start(bf16[192,768]{1,0:T(8,128)(2,1)S(1)} %get-tuple-element.138), channel_id=1, source_target_pairs={{0,3},{1,2},{2,1},{3,0},{4,7},{5,6},{6,5},{7,4},{8,11},{9,10},{10,... | collective-permute-start | bytes 884744 | tf_op jit(solution)/shard_map/ppermute | solution.py:725
  100.7 8.9 %collective-permute-start.8 = (bf16[192,384]{1,0:T(8,128)(2,1)S(1)}, bf16[192,384]{1,0:T(8,128)(2,1)S(1)}, u32[]{:S(2)}, u32[]{:S(2)}) collective-permute-start(bf16[192,384]{1,0:T(8,128)(2,1)S(1)} %get-tuple-element.127), channel_id=1, source_target_pairs={{0,3},{1,2},{2,1},{3,0},{4,7},{5,6},{6,5},{7,4},{8,11},{9,10},{10,... | collective-permute-start | bytes 442376 | tf_op jit(solution)/shard_map/ppermute | solution.py:725
  100.8 11.0 %copy-start = (f32[192,768]{1,0:T(8,128)}, f32[192,768]{1,0:T(8,128)S(1)}, u32[]{:S(2)}) copy-start(f32[192,768]{1,0:T(8,128)S(1)} %bitcast_add_fusion.2.refs_9_) | copy-start | bytes 1769476
  109.6 30.3 %collective-permute-start.19 = (bf16[208,3072]{1,0:T(8,128)(2,1)S(1)}, bf16[208,3072]{1,0:T(8,128)(2,1)S(1)}, u32[]{:S(2)}, u32[]{:S(2)}) collective-permute-start(bf16[208,3072]{1,0:T(8,128)(2,1)S(1)} %get-tuple-element.139.refs_8_.refs_4_), channel_id=1, source_target_pairs={{0,2},{1,3},{2,0},{3,1},{4,6},{5,7},{6,4},{7,5},{8,10},{9,11},{10,... | collective-permute-start | bytes 3833864 | tf_op jit(solution)/shard_map/ppermute | solution.py:725
  111.9 21.5 %collective-permute-start.21 = (bf16[2,192,768]{2,1,0:T(8,128)(2,1)S(1)}, bf16[2,192,768]{2,1,0:T(8,128)(2,1)S(1)}, u32[]{:S(2)}, u32[]{:S(2)}) collective-permute-start(bf16[2,192,768]{2,1,0:T(8,128)(2,1)S(1)} %get-tuple-element.143), channel_id=1, source_target_pairs={{0,4},{1,5},{2,6},{3,7},{4,0},{5,1},{6,2},{7,3},{8,12},{9,13},{10,... | collective-permute-start | bytes 1769480 | tf_op jit(solution)/shard_map/ppermute | solution.py:725
  112.4 19.0 %collective-permute-start.22 = (bf16[192,768]{1,0:T(8,128)(2,1)S(1)}, bf16[192,768]{1,0:T(8,128)(2,1)S(1)}, u32[]{:S(2)}, u32[]{:S(2)}) collective-permute-start(bf16[192,768]{1,0:T(8,128)(2,1)S(1)} %fusion.3.refs_8_), channel_id=1, source_target_pairs={{0,8},{1,9},{2,10},{3,11},{4,12},{5,13},{6,14},{7,15},{8,0},{9,1},... | collective-permute-start | bytes 884744 | tf_op jit(solution)/shard_map/ppermute | solution.py:725
  114.9 25.0 %collective-permute-start.18 = (bf16[208,3072]{1,0:T(8,128)(2,1)S(1)}, bf16[208,3072]{1,0:T(8,128)(2,1)S(1)}, u32[]{:S(2)}, u32[]{:S(2)}) collective-permute-start(bf16[208,3072]{1,0:T(8,128)(2,1)S(1)} %get-tuple-element.139.refs_8_.refs_4_), channel_id=1, source_target_pairs={{0,1},{1,0},{2,3},{3,2},{4,5},{5,4},{6,7},{7,6},{8,9},{9,8},{10,11... | collective-permute-start | bytes 3833864 | tf_op jit(solution)/shard_map/ppermute | solution.py:725
  133.4 13.6 %copy-start.9 = (bf16[2,192,768]{2,1,0:T(8,128)(2,1)}, bf16[2,192,768]{2,1,0:T(8,128)(2,1)S(1)}, u32[]{:S(2)}) copy-start(bf16[2,192,768]{2,1,0:T(8,128)(2,1)S(1)} %collective-permute-done.21) | copy-start | bytes 1769476
  139.9 3.0 %collective-permute-start.23 = (bf16[208,3072]{1,0:T(8,128)(2,1)S(1)}, bf16[208,3072]{1,0:T(8,128)(2,1)S(1)}, u32[]{:S(2)}, u32[]{:S(2)}) collective-permute-start(bf16[208,3072]{1,0:T(8,128)(2,1)S(1)} %collective-permute-done.19.refs_6_), channel_id=1, source_target_pairs={{0,1},{1,0},{2,3},{3,2},{4,5},{5,4},{6,7},{7,6},{8,9},{9,8},{10,11... | collective-permute-start | bytes 3833864 | tf_op jit(solution)/shard_map/ppermute | solution.py:725
  147.0 17.5 %collective-permute-start.24 = (bf16[112,1536]{1,0:T(8,128)(2,1)}, bf16[112,1536]{1,0:T(8,128)(2,1)}, u32[]{:S(2)}, u32[]{:S(2)}) collective-permute-start(bf16[112,1536]{1,0:T(8,128)(2,1)} %get-tuple-element.146), channel_id=1, source_target_pairs={{0,4},{1,5},{2,6},{3,7},{4,0},{5,1},{6,2},{7,3},{8,12},{9,13},{10,... | collective-permute-start | bytes 1032200 | tf_op jit(solution)/shard_map/ppermute | solution.py:725
  147.5 18.2 %collective-permute-start.28 = (bf16[192,768]{1,0:T(8,128)(2,1)S(1)}, bf16[192,768]{1,0:T(8,128)(2,1)S(1)}, u32[]{:S(2)}, u32[]{:S(2)}) collective-permute-start(bf16[192,768]{1,0:T(8,128)(2,1)S(1)} %fusion.4.refs_8_), channel_id=1, source_target_pairs={{0,8},{1,9},{2,10},{3,11},{4,12},{5,13},{6,14},{7,15},{8,0},{9,1},... | collective-permute-start | bytes 884744 | tf_op jit(solution)/shard_map/ppermute | solution.py:725
  148.8 23.3 %collective-permute-start.26 = (bf16[2,48,1536]{2,1,0:T(8,128)(2,1)}, bf16[2,48,1536]{2,1,0:T(8,128)(2,1)S(1)}, u32[]{:S(2)}, u32[]{:S(2)}) collective-permute-start(bf16[2,48,1536]{2,1,0:T(8,128)(2,1)} %get-tuple-element.154), channel_id=1, source_target_pairs={{0,4},{1,5},{2,6},{3,7},{4,0},{5,1},{6,2},{7,3},{8,12},{9,13},{10,... | collective-permute-start | bytes 884744 | tf_op jit(solution)/shard_map/ppermute | solution.py:725
  165.6 17.6 %collective-permute-start.25 = (bf16[64,1536]{1,0:T(8,128)(2,1)S(1)}, bf16[64,1536]{1,0:T(8,128)(2,1)S(1)}, u32[]{:S(2)}, u32[]{:S(2)}) collective-permute-start(bf16[64,1536]{1,0:T(8,128)(2,1)S(1)} %get-tuple-element.149), channel_id=1, source_target_pairs={{0,8},{1,9},{2,10},{3,11},{4,12},{5,13},{6,14},{7,15},{8,0},{9,1},... | collective-permute-start | bytes 589832 | tf_op jit(solution)/shard_map/ppermute | solution.py:725
  166.8 17.2 %collective-permute-start.31 = (bf16[48,1536]{1,0:T(8,128)(2,1)S(1)}, bf16[48,1536]{1,0:T(8,128)(2,1)S(1)}, u32[]{:S(2)}, u32[]{:S(2)}) collective-permute-start(bf16[48,1536]{1,0:T(8,128)(2,1)S(1)} %pad_maximum_fusion.3), channel_id=1, source_target_pairs={{0,3},{1,2},{2,1},{3,0},{4,7},{5,6},{6,5},{7,4},{8,11},{9,10},{10,... | collective-permute-start | bytes 442376 | tf_op jit(solution)/shard_map/ppermute | solution.py:725
  166.9 17.1 %collective-permute-start.30 = (bf16[48,1536]{1,0:T(8,128)(2,1)S(1)}, bf16[48,1536]{1,0:T(8,128)(2,1)S(1)}, u32[]{:S(2)}, u32[]{:S(2)}) collective-permute-start(bf16[48,1536]{1,0:T(8,128)(2,1)S(1)} %pad_maximum_fusion.2), channel_id=1, source_target_pairs={{0,2},{1,3},{2,0},{3,1},{4,6},{5,7},{6,4},{7,5},{8,10},{9,11},{10,... | collective-permute-start | bytes 442376 | tf_op jit(solution)/shard_map/ppermute | solution.py:725
  167.5 16.5 %collective-permute-start.29 = (bf16[48,1536]{1,0:T(8,128)(2,1)S(1)}, bf16[48,1536]{1,0:T(8,128)(2,1)S(1)}, u32[]{:S(2)}, u32[]{:S(2)}) collective-permute-start(bf16[48,1536]{1,0:T(8,128)(2,1)S(1)} %pad_maximum_fusion.1), channel_id=1, source_target_pairs={{0,1},{1,0},{2,3},{3,2},{4,5},{5,4},{6,7},{7,6},{8,9},{9,8},{10,11... | collective-permute-start | bytes 442376 | tf_op jit(solution)/shard_map/ppermute | solution.py:725
  172.2 10.2 %collective-permute-start.27 = (bf16[48,1536]{1,0:T(8,128)(2,1)S(1)}, bf16[48,1536]{1,0:T(8,128)(2,1)S(1)}, u32[]{:S(2)}, u32[]{:S(2)}) collective-permute-start(bf16[48,1536]{1,0:T(8,128)(2,1)S(1)} %get-tuple-element.165), channel_id=1, source_target_pairs={{0,8},{1,9},{2,10},{3,11},{4,12},{5,13},{6,14},{7,15},{8,0},{9,1},... | collective-permute-start | bytes 442376 | tf_op jit(solution)/shard_map/ppermute | solution.py:725
where the time goes:
time: 187 us
  waiting for transfers between devices  96.3 us (51%)
  Pallas kernels  60.2 us (32%)
  starting transfers between devices  25.1 us (13%)
  other arithmetic  2.35 us (1%)
  local copies, waits for them, and re-layouts  1.99 us (1%)
    ppermute x30, waiting for transfers between devices, exchange(): lax.ppermute(value, 'dp', [(source, source ^ flips) for source in range(c...  80.7 us
    ppermute x30, starting transfers between devices, exchange(): lax.ppermute(value, 'dp', [(source, source ^ flips) for source in range(c...  20.5 us
    ppermute x2, waiting for transfers between devices, local(): message = lax.ppermute(message, 'section', [(0, 1), (1, 0)])  15.7 us
    pallas_call x1, Pallas kernels, relay_backward(): pl.pallas_call(relay_kernel, out_shape=shape((tokens + EXTRA, width), bfl...  12.7 us
    pallas_call x1, Pallas kernels, forward_lite(): pl.pallas_call(forward_lite_kernel, out_shape=[jax.ShapeDtypeStruct((toke...  11.9 us
    pallas_call x1, Pallas kernels, forward(): pl.pallas_call(lambda *refs: forward_kernel(fast, *refs), out_shape=[shap...  9.02 us
    pallas_call x1, Pallas kernels, attn_backward(): pl.pallas_call(attn_kernel, out_shape=[shape((1, tokens, 2 * width), bflo...  7.91 us
    pallas_call x1, Pallas kernels, ffn_backward(): pl.pallas_call(ffn_kernel, out_shape=[shape((tokens, width), bfloat)] * 8...  5.34 us
  transfers between devices with their start and end apart: 32, of which 14 were waited for; matrix products, arithmetic and copies ran while one was open for 1% of the time, Pallas kernels for 17%

commit v1 on v0

--- a/solution.py
+++ b/solution.py
@@ -15,6 +15,7 @@
 GELU_A = 0.7978845608028654
 GELU_B = 0.044715
 EXTRA = 16
+CHUNK = 256
 SCOPED = 12
 bfloat = jnp.bfloat16
 floating = jnp.float32
@@ -346,21 +347,21 @@
     section = lax.axis_index("section")
     if message is not None:
         got = read_scalars(message[tokens : tokens + EXTRA, :PAIR].astype(floating), 4)
-    place = lax.broadcasted_iota(jnp.int32, (length, width), 0)
-    for row in range(rows):
-        span = slice(row * length, (row + 1) * length)
-        valid = place < counts_ref[row]
-        own_a = jnp.where(valid, grad_ref[span, :width].astype(floating), 0.0)
-        own_b = jnp.where(valid, grad_ref[span, width:].astype(floating), 0.0)
-        if message is not None:
-            later_b = own_b + message[span, :].astype(floating)
-            far_a = own_a + (got[0] * own_a + got[2] * later_b)
-            far_b = later_b + (got[1] * own_a + got[3] * later_b)
-            own_a = jnp.where(section == 0, far_a, own_a).astype(bfloat).astype(floating)
-            own_b = jnp.where(section == 0, far_b, own_b).astype(bfloat).astype(floating)
-        g_ref[span, :width] = own_a.astype(bfloat)
-        g_ref[span, width:] = own_b.astype(bfloat)
-        low_ref[span, :] = (cor_ref[0, 0] * own_a + cor_ref[0, 1] * own_b).astype(bfloat)
+    place = lax.broadcasted_iota(jnp.int32, (tokens, width), 0)
+    valid = place < counts_ref[0]
+    for row in range(1, rows):
+        valid = valid | ((place >= row * length) & (place < row * length + counts_ref[row]))
+    own_a = jnp.where(valid, grad_ref[:, :width].astype(floating), 0.0)
+    own_b = jnp.where(valid, grad_ref[:, width:].astype(floating), 0.0)
+    if message is not None:
+        later_b = own_b + message[:tokens, :].astype(floating)
+        far_a = own_a + (got[0] * own_a + got[2] * later_b)
+        far_b = later_b + (got[1] * own_a + got[3] * later_b)
+        own_a = jnp.where(section == 0, far_a, own_a).astype(bfloat).astype(floating)
+        own_b = jnp.where(section == 0, far_b, own_b).astype(bfloat).astype(floating)
+    g_ref[:, :width] = own_a.astype(bfloat)
+    g_ref[:, width:] = own_b.astype(bfloat)
+    low_ref[...] = (cor_ref[0, 0] * own_a + cor_ref[0, 1] * own_b).astype(bfloat)
 
 
 def start(message, out_grad, counts, correction, before):
@@ -526,17 +527,7 @@
                  acc, g_in, low_ref, do_ref, dqkv_ref):
     tokens, width = low_ref.shape
     start_rows(None, grad_in, counts_ref, cor_ref, g_in, low_ref)
-    acc[...] = jnp.zeros_like(acc)
-
-    def one_piece(piece, carry):
-        span = pl.ds(pl.multiple_of(piece * width, width), width)
-        grad_hidden = dot_t(low_ref[...], wd[0, span, :])
-        dgate = (grad_hidden * one[piece]).astype(bfloat)
-        dup = (grad_hidden * two[piece]).astype(bfloat)
-        acc[...] += dot_t(dgate, wg[0, :, span]) + dot_t(dup, wu[0, :, span])
-        return carry
-
-    lax.fori_loop(0, one.shape[0], one_piece, 0)
+    ffn_steps(low_ref, one, two, wg, wu, wd, acc, lambda *parts: None)
     grad_values = norm_backward(mid_ref[...], gf_ref[...], acc[...], False)[1]
     cor = [cor_ref[0, i] for i in range(2)]
     block = cor[0] * g_in[:, :width].astype(floating) + cor[1] * g_in[:, width:].astype(floating)
@@ -572,39 +563,62 @@
       *weights)
 
 
-def quarter_kernel(base, products, block, refs):
-    count = 4
-    lefts = refs[:count]
-    rights = refs[count : 2 * count]
-    send_ref, keep_ref = refs[-2:]
-    quarter_parts(base, products, block, lefts, rights, send_ref, keep_ref)
-
-
-def quarter_parts(base, products, block, lefts, rights, send_ref, keep_ref):
+def quarter_parts(base, products, block, lefts, rights, own_ref, far_ref, keep_ref):
     tokens = lefts[0].shape[0]
     tail = lefts[0].shape[1] - lefts[-1].shape[1]
     index = lax.axis_index("dp")
     near = (index >> 2) & 1
     far = (index >> 3) & 1
     for left_at, left_wide, right_at, right_wide in products:
-        columns = slice(right_at, right_at + right_wide)
-        total = 0.0
-        for left, right in zip(lefts, rights):
-            at = left_at if left.shape[1] > left_at else left_at - tail
-            total = total + t_dot(left[:, at : at + left_wide], right[:tokens, columns])
-        span = slice(right_at - base, right_at - base + right_wide)
-        for place in range(4):
-            part = total[place * block : (place + 1) * block, :]
-            slot = (place >> 1) ^ far
-            mine = (place & 1) == near
-
-            @pl.when(mine)
-            def _():
-                keep_ref[slot, :, span] = part
-
-            @pl.when(jnp.logical_not(mine))
-            def _():
-                send_ref[slot, :, span] = part.astype(bfloat)
+        starts = [left_at if left.shape[1] > left_at else left_at - tail for left in lefts]
+
+        def one_chunk(step, carry, starts=starts, left_wide=left_wide, right_at=right_at):
+            columns = pl.ds(pl.multiple_of(right_at + step * CHUNK, PAIR), CHUNK)
+            span = pl.ds(pl.multiple_of(right_at - base + step * CHUNK, PAIR), CHUNK)
+            total = 0.0
+            for left, right, at in zip(lefts, rights, starts):
+                total = total + t_dot(left[:, at : at + left_wide], right[:tokens, columns])
+            for place in range(4):
+                part = total[place * block : (place + 1) * block, :]
+                slot = (place >> 1) ^ far
+                mine = (place & 1) == near
+
+                @pl.when(mine)
+                def _():
+                    keep_ref[slot, :, span] = part
+
+                @pl.when(jnp.logical_and(jnp.logical_not(mine), slot == 0))
+                def _():
+                    own_ref[:block, span] = part.astype(bfloat)
+
+                @pl.when(jnp.logical_and(jnp.logical_not(mine), slot == 1))
+                def _():
+                    far_ref[:block, span] = part.astype(bfloat)
+
+            return carry
+
+        lax.fori_loop(0, right_wide // CHUNK, one_chunk, 0)
+
+
+def quarter_product(lefts, rights, block, before, name, parted):
+    rows, wide = lefts[0].shape[0], rights[0].shape[1]
+    shape = jax.ShapeDtypeStruct
+    products = [(0, 4 * block, 0, wide)]
+    sends = [shape((block, wide), bfloat)] * 2 if parted else [shape((2, block, wide), bfloat)]
+
+    def kernel(*refs):
+        own_ref, far_ref = refs[-3:-1] if parted else (refs[-2].at[0], refs[-2].at[1])
+        quarter_parts(0, products, block, refs[:4], refs[4:8], own_ref, far_ref, refs[-1])
+
+    return pl.pallas_call(
+        kernel,
+        out_shape=sends + [shape((2, block, wide), floating)],
+        in_specs=[VMEM] * 8 + [ANY] * len(before),
+        out_specs=[VMEM] * (len(sends) + 1),
+        compiler_params=params(SCOPED),
+        cost_estimate=cost(32 * rows * block * wide, 16 * block * wide),
+        name=name,
+    )(*lefts, *rights, *before)
 
 
 def attn_product_kernel(halves, block, refs):
@@ -612,13 +626,12 @@
     first_send, first_keep, small_ref, second_send, second_keep, stage = refs[-6:]
     tokens = lefts[0].shape[0]
     wide = first_keep.shape[2]
-    quarter_parts(0, halves[0], block, lefts, rights, stage, first_keep)
-    first_send[:block, :] = stage[0]
-    first_send[block : 2 * block, :] = stage[1]
+    quarter_parts(0, halves[0], block, lefts, rights, first_send, stage, first_keep)
+    first_send[block : 2 * block, :] = stage[...]
     small = sum(gathered_parts(right[tokens:, :wide]) for right in rights)
     small_ref[...] = small
     first_send[2 * block :, :] = spread(small)
-    quarter_parts(wide, halves[1], block, lefts, rights, second_send, second_keep)
+    quarter_parts(wide, halves[1], block, lefts, rights, second_send.at[0], second_send.at[1], second_keep)
 
 
 def attn_product(lefts, rights, halves, block, before):
@@ -630,7 +643,7 @@
         out_shape=[shape((2 * block + EXTRA, wide), bfloat), keep, shape((8, wide // 2), floating), send, keep],
         in_specs=[VMEM] * 8 + [ANY] * len(before),
         out_specs=[VMEM] * 5,
-        scratch_shapes=[pltpu.VMEM(send.shape, bfloat)],
+        scratch_shapes=[pltpu.VMEM(send.shape[1:], bfloat)],
         compiler_params=params(SCOPED),
         cost_estimate=cost(wide, wide),
         name="product_attn",
@@ -679,22 +692,6 @@
         cost_estimate=cost(wide, wide),
         name="first_end",
     )(held, came, small)
-
-
-def quarter_product(lefts, rights, products, block, before, name):
-    base = products[0][2]
-    wide = sum(one[3] for one in products)
-    shape = jax.ShapeDtypeStruct
-    flops = sum(2 * 4 * lefts[0].shape[0] * one[1] * one[3] for one in products)
-    return pl.pallas_call(
-        lambda *refs: quarter_kernel(base, products, block, refs),
-        out_shape=[shape((2, block, wide), bfloat), shape((2, block, wide), floating)],
-        in_specs=[VMEM] * 8 + [ANY] * len(before),
-        out_specs=[VMEM, VMEM],
-        compiler_params=params(SCOPED),
-        cost_estimate=cost(flops, 12 * block * wide),
-        name=name,
-    )(*lefts, *rights, *before)
 
 
 def assemble_kernel(own, one, two, three, gate_ref, up_ref):
@@ -783,6 +780,12 @@
     return [pieces[0]] + [exchange(pieces[flips], flips) for flips in (1, 2, 3)]
 
 
+def parts_once(product, *earlier):
+    own, far, keep = product
+    own, far = after((exchange(own, 4), exchange(far, 4)), *earlier)
+    return keep[0] + own.astype(floating), (keep[1] + far.astype(floating)).astype(bfloat)
+
+
 def sum_once(pair, *earlier):
     send, keep = pair
     arrived = after(exchange(send, 4), *earlier)
@@ -803,16 +806,15 @@
     width = normed_ffn[0].shape[1]
     share = width // 16
     block = 4 * share
-    whole = [(0, width, 0, width)]
     gates = swapped(slots[:4])
     ups, nearby = after((slots[4:], nearby), right)
     ups, nearby = swapped(list(ups)), exchange(nearby, 3)
     down_sums = sum_once(down_pair, right)
-    gate_pair = quarter_product(normed_ffn, gates, whole, block, [right, down_sums[1]], "product_gate")
+    gate_pair = quarter_product(normed_ffn, gates, block, [right, down_sums[1]], "product_gate", True)
     grad_down = sum_twice(*down_sums)
-    rights = gather_start(after(right, gate_pair[0], grad_down, ups[1:], nearby))
-    gate_sums = sum_once(gate_pair)
-    up_pair = quarter_product(normed_ffn, ups, whole, block, [gate_sums[1], grad_down], "product_up")
+    rights = gather_start(after(right, gate_pair[0], ups[1:]))
+    gate_sums = parts_once(gate_pair)
+    up_pair = quarter_product(normed_ffn, ups, block, [gate_sums[1], grad_down, nearby], "product_up", False)
     up_sums = sum_once(up_pair)
     gate_tile = sum_twice(*gate_sums).astype(bfloat)
     rights = gather_end(rights, up_sums[1], gate_tile)
@@ -866,7 +868,7 @@
         lows = gather_end(gather_start(low), before)
         beside, across = (one[:, width + width // 2 :] for one in kept[1:3])
         normed_ffn = gather_end([normed_ffn, beside, across], before)
-        down_pair = quarter_product(kept, lows, [(0, width, 0, width)], width // 4, [before], "product_down")
+        down_pair = quarter_product(kept, lows, width // 4, [before], "product_down", False)
         before = down_pair[0]
     state_grads, right, small = attn_backward(x, g_in, grad_middle, grad_att, active, change, queries, key_rows, value_rows, probs,
                                               ffn_gain, gain_attn, mixing, correction, before, weights)

time: 187 us -> 185 us (0.989)
  waiting for transfers between devices: 96.3 us -> 86.2 us
  starting transfers between devices: 25.1 us -> 30.1 us
  Pallas kernels: 60.2 us -> 63.3 us
    ppermute x30 -> x31, waiting for transfers between devices: 80.7 us -> 70.5 us  [exchange(): lax.ppermute(value, 'dp', [(source, source ^ flips) for source in range(c...]
    ppermute x30 -> x31, starting transfers between devices: 20.5 us -> 25.6 us  [exchange(): lax.ppermute(value, 'dp', [(source, source ^ flips) for source in range(c...]
    pallas_call x1, Pallas kernels: 4.1 us -> 7.11 us  [attn_product(): pl.pallas_call(lambda *refs: attn_product_kernel(halves, block, refs), ou...]
  transfers between devices with their start and end apart: 32 -> 33, of which waited for: 14 -> 16; matrix products, arithmetic and copies ran while one was open for 1% -> 1% of each run, Pallas kernels for 17% -> 17%
where the time goes in v1:
time: 185 us
  waiting for transfers between devices  86.2 us (47%)
  Pallas kernels  63.3 us (34%)
  starting transfers between devices  30.1 us (16%)
  other arithmetic  2.36 us (1%)
  local copies, waits for them, and re-layouts  1.99 us (1%)
    ppermute x31, waiting for transfers between devices, exchange(): lax.ppermute(value, 'dp', [(source, source ^ flips) for source in range(c...  70.5 us
    ppermute x31, starting transfers between devices, exchange(): lax.ppermute(value, 'dp', [(source, source ^ flips) for source in range(c...  25.6 us
    ppermute x2, waiting for transfers between devices, local(): message = lax.ppermute(message, 'section', [(0, 1), (1, 0)])  15.7 us
    pallas_call x1, Pallas kernels, forward_lite(): pl.pallas_call(forward_lite_kernel, out_shape=[jax.ShapeDtypeStruct((toke...  11.9 us
    pallas_call x1, Pallas kernels, relay_backward(): pl.pallas_call(relay_kernel, out_shape=shape((tokens + EXTRA, width), bfl...  11 us
    pallas_call x1, Pallas kernels, forward(): pl.pallas_call(lambda *refs: forward_kernel(fast, *refs), out_shape=[shap...  9.02 us
    pallas_call x1, Pallas kernels, attn_backward(): pl.pallas_call(attn_kernel, out_shape=[shape((1, tokens, 2 * width), bflo...  7.92 us
    pallas_call x1, Pallas kernels, attn_product(): pl.pallas_call(lambda *refs: attn_product_kernel(halves, block, refs), ou...  7.11 us
  transfers between devices with their start and end apart: 33, of which 16 were waited for; matrix products, arithmetic and copies ran while one was open for 1% of the time, Pallas kernels for 17%

profile of v1, /device:TPU:0, one launch (start us, length us, event | category | flops | bytes accessed | tf_op | source)
XLA Modules:
  0.0 185.0 jit_solution(13661208070015969639)
XLA Ops:
  0.7 11.9 %forward_lite.1 = (bf16[208,768]{1,0:T(8,128)(2,1)S(1)}, bf16[1,768,768]{2,1,0:T(8,128)(2,1)S(1)}, bf16[1,768,768]{2,1,0:T(8,128)(2,1)S(1)}, bf16[1,768,768]{2,1...) custom-call(bf16[192,1536]{1,0:T(8,128)(2,1)} %refs_0_.1, ...), custom_call_target="tpu_custom_call" | custom-call | flops 3623878 | bytes 18874 | tf_op jit(solution)/shard_map/forward_lite/pallas_call | solution.py:219
  12.6 3.0 %collective-permute-start = (bf16[208,768]{1,0:T(8,128)(2,1)S(1)}, bf16[208,768]{1,0:T(8,128)(2,1)S(1)}, u32[]{:S(2)}, u32[]{:S(2)}) collective-permute-start(bf16[208,768]{1,0:T(8,128)(2,1)S(1)} %get-tuple-element.92), channel_id=1, source_target_pairs={{0,16},{16,0},{1,17},{17,1},{2,18},{18,2},{3,19},{19,3},{4,20},{20... | collective-permute-start | bytes 958472 | tf_op jit(solution)/shard_map/ppermute | solution.py:854
  15.6 7.5 %collective-permute-done.refs_1_ = bf16[208,768]{1,0:T(8,128)(2,1)S(1)} collective-permute-done((bf16[208,768]{1,0:T(8,128)(2,1)S(1)}, bf16[208,768]{1,0:T(8,128)(2,1)S(1)}, u32[]{:S(2)}, u32[]{:S(2)}) %collective-permute-start) | collective-permute-done | bytes 319520 | tf_op jit(solution)/shard_map/ppermute | solution.py:854
  23.2 9.0 %forward_full.1 = (bf16[192,1536]{1,0:T(8,128)(2,1)S(1)}, bf16[1,192,1536]{2,1,0:T(8,128)(2,1)}, bf16[192,768]{1,0:T(8,128)(2,1)S(1)}, bf16[192,768]{1,0:T(8,128...) custom-call(bf16[192,1536]{1,0:T(8,128)(2,1)S(1)} %copy-done.1, ...), custom_call_target="tpu_custom_call" | custom-call | flops 3623878 | bytes 18874 | tf_op jit(solution)/shard_map/forward_full/pallas_call | solution.py:331
  32.2 1.8 collective-permute-start.3
  34.0 11.0 %backward_relay.1 = bf16[208,768]{1,0:T(8,128)(2,1)S(1)} custom-call(bf16[192,1536]{1,0:T(8,128)(2,1)S(1)} %copy-done.2, s32[2]{0:T(128)S(1)} %copy-done.8, f32[1,2]{1,0:T(1,128)S(1)} %copy-done.5, f32[1,2,2]{2,1,0:T(2,128)S(1)} %copy-done.6, f32[1,768]{1,0:T(1,128)S(1)} %copy-done.3, f32[1,768]{1,0:T(1,128)S(1)} %copy-done.4, ...), custom_call_target="tpu_custom_call" | custom-call | flops 3623878 | bytes 18874 | tf_op jit(solution)/shard_map/backward_relay/pallas_call | solution.py:553
  45.0 1.6 collective-permute-start.1
  46.6 8.1 %collective-permute-done.1.refs_0_ = bf16[208,768]{1,0:T(8,128)(2,1)S(1)} collective-permute-done((bf16[208,768]{1,0:T(8,128)(2,1)S(1)}, bf16[208,768]{1,0:T(8,128)(2,1)S(1)}, u32[]{:S(2)}, u32[]{:S(2)}) %collective-permute-start.1) | collective-permute-done | bytes 319520 | tf_op jit(solution)/shard_map/ppermute | solution.py:863
  54.7 1.5 backward_start.1
  57.1 5.3 %backward_ffn.1 = (bf16[192,768]{1,0:T(8,128)(2,1)S(1)}, bf16[192,768]{1,0:T(8,128)(2,1)S(1)}, bf16[192,768]{1,0:T(8,128)(2,1)S(1)}, bf16[192,768]{1,0:T(8,128)(...) custom-call(bf16[192,1536]{1,0:T(8,128)(2,1)S(1)} %get-tuple-element, ...), custom_call_target="tpu_custom_call" | custom-call | flops 2717908 | bytes 14155 | tf_op jit(solution)/shard_map/backward_ffn/pallas_call | solution.py:429
  62.4 2.1 %collective-permute-done.6.refs_6_ = bf16[192,768]{1,0:T(8,128)(2,1)S(1)} collective-permute-done((bf16[192,768]{1,0:T(8,128)(2,1)S(1)}, bf16[192,768]{1,0:T(8,128)(2,1)S(1)}, u32[]{:S(2)}, u32[]{:S(2)}) %collective-permute-start.6) | collective-permute-done | bytes 294944 | tf_op jit(solution)/shard_map/ppermute | solution.py:722
  64.6 1.6 collective-permute-done.7.refs_7_
  66.2 2.4 %product_down.1 = (bf16[2,192,768]{2,1,0:T(8,128)(2,1)S(1)}, f32[2,192,768]{2,1,0:T(8,128)S(1)}) custom-call(bf16[192,1152]{1,0:T(8,128)(2,1)S(1)} %get-tuple-element.119.refs_0_, bf16[192,1920]{1,0:T(8,128)(2,1)S(1)} %collective-permute-done.2.refs_0_.refs_1_, bf16[192,1920]{1,0:T(8,128)(2,1)S(1)} %collective-permute-done.3.refs_1_.refs_2_, ...), custom_call_target="tpu_custom_call" | custom-call | flops 905969 | bytes 2359 | tf_op jit(solution)/shard_map/product_down/pallas_call | solution.py:613
  68.6 1.6 collective-permute-start.13
  70.8 0.9 collective-permute-start.11
  72.3 7.9 %backward_attn.1 = (bf16[1,192,1536]{2,1,0:T(8,128)(2,1)}, bf16[208,3072]{1,0:T(8,128)(2,1)S(1)}, f32[8,768]{1,0:T(8,128)}) custom-call(bf16[192,768]{1,0:T(8,128)(2,1)S(1)} %get-tuple-element.114.datt_ref, bf16[192,768]{1,0:T(8,128)(2,1)S(1)} %get-tuple-element.104.q_ref, bf16[192,768]{1,0:T(8,128)(2,1)S(1)} %get-tuple-element.105.k_ref, ...), custom_call_target="tpu_custom_call" | custom-call | flops 1132462 | bytes 4718 | tf_op jit(solution)/shard_map/backward_attn/pallas_call | solution.py:509
  80.2 3.8 %collective-permute-done.13 = bf16[2,192,768]{2,1,0:T(8,128)(2,1)S(1)} collective-permute-done((bf16[2,192,768]{2,1,0:T(8,128)(2,1)S(1)}, bf16[2,192,768]{2,1,0:T(8,128)(2,1)S(1)}, u32[]{:S(2)}, u32[]{:S(2)}) %collective-permute-start.13) | collective-permute-done | bytes 589856 | tf_op jit(solution)/shard_map/ppermute | solution.py:722
  84.1 1.0 collective-permute-start.15
  85.1 0.9 collective-permute-start.16
  86.1 2.2 %product_gate.1 = (bf16[192,768]{1,0:T(8,128)(2,1)S(1)}, bf16[192,768]{1,0:T(8,128)(2,1)S(1)}, f32[2,192,768]{2,1,0:T(8,128)S(1)}) custom-call(bf16[192,768]{1,0:T(8,128)(2,1)S(1)} %get-tuple-element.131.refs_0_, bf16[192,768]{1,0:T(8,128)(2,1)S(1)} %slice.100.refs_1_, bf16[192,768]{1,0:T(8,128)(2,1)S(1)} %slice.101.refs_2_, ...), custom_call_target="tpu_custom_call" | custom-call | flops 905969 | bytes 2359 | tf_op jit(solution)/shard_map/product_gate/pallas_call | solution.py:613
  88.2 1.7 collective-permute-start.19
  90.3 2.6 %collective-permute-start.21 = (bf16[192,768]{1,0:T(8,128)(2,1)S(1)}, bf16[192,768]{1,0:T(8,128)(2,1)S(1)}, u32[]{:S(2)}, u32[]{:S(2)}) collective-permute-start(bf16[192,768]{1,0:T(8,128)(2,1)S(1)} %fusion.4.refs_9_), channel_id=1, source_target_pairs={{0,8},{1,9},{2,10},{3,11},{4,12},{5,13},{6,14},{7,15},{8,0},{9,1},... | collective-permute-start | bytes 884744 | tf_op jit(solution)/shard_map/ppermute | solution.py:722
  92.9 1.1 collective-permute-done.15.refs_6_
  94.0 5.5 %collective-permute-done.16.refs_7_ = bf16[192,768]{1,0:T(8,128)(2,1)S(1)} collective-permute-done((bf16[192,768]{1,0:T(8,128)(2,1)S(1)}, bf16[192,768]{1,0:T(8,128)(2,1)S(1)}, u32[]{:S(2)}, u32[]{:S(2)}) %collective-permute-start.16) | collective-permute-done | bytes 294944 | tf_op jit(solution)/shard_map/ppermute | solution.py:722
  99.5 0.9 collective-permute-start.18
  100.5 4.0 %collective-permute-done.19 = bf16[192,768]{1,0:T(8,128)(2,1)S(1)} collective-permute-done((bf16[192,768]{1,0:T(8,128)(2,1)S(1)}, bf16[192,768]{1,0:T(8,128)(2,1)S(1)}, u32[]{:S(2)}, u32[]{:S(2)}) %collective-permute-start.19) | collective-permute-done | bytes 294944 | tf_op jit(solution)/shard_map/ppermute | solution.py:722
  104.5 5.7 %collective-permute-done.20 = bf16[192,768]{1,0:T(8,128)(2,1)S(1)} collective-permute-done((bf16[192,768]{1,0:T(8,128)(2,1)S(1)}, bf16[192,768]{1,0:T(8,128)(2,1)S(1)}, u32[]{:S(2)}, u32[]{:S(2)}) %collective-permute-start.20) | collective-permute-done | bytes 294944 | tf_op jit(solution)/shard_map/ppermute | solution.py:722
  110.3 2.2 %product_up.1 = (bf16[2,192,768]{2,1,0:T(8,128)(2,1)S(1)}, f32[2,192,768]{2,1,0:T(8,128)S(1)}) custom-call(bf16[192,768]{1,0:T(8,128)(2,1)S(1)} %get-tuple-element.131.refs_0_, bf16[192,768]{1,0:T(8,128)(2,1)S(1)} %slice.100.refs_1_, bf16[192,768]{1,0:T(8,128)(2,1)S(1)} %slice.101.refs_2_, bf16[192,768]{1,0:T(8,128)(2,1)S(1)} %collective-permute-done.9.refs_3_, ...), custom_call_target="tpu_custom_call" | custom-call | flops 905969 | bytes 2359 | tf_op jit(solution)/shard_map/product_up/pallas_call | solution.py:613
  112.5 2.7 %collective-permute-start.22 = (bf16[2,192,768]{2,1,0:T(8,128)(2,1)S(1)}, bf16[2,192,768]{2,1,0:T(8,128)(2,1)S(1)}, u32[]{:S(2)}, u32[]{:S(2)}) collective-permute-start(bf16[2,192,768]{2,1,0:T(8,128)(2,1)S(1)} %get-tuple-element.148), channel_id=1, source_target_pairs={{0,4},{1,5},{2,6},{3,7},{4,0},{5,1},{6,2},{7,3},{8,12},{9,13},{10,... | collective-permute-start | bytes 1769480 | tf_op jit(solution)/shard_map/ppermute | solution.py:722
  115.2 1.6 collective-permute-start.23
  116.8 16.9 %collective-permute-done.23 = bf16[192,768]{1,0:T(8,128)(2,1)S(1)} collective-permute-done((bf16[192,768]{1,0:T(8,128)(2,1)S(1)}, bf16[192,768]{1,0:T(8,128)(2,1)S(1)}, u32[]{:S(2)}, u32[]{:S(2)}) %collective-permute-start.23) | collective-permute-done | bytes 294944 | tf_op jit(solution)/shard_map/ppermute | solution.py:722
  133.8 0.6 collective-permute-done.22
  134.6 3.0 %collective-permute-done.24.refs_7_ = bf16[208,3072]{1,0:T(8,128)(2,1)S(1)} collective-permute-done((bf16[208,3072]{1,0:T(8,128)(2,1)S(1)}, bf16[208,3072]{1,0:T(8,128)(2,1)S(1)}, u32[]{:S(2)}, u32[]{:S(2)}) %collective-permute-start.24) | collective-permute-done | bytes 1277984 | tf_op jit(solution)/shard_map/ppermute | solution.py:722
  137.6 7.1 %product_attn.1 = (bf16[112,1536]{1,0:T(8,128)(2,1)}, f32[2,48,1536]{2,1,0:T(8,128)S(1)}, f32[8,768]{1,0:T(8,128)S(1)}, bf16[2,48,1536]{2,1,0:T(8,128)(2,1)}, f32[2,48,1536]{2,1,0:T(8,128)S(1)}) custom-call(bf16[192,1152]{1,0:T(8,128)(2,1)S(1)} %get-tuple-element.119.refs_0_, bf16[192,1920]{1,0:T(8,128)(2,1)S(1)} %collective-permute-done.2.refs_0_.refs_1_, ...), custom_call_target="tpu_custom_call" | custom-call | flops 1 | bytes 1 | tf_op jit(solution)/shard_map/product_attn/pallas_call | solution.py:641
  144.7 1.8 collective-permute-start.25
  146.5 1.6 collective-permute-start.29
  148.1 1.4 collective-permute-start.27
  149.5 12.8 %collective-permute-done.25.came_ref = bf16[112,1536]{1,0:T(8,128)(2,1)} collective-permute-done((bf16[112,1536]{1,0:T(8,128)(2,1)}, bf16[112,1536]{1,0:T(8,128)(2,1)}, u32[]{:S(2)}, u32[]{:S(2)}) %collective-permute-start.25) | collective-permute-done | bytes 344096 | tf_op jit(solution)/shard_map/ppermute | solution.py:722
  162.2 1.0 first_sum.1
  163.3 1.0 collective-permute-start.26
  164.2 1.1 fusion
  165.5 1.0 collective-permute-start.31
  166.5 1.0 collective-permute-start.30
  167.5 4.4 %collective-permute-done.27 = bf16[2,48,1536]{2,1,0:T(8,128)(2,1)S(1)} collective-permute-done((bf16[2,48,1536]{2,1,0:T(8,128)(2,1)}, bf16[2,48,1536]{2,1,0:T(8,128)(2,1)S(1)}, u32[]{:S(2)}, u32[]{:S(2)}) %collective-permute-start.27) | collective-permute-done | bytes 294944 | tf_op jit(solution)/shard_map/ppermute | solution.py:722
  172.1 8.4 %collective-permute-done.28 = bf16[48,1536]{1,0:T(8,128)(2,1)S(1)} collective-permute-done((bf16[48,1536]{1,0:T(8,128)(2,1)S(1)}, bf16[48,1536]{1,0:T(8,128)(2,1)S(1)}, u32[]{:S(2)}, u32[]{:S(2)}) %collective-permute-start.28) | collective-permute-done | bytes 147488 | tf_op jit(solution)/shard_map/ppermute | solution.py:722
  180.4 0.7 fusion.7
  181.2 0.7 first_end.1
  183.9 1.1 assemble.1
  (72 shorter events, 5.2 us)
Async XLA Ops:
  0.6 22.5 %copy-start.1 = (bf16[192,1536]{1,0:T(8,128)(2,1)S(1)}, bf16[192,1536]{1,0:T(8,128)(2,1)}, u32[]{:S(2)}) copy-start(bf16[192,1536]{1,0:T(8,128)(2,1)} %refs_0_.1) | copy-start | bytes 1769476
  0.7 22.5 %copy-start.7 = (s32[2,96]{1,0:T(2,128)S(1)}, s32[2,96]{1,0:T(2,128)}, u32[]{:S(2)}) copy-start(s32[2,96]{1,0:T(2,128)} %refs_2_.2) | copy-start | bytes 2308
  0.7 22.4 %copy-start.6 = (f32[1,2,2]{2,1,0:T(2,128)S(1)}, f32[1,2,2]{2,1,0:T(2,128)}, u32[]{:S(2)}) copy-start(f32[1,2,2]{2,1,0:T(2,128)} %mix_ref.3) | copy-start | bytes 52
  0.7 22.4 %copy-start.5 = (f32[1,2]{1,0:T(1,128)S(1)}, f32[1,2]{1,0:T(1,128)}, u32[]{:S(2)}) copy-start(f32[1,2]{1,0:T(1,128)} %cor_ref.5) | copy-start | bytes 28
  0.7 22.4 %copy-start.4 = (f32[1,768]{1,0:T(1,128)S(1)}, f32[1,768]{1,0:T(1,128)}, u32[]{:S(2)}) copy-start(f32[1,768]{1,0:T(1,128)} %ga_ref.3) | copy-start | bytes 9220
  0.7 22.4 %copy-start.3 = (f32[1,768]{1,0:T(1,128)S(1)}, f32[1,768]{1,0:T(1,128)}, u32[]{:S(2)}) copy-start(f32[1,768]{1,0:T(1,128)} %gf_ref.3) | copy-start | bytes 9220
  12.6 10.5 %collective-permute-start = (bf16[208,768]{1,0:T(8,128)(2,1)S(1)}, bf16[208,768]{1,0:T(8,128)(2,1)S(1)}, u32[]{:S(2)}, u32[]{:S(2)}) collective-permute-start(bf16[208,768]{1,0:T(8,128)(2,1)S(1)} %get-tuple-element.92), channel_id=1, source_target_pairs={{0,16},{16,0},{1,17},{17,1},{2,18},{18,2},{3,19},{19,3},{4,20},{20... | collective-permute-start | bytes 958472 | tf_op jit(solution)/shard_map/ppermute | solution.py:854
  23.2 10.8 %copy-start.2 = (bf16[192,1536]{1,0:T(8,128)(2,1)S(1)}, bf16[192,1536]{1,0:T(8,128)(2,1)}, u32[]{:S(2)}) copy-start(bf16[192,1536]{1,0:T(8,128)(2,1)} %refs_1_.1) | copy-start | bytes 1769476
  23.2 10.8 %copy-start.8 = (s32[2]{0:T(128)S(1)}, s32[2]{0:T(128)}, u32[]{:S(2)}) copy-start(s32[2]{0:T(128)} %refs_2_.3) | copy-start | bytes 28
  32.2 24.9 %collective-permute-start.2 = (bf16[192,1920]{1,0:T(8,128)(2,1)S(1)}, bf16[192,1920]{1,0:T(8,128)(2,1)S(1)}, u32[]{:S(2)}, u32[]{:S(2)}) collective-permute-start(bf16[192,1920]{1,0:T(8,128)(2,1)S(1)} %get-tuple-element.111), channel_id=1, source_target_pairs={{0,1},{1,0},{2,3},{3,2},{4,5},{5,4},{6,7},{7,6},{8,9},{9,8},{10,11... | collective-permute-start | bytes 2211848 | tf_op jit(solution)/shard_map/ppermute | solution.py:722
  32.2 24.9 %collective-permute-start.3 = (bf16[192,1920]{1,0:T(8,128)(2,1)S(1)}, bf16[192,1920]{1,0:T(8,128)(2,1)S(1)}, u32[]{:S(2)}, u32[]{:S(2)}) collective-permute-start(bf16[192,1920]{1,0:T(8,128)(2,1)S(1)} %get-tuple-element.112), channel_id=1, source_target_pairs={{0,2},{1,3},{2,0},{3,1},{4,6},{5,7},{6,4},{7,5},{8,10},{9,11},{10,... | collective-permute-start | bytes 2211848 | tf_op jit(solution)/shard_map/ppermute | solution.py:722
  45.0 9.7 %collective-permute-start.1 = (bf16[208,768]{1,0:T(8,128)(2,1)S(1)}, bf16[208,768]{1,0:T(8,128)(2,1)S(1)}, u32[]{:S(2)}, u32[]{:S(2)}) collective-permute-start(bf16[208,768]{1,0:T(8,128)(2,1)S(1)} %backward_relay.1), channel_id=1, source_target_pairs={{0,16},{16,0},{1,17},{17,1},{2,18},{18,2},{3,19},{19,3},{4,20},{20... | collective-permute-start | bytes 958472 | tf_op jit(solution)/shard_map/ppermute | solution.py:863
  46.5 10.6 %collective-permute-start.4 = (bf16[192,768]{1,0:T(8,128)(2,1)S(1)}, bf16[192,768]{1,0:T(8,128)(2,1)S(1)}, u32[]{:S(2)}, u32[]{:S(2)}) collective-permute-start(bf16[192,768]{1,0:T(8,128)(2,1)S(1)} %get-tuple-element.113), channel_id=1, source_target_pairs={{0,3},{1,2},{2,1},{3,0},{4,7},{5,6},{6,5},{7,4},{8,11},{9,10},{10,... | collective-permute-start | bytes 884744 | tf_op jit(solution)/shard_map/ppermute | solution.py:722
  56.2 8.4 %collective-permute-start.6 = (bf16[192,768]{1,0:T(8,128)(2,1)S(1)}, bf16[192,768]{1,0:T(8,128)(2,1)S(1)}, u32[]{:S(2)}, u32[]{:S(2)}) collective-permute-start(bf16[192,768]{1,0:T(8,128)(2,1)S(1)} %get-tuple-element.110.low_ref.refs_4_), channel_id=1, source_target_pairs={{0,2},{1,3},{2,0},{3,1},{4,6},{5,7},{6,4},{7,5},{8,10},{9,11},{10,... | collective-permute-start | bytes 884744 | tf_op jit(solution)/shard_map/ppermute | solution.py:722
  56.5 8.0 %collective-permute-start.5 = (bf16[192,768]{1,0:T(8,128)(2,1)S(1)}, bf16[192,768]{1,0:T(8,128)(2,1)S(1)}, u32[]{:S(2)}, u32[]{:S(2)}) collective-permute-start(bf16[192,768]{1,0:T(8,128)(2,1)S(1)} %get-tuple-element.110.low_ref.refs_4_), channel_id=1, source_target_pairs={{0,1},{1,0},{2,3},{3,2},{4,5},{5,4},{6,7},{7,6},{8,9},{9,8},{10,11... | collective-permute-start | bytes 884744 | tf_op jit(solution)/shard_map/ppermute | solution.py:722
  64.6 1.6 collective-permute-start.7
  68.6 15.4 %collective-permute-start.13 = (bf16[2,192,768]{2,1,0:T(8,128)(2,1)S(1)}, bf16[2,192,768]{2,1,0:T(8,128)(2,1)S(1)}, u32[]{:S(2)}, u32[]{:S(2)}) collective-permute-start(bf16[2,192,768]{2,1,0:T(8,128)(2,1)S(1)} %get-tuple-element.122.before), channel_id=1, source_target_pairs={{0,4},{1,5},{2,6},{3,7},{4,0},{5,1},{6,2},{7,3},{8,12},{9,13},{10,... | collective-permute-start | bytes 1769480 | tf_op jit(solution)/shard_map/ppermute | solution.py:722
  70.3 13.9 %collective-permute-start.9 = (bf16[192,768]{1,0:T(8,128)(2,1)S(1)}, bf16[192,768]{1,0:T(8,128)(2,1)S(1)}, u32[]{:S(2)}, u32[]{:S(2)}) collective-permute-start(bf16[192,768]{1,0:T(8,128)(2,1)S(1)} %slice.101.refs_2_), channel_id=1, source_target_pairs={{0,1},{1,0},{2,3},{3,2},{4,5},{5,4},{6,7},{7,6},{8,9},{9,8},{10,11... | collective-permute-start | bytes 884744 | tf_op jit(solution)/shard_map/ppermute | solution.py:722
  70.4 14.8 %collective-permute-start.10 = (bf16[192,768]{1,0:T(8,128)(2,1)S(1)}, bf16[192,768]{1,0:T(8,128)(2,1)S(1)}, u32[]{:S(2)}, u32[]{:S(2)}) collective-permute-start(bf16[192,768]{1,0:T(8,128)(2,1)S(1)} %get-tuple-element.133), channel_id=1, source_target_pairs={{0,1},{1,0},{2,3},{3,2},{4,5},{5,4},{6,7},{7,6},{8,9},{9,8},{10,11... | collective-permute-start | bytes 884744 | tf_op jit(solution)/shard_map/ppermute | solution.py:722
  70.8 15.2 %collective-permute-start.11 = (bf16[192,768]{1,0:T(8,128)(2,1)S(1)}, bf16[192,768]{1,0:T(8,128)(2,1)S(1)}, u32[]{:S(2)}, u32[]{:S(2)}) collective-permute-start(bf16[192,768]{1,0:T(8,128)(2,1)S(1)} %get-tuple-element.134), channel_id=1, source_target_pairs={{0,2},{1,3},{2,0},{3,1},{4,6},{5,7},{6,4},{7,5},{8,10},{9,11},{10,... | collective-permute-start | bytes 884744 | tf_op jit(solution)/shard_map/ppermute | solution.py:722
  71.8 14.3 %collective-permute-start.12 = (bf16[192,768]{1,0:T(8,128)(2,1)S(1)}, bf16[192,768]{1,0:T(8,128)(2,1)S(1)}, u32[]{:S(2)}, u32[]{:S(2)}) collective-permute-start(bf16[192,768]{1,0:T(8,128)(2,1)S(1)} %get-tuple-element.135), channel_id=1, source_target_pairs={{0,3},{1,2},{2,1},{3,0},{4,7},{5,6},{6,5},{7,4},{8,11},{9,10},{10,... | collective-permute-start | bytes 884744 | tf_op jit(solution)/shard_map/ppermute | solution.py:722
  84.0 6.3 %collective-permute-start.14 = (bf16[192,768]{1,0:T(8,128)(2,1)S(1)}, bf16[192,768]{1,0:T(8,128)(2,1)S(1)}, u32[]{:S(2)}, u32[]{:S(2)}) collective-permute-start(bf16[192,768]{1,0:T(8,128)(2,1)S(1)} %get-tuple-element.139), channel_id=1, source_target_pairs={{0,1},{1,0},{2,3},{3,2},{4,5},{5,4},{6,7},{7,6},{8,9},{9,8},{10,11... | collective-permute-start | bytes 884744 | tf_op jit(solution)/shard_map/ppermute | solution.py:722
  84.1 9.9 %collective-permute-start.15 = (bf16[192,768]{1,0:T(8,128)(2,1)S(1)}, bf16[192,768]{1,0:T(8,128)(2,1)S(1)}, u32[]{:S(2)}, u32[]{:S(2)}) collective-permute-start(bf16[192,768]{1,0:T(8,128)(2,1)S(1)} %get-tuple-element.140), channel_id=1, source_target_pairs={{0,2},{1,3},{2,0},{3,1},{4,6},{5,7},{6,4},{7,5},{8,10},{9,11},{10,... | collective-permute-start | bytes 884744 | tf_op jit(solution)/shard_map/ppermute | solution.py:722
  85.1 14.4 %collective-permute-start.16 = (bf16[192,768]{1,0:T(8,128)(2,1)S(1)}, bf16[192,768]{1,0:T(8,128)(2,1)S(1)}, u32[]{:S(2)}, u32[]{:S(2)}) collective-permute-start(bf16[192,768]{1,0:T(8,128)(2,1)S(1)} %get-tuple-element.141), channel_id=1, source_target_pairs={{0,3},{1,2},{2,1},{3,0},{4,7},{5,6},{6,5},{7,4},{8,11},{9,10},{10,... | collective-permute-start | bytes 884744 | tf_op jit(solution)/shard_map/ppermute | solution.py:722
  88.2 16.2 %collective-permute-start.19 = (bf16[192,768]{1,0:T(8,128)(2,1)S(1)}, bf16[192,768]{1,0:T(8,128)(2,1)S(1)}, u32[]{:S(2)}, u32[]{:S(2)}) collective-permute-start(bf16[192,768]{1,0:T(8,128)(2,1)S(1)} %get-tuple-element.138), channel_id=1, source_target_pairs={{0,4},{1,5},{2,6},{3,7},{4,0},{5,1},{6,2},{7,3},{8,12},{9,13},{10,... | collective-permute-start | bytes 884744 | tf_op jit(solution)/shard_map/ppermute | solution.py:722
  89.9 20.2 %collective-permute-start.20 = (bf16[192,768]{1,0:T(8,128)(2,1)S(1)}, bf16[192,768]{1,0:T(8,128)(2,1)S(1)}, u32[]{:S(2)}, u32[]{:S(2)}) collective-permute-start(bf16[192,768]{1,0:T(8,128)(2,1)S(1)} %get-tuple-element.145), channel_id=1, source_target_pairs={{0,4},{1,5},{2,6},{3,7},{4,0},{5,1},{6,2},{7,3},{8,12},{9,13},{10,... | collective-permute-start | bytes 884744 | tf_op jit(solution)/shard_map/ppermute | solution.py:722
  90.3 19.8 %collective-permute-start.21 = (bf16[192,768]{1,0:T(8,128)(2,1)S(1)}, bf16[192,768]{1,0:T(8,128)(2,1)S(1)}, u32[]{:S(2)}, u32[]{:S(2)}) collective-permute-start(bf16[192,768]{1,0:T(8,128)(2,1)S(1)} %fusion.4.refs_9_), channel_id=1, source_target_pairs={{0,8},{1,9},{2,10},{3,11},{4,12},{5,13},{6,14},{7,15},{8,0},{9,1},... | collective-permute-start | bytes 884744 | tf_op jit(solution)/shard_map/ppermute | solution.py:722
  94.0 16.3 %collective-permute-start.8 = (bf16[192,384]{1,0:T(8,128)(2,1)S(1)}, bf16[192,384]{1,0:T(8,128)(2,1)S(1)}, u32[]{:S(2)}, u32[]{:S(2)}) collective-permute-start(bf16[192,384]{1,0:T(8,128)(2,1)S(1)} %get-tuple-element.130), channel_id=1, source_target_pairs={{0,3},{1,2},{2,1},{3,0},{4,7},{5,6},{6,5},{7,4},{8,11},{9,10},{10,... | collective-permute-start | bytes 442376 | tf_op jit(solution)/shard_map/ppermute | solution.py:722
  99.5 35.0 %collective-permute-start.18 = (bf16[208,3072]{1,0:T(8,128)(2,1)S(1)}, bf16[208,3072]{1,0:T(8,128)(2,1)S(1)}, u32[]{:S(2)}, u32[]{:S(2)}) collective-permute-start(bf16[208,3072]{1,0:T(8,128)(2,1)S(1)} %get-tuple-element.142.refs_8_.refs_4_), channel_id=1, source_target_pairs={{0,2},{1,3},{2,0},{3,1},{4,6},{5,7},{6,4},{7,5},{8,10},{9,11},{10,... | collective-permute-start | bytes 3833864 | tf_op jit(solution)/shard_map/ppermute | solution.py:722
  110.2 2.3 %copy-start = (f32[192,768]{1,0:T(8,128)}, f32[192,768]{1,0:T(8,128)S(1)}, u32[]{:S(2)}) copy-start(f32[192,768]{1,0:T(8,128)S(1)} %bitcast_add_fusion.2.refs_9_) | copy-start | bytes 1769476
  112.5 21.9 %collective-permute-start.22 = (bf16[2,192,768]{2,1,0:T(8,128)(2,1)S(1)}, bf16[2,192,768]{2,1,0:T(8,128)(2,1)S(1)}, u32[]{:S(2)}, u32[]{:S(2)}) collective-permute-start(bf16[2,192,768]{2,1,0:T(8,128)(2,1)S(1)} %get-tuple-element.148), channel_id=1, source_target_pairs={{0,4},{1,5},{2,6},{3,7},{4,0},{5,1},{6,2},{7,3},{8,12},{9,13},{10,... | collective-permute-start | bytes 1769480 | tf_op jit(solution)/shard_map/ppermute | solution.py:722
  115.2 18.5 %collective-permute-start.23 = (bf16[192,768]{1,0:T(8,128)(2,1)S(1)}, bf16[192,768]{1,0:T(8,128)(2,1)S(1)}, u32[]{:S(2)}, u32[]{:S(2)}) collective-permute-start(bf16[192,768]{1,0:T(8,128)(2,1)S(1)} %fusion.3.refs_8_), channel_id=1, source_target_pairs={{0,8},{1,9},{2,10},{3,11},{4,12},{5,13},{6,14},{7,15},{8,0},{9,1},... | collective-permute-start | bytes 884744 | tf_op jit(solution)/shard_map/ppermute | solution.py:722
  116.8 17.8 %collective-permute-start.17 = (bf16[208,3072]{1,0:T(8,128)(2,1)S(1)}, bf16[208,3072]{1,0:T(8,128)(2,1)S(1)}, u32[]{:S(2)}, u32[]{:S(2)}) collective-permute-start(bf16[208,3072]{1,0:T(8,128)(2,1)S(1)} %get-tuple-element.142.refs_8_.refs_4_), channel_id=1, source_target_pairs={{0,1},{1,0},{2,3},{3,2},{4,5},{5,4},{6,7},{7,6},{8,9},{9,8},{10,11... | collective-permute-start | bytes 3833864 | tf_op jit(solution)/shard_map/ppermute | solution.py:722
  134.4 10.2 %copy-start.9 = (bf16[2,192,768]{2,1,0:T(8,128)(2,1)}, bf16[2,192,768]{2,1,0:T(8,128)(2,1)S(1)}, u32[]{:S(2)}) copy-start(bf16[2,192,768]{2,1,0:T(8,128)(2,1)S(1)} %collective-permute-done.22) | copy-start | bytes 1769476
  134.5 3.1 %collective-permute-start.24 = (bf16[208,3072]{1,0:T(8,128)(2,1)S(1)}, bf16[208,3072]{1,0:T(8,128)(2,1)S(1)}, u32[]{:S(2)}, u32[]{:S(2)}) collective-permute-start(bf16[208,3072]{1,0:T(8,128)(2,1)S(1)} %collective-permute-done.18.refs_6_), channel_id=1, source_target_pairs={{0,1},{1,0},{2,3},{3,2},{4,5},{5,4},{6,7},{7,6},{8,9},{9,8},{10,11... | collective-permute-start | bytes 3833864 | tf_op jit(solution)/shard_map/ppermute | solution.py:722
  144.7 17.5 %collective-permute-start.25 = (bf16[112,1536]{1,0:T(8,128)(2,1)}, bf16[112,1536]{1,0:T(8,128)(2,1)}, u32[]{:S(2)}, u32[]{:S(2)}) collective-permute-start(bf16[112,1536]{1,0:T(8,128)(2,1)} %get-tuple-element.152), channel_id=1, source_target_pairs={{0,4},{1,5},{2,6},{3,7},{4,0},{5,1},{6,2},{7,3},{8,12},{9,13},{10,... | collective-permute-start | bytes 1032200 | tf_op jit(solution)/shard_map/ppermute | solution.py:722
  146.5 17.8 %collective-permute-start.29 = (bf16[192,768]{1,0:T(8,128)(2,1)S(1)}, bf16[192,768]{1,0:T(8,128)(2,1)S(1)}, u32[]{:S(2)}, u32[]{:S(2)}) collective-permute-start(bf16[192,768]{1,0:T(8,128)(2,1)S(1)} %fusion.5.refs_8_), channel_id=1, source_target_pairs={{0,8},{1,9},{2,10},{3,11},{4,12},{5,13},{6,14},{7,15},{8,0},{9,1},... | collective-permute-start | bytes 884744 | tf_op jit(solution)/shard_map/ppermute | solution.py:722
  148.1 23.8 %collective-permute-start.27 = (bf16[2,48,1536]{2,1,0:T(8,128)(2,1)}, bf16[2,48,1536]{2,1,0:T(8,128)(2,1)S(1)}, u32[]{:S(2)}, u32[]{:S(2)}) collective-permute-start(bf16[2,48,1536]{2,1,0:T(8,128)(2,1)} %get-tuple-element.160), channel_id=1, source_target_pairs={{0,4},{1,5},{2,6},{3,7},{4,0},{5,1},{6,2},{7,3},{8,12},{9,13},{10,... | collective-permute-start | bytes 884744 | tf_op jit(solution)/shard_map/ppermute | solution.py:722
  163.3 17.9 %collective-permute-start.26 = (bf16[64,1536]{1,0:T(8,128)(2,1)S(1)}, bf16[64,1536]{1,0:T(8,128)(2,1)S(1)}, u32[]{:S(2)}, u32[]{:S(2)}) collective-permute-start(bf16[64,1536]{1,0:T(8,128)(2,1)S(1)} %get-tuple-element.155), channel_id=1, source_target_pairs={{0,8},{1,9},{2,10},{3,11},{4,12},{5,13},{6,14},{7,15},{8,0},{9,1},... | collective-permute-start | bytes 589832 | tf_op jit(solution)/shard_map/ppermute | solution.py:722
  165.4 16.6 %collective-permute-start.32 = (bf16[48,1536]{1,0:T(8,128)(2,1)S(1)}, bf16[48,1536]{1,0:T(8,128)(2,1)S(1)}, u32[]{:S(2)}, u32[]{:S(2)}) collective-permute-start(bf16[48,1536]{1,0:T(8,128)(2,1)S(1)} %pad_maximum_fusion.3), channel_id=1, source_target_pairs={{0,3},{1,2},{2,1},{3,0},{4,7},{5,6},{6,5},{7,4},{8,11},{9,10},{10,... | collective-permute-start | bytes 442376 | tf_op jit(solution)/shard_map/ppermute | solution.py:722
  165.5 16.5 %collective-permute-start.31 = (bf16[48,1536]{1,0:T(8,128)(2,1)S(1)}, bf16[48,1536]{1,0:T(8,128)(2,1)S(1)}, u32[]{:S(2)}, u32[]{:S(2)}) collective-permute-start(bf16[48,1536]{1,0:T(8,128)(2,1)S(1)} %pad_maximum_fusion.2), channel_id=1, source_target_pairs={{0,2},{1,3},{2,0},{3,1},{4,6},{5,7},{6,4},{7,5},{8,10},{9,11},{10,... | collective-permute-start | bytes 442376 | tf_op jit(solution)/shard_map/ppermute | solution.py:722
  166.5 15.5 %collective-permute-start.30 = (bf16[48,1536]{1,0:T(8,128)(2,1)S(1)}, bf16[48,1536]{1,0:T(8,128)(2,1)S(1)}, u32[]{:S(2)}, u32[]{:S(2)}) collective-permute-start(bf16[48,1536]{1,0:T(8,128)(2,1)S(1)} %pad_maximum_fusion.1), channel_id=1, source_target_pairs={{0,1},{1,0},{2,3},{3,2},{4,5},{5,4},{6,7},{7,6},{8,9},{9,8},{10,11... | collective-permute-start | bytes 442376 | tf_op jit(solution)/shard_map/ppermute | solution.py:722
  172.0 8.5 %collective-permute-start.28 = (bf16[48,1536]{1,0:T(8,128)(2,1)S(1)}, bf16[48,1536]{1,0:T(8,128)(2,1)S(1)}, u32[]{:S(2)}, u32[]{:S(2)}) collective-permute-start(bf16[48,1536]{1,0:T(8,128)(2,1)S(1)} %get-tuple-element.171), channel_id=1, source_target_pairs={{0,8},{1,9},{2,10},{3,11},{4,12},{5,13},{6,14},{7,15},{8,0},{9,1},... | collective-permute-start | bytes 442376 | tf_op jit(solution)/shard_map/ppermute | solution.py:722

commit v2 on v1

--- a/solution.py
+++ b/solution.py
@@ -15,7 +15,6 @@
 GELU_A = 0.7978845608028654
 GELU_B = 0.044715
 EXTRA = 16
-CHUNK = 256
 SCOPED = 12
 bfloat = jnp.bfloat16
 floating = jnp.float32
@@ -43,19 +42,6 @@
 
 def cost(flops, moved):
     return pl.CostEstimate(flops=flops // 1000, bytes_accessed=moved // 1000, transcendentals=0)
-
-
-def scalar_rows(values, rows, width):
-    lane = lax.broadcasted_iota(jnp.int32, (rows, width), 1)
-    row = lax.broadcasted_iota(jnp.int32, (rows, width), 0)
-    whole = jnp.zeros((rows, width), floating)
-    for place, value in enumerate(values):
-        whole = jnp.where(lane == place, value, whole)
-    high = whole.astype(bfloat).astype(floating)
-    middle = (whole - high).astype(bfloat).astype(floating)
-    low = whole - high - middle
-    part = jnp.where(row == 0, high, jnp.where(row == 1, middle, jnp.where(row == 2, low, 0.0)))
-    return part.astype(bfloat)
 
 
 def spread(value):
@@ -71,11 +57,6 @@
     block = block.astype(floating)
     width = block.shape[1] // 2
     return block[:8, :width] + block[:8, width:] + block[8:, :width]
-
-
-def read_scalars(block, count):
-    lane = lax.broadcasted_iota(jnp.int32, block.shape, 1)
-    return [jnp.sum(jnp.where(lane == place, block, 0.0)) for place in range(count)]
 
 
 def rms_scale(values):
@@ -161,7 +142,6 @@
 
     for copy in small + queue:
         copy.start()
-    start_group(0)
     for copy in small:
         copy.wait()
     section = lax.axis_index("section")
@@ -174,10 +154,11 @@
     active = jnp.where(section == 0, xa, xb) + (own_a * xa + own_b * xb)
     act_ref[...] = active
     nrm_ref[...] = (active * rms_scale(active) * ga_ref[...]).astype(bfloat)
-    for copy, weight, target in zip(queue, (wq_s, wk_s, wv_s), (q_ref, k_ref, v_ref)):
+    for place, (copy, weight, target) in enumerate(zip(queue, (wq_s, wk_s, wv_s), (q_ref, k_ref, v_ref))):
         copy.wait()
+        if place != 1:
+            start_group(place // 2)
         target[...] = dot(nrm_ref[...], weight[0]).astype(bfloat)
-    start_group(1)
     attention(q_ref, k_ref, v_ref, seg_ref, att_ref, None)
     for piece in range(2, pieces):
         start_group(piece)
@@ -198,9 +179,11 @@
         acc[...] += dot(hidden, wd_s[0, span, :])
         return carry
 
-    lax.fori_loop(0, pieces, one_piece, 0)
-    out_ref[:tokens, :] = acc[...].astype(bfloat)
-    out_ref[tokens:, :] = scalar_rows(mix[0] + mix[1] + cor, EXTRA, width)
+    lax.fori_loop(0, pieces, one_piece, 0, unroll=2)
+    xa = x_in[:, :width].astype(floating)
+    xb = x_in[:, width:].astype(floating)
+    out_ref[:, :width] = (xa + (mix[0][0] * xa + mix[0][1] * xb) + cor[0] * acc[...]).astype(bfloat)
+    out_ref[:, width:] = (xb + (mix[1][0] * xa + mix[1][1] * xb) + cor[1] * acc[...]).astype(bfloat)
 
 
 def forward_lite(x_in, segments, mixing, correction, gain_attn, gain_ffn, weights):
@@ -218,7 +201,7 @@
     scratch += [pltpu.SemaphoreType.DMA((4 + 3 * (weights[4].shape[2] // width),)), pltpu.SemaphoreType.DMA((6,))]
     return pl.pallas_call(
         forward_lite_kernel,
-        out_shape=[jax.ShapeDtypeStruct((tokens + EXTRA, width), bfloat)]
+        out_shape=[jax.ShapeDtypeStruct((tokens, 2 * width), bfloat)]
         + [jax.ShapeDtypeStruct(weight.shape, bfloat) for weight in weights],
         in_specs=[ANY] * len(args),
         out_specs=[VMEM] * 8,
@@ -241,14 +224,7 @@
     quarter = lax.axis_index("dp") & 3
     mix = [[mix_ref[0, i, j] for j in range(2)] for i in range(2)]
     cor = [cor_ref[0, i] for i in range(2)]
-    xa = x_in[:, :width].astype(floating)
-    xb = x_in[:, width:].astype(floating)
-    got = read_scalars(message[tokens : tokens + EXTRA, :PAIR].astype(floating), 6)
-    moved = message[:tokens, :].astype(floating)
-    sent_a = (xa + (got[0] * xa + got[1] * xb) + got[4] * moved).astype(bfloat)
-    sent_b = (xb + (got[2] * xa + got[3] * xb) + got[5] * moved).astype(bfloat)
-    x_ref[:, :width] = jnp.where(section == 0, x_in[:, :width], sent_a)
-    x_ref[:, width:] = jnp.where(section == 0, x_in[:, width:], sent_b)
+    x_ref[...] = jnp.where(section == 0, x_in[...], message[...])
     xa = x_ref[:, :width].astype(floating)
     xb = x_ref[:, width:].astype(floating)
     own_a = jnp.where(section == 0, mix[0][0], mix[1][0])
@@ -345,8 +321,6 @@
     rows = counts_ref.shape[0]
     length = tokens // rows
     section = lax.axis_index("section")
-    if message is not None:
-        got = read_scalars(message[tokens : tokens + EXTRA, :PAIR].astype(floating), 4)
     place = lax.broadcasted_iota(jnp.int32, (tokens, width), 0)
     valid = place < counts_ref[0]
     for row in range(1, rows):
@@ -354,11 +328,8 @@
     own_a = jnp.where(valid, grad_ref[:, :width].astype(floating), 0.0)
     own_b = jnp.where(valid, grad_ref[:, width:].astype(floating), 0.0)
     if message is not None:
-        later_b = own_b + message[:tokens, :].astype(floating)
-        far_a = own_a + (got[0] * own_a + got[2] * later_b)
-        far_b = later_b + (got[1] * own_a + got[3] * later_b)
-        own_a = jnp.where(section == 0, far_a, own_a).astype(bfloat).astype(floating)
-        own_b = jnp.where(section == 0, far_b, own_b).astype(bfloat).astype(floating)
+        own_a = jnp.where(section == 0, message[:, :width].astype(floating), own_a)
+        own_b = jnp.where(section == 0, message[:, width:].astype(floating), own_b)
     g_ref[:, :width] = own_a.astype(bfloat)
     g_ref[:, width:] = own_b.astype(bfloat)
     low_ref[...] = (cor_ref[0, 0] * own_a + cor_ref[0, 1] * own_b).astype(bfloat)
@@ -366,7 +337,7 @@
 
 def start(message, out_grad, counts, correction, before):
     tokens = out_grad.shape[0]
-    width = message.shape[1]
+    width = message.shape[1] // 2
     shape = jax.ShapeDtypeStruct
     return pl.pallas_call(
         lambda *refs: start_rows(*refs[:4], *refs[-2:]),
@@ -537,10 +508,12 @@
     attn_steps(q_ref, k_ref, v_ref, p_ref, do_ref, parts)
     grad_normed = normed_grad(parts, tokens, width, wq, wk, wv)
     grad_values = norm_backward(act_ref[...], ga_ref[...], grad_normed, False)[1]
-    block = cor[0] * g_in[:, :width].astype(floating) + cor[1] * g_in[:, width:].astype(floating)
-    msg_ref[:tokens, :] = (acc[...] + grad_values - block).astype(bfloat)
+    out_a = g_in[:, :width].astype(floating)
+    out_b = g_in[:, width:].astype(floating)
+    pred_b = out_b + (acc[...] + grad_values - (cor[0] * out_a + cor[1] * out_b))
     mix = [[mix_ref[0, i, j] for j in range(2)] for i in range(2)]
-    msg_ref[tokens:, :] = scalar_rows(mix[0] + mix[1], EXTRA, width)
+    msg_ref[:, :width] = (out_a + (mix[0][0] * out_a + mix[1][0] * pred_b)).astype(bfloat)
+    msg_ref[:, width:] = (pred_b + (mix[0][1] * out_a + mix[1][1] * pred_b)).astype(bfloat)
 
 
 def relay_backward(out_grad, counts, correction, mixing, gain_ffn, gain_attn, one, two, middle, queries, key_rows, value_rows,
@@ -552,7 +525,7 @@
     size = sum(weight.size for weight in weights)
     return pl.pallas_call(
         relay_kernel,
-        out_shape=shape((tokens + EXTRA, width), bfloat),
+        out_shape=shape((tokens, 2 * width), bfloat),
         in_specs=[VMEM, SMEM, SMEM, SMEM] + [VMEM] * 17,
         out_specs=VMEM,
         scratch_shapes=[wide, pltpu.VMEM((tokens, 2 * width), bfloat), narrow, narrow, pltpu.VMEM((tokens, 3 * width), bfloat)],
@@ -563,41 +536,23 @@
       *weights)
 
 
-def quarter_parts(base, products, block, lefts, rights, own_ref, far_ref, keep_ref):
+def quarter_parts(base, products, block, lefts, rights, own_ref, far_ref, all_ref, left_s, right_s):
     tokens = lefts[0].shape[0]
     tail = lefts[0].shape[1] - lefts[-1].shape[1]
-    index = lax.axis_index("dp")
-    near = (index >> 2) & 1
-    far = (index >> 3) & 1
+    mine = (lax.axis_index("dp") >> 2) & 3
     for left_at, left_wide, right_at, right_wide in products:
-        starts = [left_at if left.shape[1] > left_at else left_at - tail for left in lefts]
-
-        def one_chunk(step, carry, starts=starts, left_wide=left_wide, right_at=right_at):
-            columns = pl.ds(pl.multiple_of(right_at + step * CHUNK, PAIR), CHUNK)
-            span = pl.ds(pl.multiple_of(right_at - base + step * CHUNK, PAIR), CHUNK)
-            total = 0.0
-            for left, right, at in zip(lefts, rights, starts):
-                total = total + t_dot(left[:, at : at + left_wide], right[:tokens, columns])
-            for place in range(4):
-                part = total[place * block : (place + 1) * block, :]
-                slot = (place >> 1) ^ far
-                mine = (place & 1) == near
-
-                @pl.when(mine)
-                def _():
-                    keep_ref[slot, :, span] = part
-
-                @pl.when(jnp.logical_and(jnp.logical_not(mine), slot == 0))
-                def _():
-                    own_ref[:block, span] = part.astype(bfloat)
-
-                @pl.when(jnp.logical_and(jnp.logical_not(mine), slot == 1))
-                def _():
-                    far_ref[:block, span] = part.astype(bfloat)
-
-            return carry
-
-        lax.fori_loop(0, right_wide // CHUNK, one_chunk, 0)
+        columns = slice(right_at, right_at + right_wide)
+        span = slice(right_at - base, right_at - base + right_wide)
+        for row, (left, right) in enumerate(zip(lefts, rights)):
+            at = left_at if left.shape[1] > left_at else left_at - tail
+            rows = slice(row * tokens, (row + 1) * tokens)
+            left_s[rows, :left_wide] = left[:, at : at + left_wide]
+            right_s[rows, :right_wide] = right[:tokens, columns]
+        total = t_dot(left_s[:, :left_wide], right_s[:, :right_wide])
+        for place in range(4):
+            all_ref[place ^ mine, :, span] = total[place * block : (place + 1) * block, :]
+    own_ref[:block, :] = all_ref[1].astype(bfloat)
+    far_ref[:block, :] = all_ref[3].astype(bfloat)
 
 
 def quarter_product(lefts, rights, block, before, name, parted):
@@ -607,14 +562,16 @@
     sends = [shape((block, wide), bfloat)] * 2 if parted else [shape((2, block, wide), bfloat)]
 
     def kernel(*refs):
-        own_ref, far_ref = refs[-3:-1] if parted else (refs[-2].at[0], refs[-2].at[1])
-        quarter_parts(0, products, block, refs[:4], refs[4:8], own_ref, far_ref, refs[-1])
+        *outs, all_ref, left_s, right_s = refs[-5:] if parted else refs[-4:]
+        own_ref, far_ref = outs if parted else (outs[0].at[0], outs[0].at[1])
+        quarter_parts(0, products, block, refs[:4], refs[4:8], own_ref, far_ref, all_ref, left_s, right_s)
 
     return pl.pallas_call(
         kernel,
-        out_shape=sends + [shape((2, block, wide), floating)],
+        out_shape=sends + [shape((4, block, wide), floating)],
         in_specs=[VMEM] * 8 + [ANY] * len(before),
         out_specs=[VMEM] * (len(sends) + 1),
+        scratch_shapes=[pltpu.VMEM((4 * rows, 4 * block), bfloat), pltpu.VMEM((4 * rows, wide), bfloat)],
         compiler_params=params(SCOPED),
         cost_estimate=cost(32 * rows * block * wide, 16 * block * wide),
         name=name,
@@ -623,27 +580,30 @@
 
 def attn_product_kernel(halves, block, refs):
     lefts, rights = refs[:4], refs[4:8]
-    first_send, first_keep, small_ref, second_send, second_keep, stage = refs[-6:]
+    first_send, first_keep, small_ref, second_send, second_keep, stage, left_s, right_s = refs[-8:]
     tokens = lefts[0].shape[0]
     wide = first_keep.shape[2]
-    quarter_parts(0, halves[0], block, lefts, rights, first_send, stage, first_keep)
+    quarter_parts(0, halves[0], block, lefts, rights, first_send, stage, first_keep, left_s, right_s)
     first_send[block : 2 * block, :] = stage[...]
     small = sum(gathered_parts(right[tokens:, :wide]) for right in rights)
     small_ref[...] = small
     first_send[2 * block :, :] = spread(small)
-    quarter_parts(wide, halves[1], block, lefts, rights, second_send.at[0], second_send.at[1], second_keep)
+    quarter_parts(wide, halves[1], block, lefts, rights, second_send.at[0], second_send.at[1], second_keep, left_s, right_s)
 
 
 def attn_product(lefts, rights, halves, block, before):
     wide = rights[0].shape[1] // 2
     shape = jax.ShapeDtypeStruct
-    send, keep = shape((2, block, wide), bfloat), shape((2, block, wide), floating)
+    send, keep = shape((2, block, wide), bfloat), shape((4, block, wide), floating)
     return pl.pallas_call(
         lambda *refs: attn_product_kernel(halves, block, refs),
         out_shape=[shape((2 * block + EXTRA, wide), bfloat), keep, shape((8, wide // 2), floating), send, keep],
         in_specs=[VMEM] * 8 + [ANY] * len(before),
         out_specs=[VMEM] * 5,
-        scratch_shapes=[pltpu.VMEM(send.shape[1:], bfloat)],
+        scratch_shapes=[
+            pltpu.VMEM(send.shape[1:], bfloat), pltpu.VMEM((4 * lefts[0].shape[0], 4 * block), bfloat),
+            pltpu.VMEM((4 * lefts[0].shape[0], wide), bfloat),
+        ],
         compiler_params=params(SCOPED),
         cost_estimate=cost(wide, wide),
         name="product_attn",
@@ -653,7 +613,7 @@
 def first_sum_kernel(keep_ref, came_ref, small_ref, held_ref, passed_ref, sums_ref):
     block = held_ref.shape[0]
     held_ref[...] = keep_ref[0] + came_ref[:block, :].astype(floating)
-    passed_ref[:block, :] = (keep_ref[1] + came_ref[block : 2 * block, :].astype(floating)).astype(bfloat)
+    passed_ref[:block, :] = (keep_ref[2] + came_ref[block : 2 * block, :].astype(floating)).astype(bfloat)
     small = small_ref[...] + gathered_parts(came_ref[2 * block :, :])
     sums_ref[...] = small
     passed_ref[block:, :] = spread(small)
@@ -783,13 +743,13 @@
 def parts_once(product, *earlier):
     own, far, keep = product
     own, far = after((exchange(own, 4), exchange(far, 4)), *earlier)
-    return keep[0] + own.astype(floating), (keep[1] + far.astype(floating)).astype(bfloat)
+    return keep[0] + own.astype(floating), (keep[2] + far.astype(floating)).astype(bfloat)
 
 
 def sum_once(pair, *earlier):
     send, keep = pair
     arrived = after(exchange(send, 4), *earlier)
-    return keep[0] + arrived[0].astype(floating), (keep[1] + arrived[1].astype(floating)).astype(bfloat)
+    return keep[0] + arrived[0].astype(floating), (keep[2] + arrived[1].astype(floating)).astype(bfloat)
 
 
 def sum_twice(held, passed, *earlier):
@@ -816,16 +776,19 @@
     gate_sums = parts_once(gate_pair)
     up_pair = quarter_product(normed_ffn, ups, block, [gate_sums[1], grad_down, nearby], "product_up", False)
     up_sums = sum_once(up_pair)
-    gate_tile = sum_twice(*gate_sums).astype(bfloat)
-    rights = gather_end(rights, up_sums[1], gate_tile)
+    part = block * 3 // 4
+    gate_came = exchange(gate_sums[1][:part], 8)
+    rights = gather_end(rights, up_sums[1], gate_came)
+    up_came = exchange(jnp.concatenate([up_sums[1], gate_sums[1][part:]], axis=0), 8)
     halves = (
         [(width, block, 0, width), (width + block, block, width, width)], [(width + block, block, 2 * width, 2 * width)])
-    before = [up_sums[1], gate_tile]
+    before = [up_sums[1], gate_came]
     first_send, first_keep, small, *second_pair = attn_product(kept[:3] + [nearby], rights, halves, share, before)
-    held, first_passed, small = first_sum(first_keep, exchange(first_send, 4), small)
-    up_tile = sum_twice(*up_sums, first_passed).astype(bfloat)
+    held, first_passed, small = first_sum(first_keep, after(exchange(first_send, 4), up_came), small)
+    gate_came, up_came = after((gate_came, up_came), first_passed)
+    gate_tile = (gate_sums[0] + jnp.concatenate([gate_came, up_came[block:]], axis=0).astype(floating)).astype(bfloat)
+    up_tile = (up_sums[0] + up_came[:block].astype(floating)).astype(bfloat)
     quarter = index & 3
-    gate_tile = after(gate_tile, first_passed)
     pieces = [
         jnp.concatenate(
             [lax.dynamic_slice_in_dim(tile, (slot ^ quarter) * share, share, axis=0) for tile in (gate_tile, up_tile)], axis=1)
@@ -835,12 +798,7 @@
     grad_out, grad_query, small = first_end(held, exchange(first_passed, 8), small)
     second_sums = sum_once(second_pair, first_passed)
     grad_gate, grad_up = assemble(list(after(pieces, second_sums[1], small)))
-    held, passed = second_sums
-    passed = exchange(passed, 8)
-    grads = [grad_down[None], grad_gate, grad_up, grad_out, grad_query]
-    for span in (slice(0, width), slice(width, 2 * width)):
-        grads.append((held[:, span] + passed[:, span].astype(floating))[None])
-    return grads, small
+    return [grad_down[None], grad_gate, grad_up, grad_out, grad_query], (second_sums[0], exchange(second_sums[1], 8)), small
 
 
 def local(states_in, out_grad, counts, segments, mixing, correction, gain_attn, w_query, w_key, w_value, w_attn_out, gain_ffn,
@@ -861,8 +819,8 @@
     message = relay_backward(out_grad, counts, correction, mixing, gain_ffn, gain_attn, one, two, middle, queries, key_rows,
                              value_rows, probs, active, weights)
     message = lax.ppermute(message, "section", [(0, 1), (1, 0)])
-    g_in, low = start(message, out_grad, counts, correction, [])
-    *slots, grad_middle, grad_att, ffn_gain = ffn_backward(g_in, low, correction, gain_ffn, middle, one, two, before, weights)
+    g_in, low = start(message, out_grad, counts, correction, before)
+    *slots, grad_middle, grad_att, ffn_gain = ffn_backward(g_in, low, correction, gain_ffn, middle, one, two, [], weights)
     before = slots[0]
     if fast:
         lows = gather_end(gather_start(low), before)
@@ -873,25 +831,31 @@
     state_grads, right, small = attn_backward(x, g_in, grad_middle, grad_att, active, change, queries, key_rows, value_rows, probs,
                                               ffn_gain, gain_attn, mixing, correction, before, weights)
     if fast:
-        grads, small = quarter_grads(normed_ffn, kept, nearby, slots, right, down_pair, index)
+        grads, last, small = quarter_grads(normed_ffn, kept, nearby, slots, right, down_pair, index)
     else:
         grads = halving_grads(kept, low, slots, right[: low.shape[0]], index, count)
         small = sum_over(small, count.bit_length() - 1)
-    grad_down, grad_gate, grad_up, grad_out, grad_query, grad_key, grad_value = grads
     share = width // count
     gains = lax.dynamic_slice(small, (0, index * share), (2, share))
+    gains = gains[0:1], gains[1:2]
     sums = jnp.sum(small[2:], axis=1)
+    sums = sums[:4].reshape(1, 2, 2), sums[4:].reshape(1, 2)
+    if fast:
+        came = after(last[1], gains, sums, grads)
+        for span in (slice(0, width), slice(width, 2 * width)):
+            grads.append((last[0][:, span] + came[:, span].astype(floating))[None])
+    grad_down, grad_gate, grad_up, grad_out, grad_query, grad_key, grad_value = grads
     return (
         states,
         state_grads,
-        sums[:4].reshape(1, 2, 2),
-        sums[4:].reshape(1, 2),
-        gains[0:1],
+        sums[0],
+        sums[1],
+        gains[0],
         grad_query,
         grad_key,
         grad_value,
         grad_out,
-        gains[1:2],
+        gains[1],
         grad_gate,
         grad_up,
         grad_down,

time: 185 us -> 182 us (0.984)
  Pallas kernels: 63.3 us -> 52.6 us
  waiting for transfers between devices: 86.2 us -> 90.5 us
  local copies, waits for them, and re-layouts: 1.99 us -> 4.35 us
    pallas_call x1, Pallas kernels: 7.11 us -> 1.55 us  [attn_product(): pl.pallas_call(lambda *refs: attn_product_kernel(halves, block, refs), ou...]
    ppermute x31, waiting for transfers between devices: 70.5 us -> 73.6 us  [exchange(): lax.ppermute(value, 'dp', [(source, source ^ flips) for source in range(c...]
    pallas_call x4, Pallas kernels: 17.7 us -> 14.7 us  [the longest x1 11.1 us: relay_backward(): pl.pallas_call(relay_kernel, out_shape=shape((tokens, 2 * width), bfloat)...]
  transfers between devices with their start and end apart: 33 -> 33, of which waited for: 16 -> 17; matrix products, arithmetic and copies ran while one was open for 1% -> 3% of each run, Pallas kernels for 17% -> 17%
where the time goes in v2:
time: 182 us
  waiting for transfers between devices  90.5 us (50%)
  Pallas kernels  52.6 us (29%)
  starting transfers between devices  30 us (16%)
  local copies, waits for them, and re-layouts  4.35 us (2%)
  other arithmetic  3.68 us (2%)
    ppermute x31, waiting for transfers between devices, exchange(): lax.ppermute(value, 'dp', [(source, source ^ flips) for source in range(c...  73.6 us
    ppermute x31, starting transfers between devices, exchange(): lax.ppermute(value, 'dp', [(source, source ^ flips) for source in range(c...  25.5 us
    ppermute x2, waiting for transfers between devices, local(): message = lax.ppermute(message, 'section', [(0, 1), (1, 0)])  16.9 us
    pallas_call x1, Pallas kernels, forward_lite(): pl.pallas_call(forward_lite_kernel, out_shape=[jax.ShapeDtypeStruct((toke...  11.4 us
    pallas_call x1, Pallas kernels, relay_backward(): pl.pallas_call(relay_kernel, out_shape=shape((tokens, 2 * width), bfloat)...  11.1 us
    pallas_call x1, Pallas kernels, forward(): pl.pallas_call(lambda *refs: forward_kernel(fast, *refs), out_shape=[shap...  8.71 us
    pallas_call x1, Pallas kernels, attn_backward(): pl.pallas_call(attn_kernel, out_shape=[shape((1, tokens, 2 * width), bflo...  8.17 us
    pallas_call x1, Pallas kernels, ffn_backward(): pl.pallas_call(ffn_kernel, out_shape=[shape((tokens, width), bfloat)] * 8...  5.33 us
  transfers between devices with their start and end apart: 33, of which 17 were waited for; matrix products, arithmetic and copies ran while one was open for 3% of the time, Pallas kernels for 17%

profile of v2, /device:TPU:0, one launch (start us, length us, event | category | flops | bytes accessed | tf_op | source)
XLA Modules:
  0.0 182.2 jit_solution(18228147109135678121)
XLA Ops:
  0.7 11.4 %forward_lite.1 = (bf16[192,1536]{1,0:T(8,128)(2,1)S(1)}, bf16[1,768,768]{2,1,0:T(8,128)(2,1)S(1)}, bf16[1,768,768]{2,1,0:T(8,128)(2,1)S(1)}, bf16[1,768,768]{2,...) custom-call(bf16[192,1536]{1,0:T(8,128)(2,1)} %refs_0_.1, ...), custom_call_target="tpu_custom_call" | custom-call | flops 3623878 | bytes 18874 | tf_op jit(solution)/shard_map/forward_lite/pallas_call | solution.py:202
  12.2 3.0 %collective-permute-start = (bf16[192,1536]{1,0:T(8,128)(2,1)S(1)}, bf16[192,1536]{1,0:T(8,128)(2,1)S(1)}, u32[]{:S(2)}, u32[]{:S(2)}) collective-permute-start(bf16[192,1536]{1,0:T(8,128)(2,1)S(1)} %get-tuple-element.94), channel_id=1, source_target_pairs={{0,16},{16,0},{1,17},{17,1},{2,18},{18,2},{3,19},{19,3},{4,20},{20... | collective-permute-start | bytes 1769480 | tf_op jit(solution)/shard_map/ppermute | solution.py:812
  15.1 13.3 %collective-permute-done.refs_1_ = bf16[192,1536]{1,0:T(8,128)(2,1)S(1)} collective-permute-done((bf16[192,1536]{1,0:T(8,128)(2,1)S(1)}, bf16[192,1536]{1,0:T(8,128)(2,1)S(1)}, u32[]{:S(2)}, u32[]{:S(2)}) %collective-permute-start) | collective-permute-done | bytes 589856 | tf_op jit(solution)/shard_map/ppermute | solution.py:812
  28.5 8.7 %forward_full.1 = (bf16[192,1536]{1,0:T(8,128)(2,1)S(1)}, bf16[1,192,1536]{2,1,0:T(8,128)(2,1)}, bf16[192,768]{1,0:T(8,128)(2,1)S(1)}, bf16[192,768]{1,0:T(8,128...) custom-call(bf16[192,1536]{1,0:T(8,128)(2,1)S(1)} %copy-done.2, ...), custom_call_target="tpu_custom_call" | custom-call | flops 3623878 | bytes 18874 | tf_op jit(solution)/shard_map/forward_full/pallas_call | solution.py:307
  37.2 1.8 collective-permute-start.3
  39.0 11.1 %backward_relay.1 = bf16[192,1536]{1,0:T(8,128)(2,1)S(1)} custom-call(bf16[192,1536]{1,0:T(8,128)(2,1)S(1)} %copy-done, s32[2]{0:T(128)S(1)} %copy-done.10, f32[1,2]{1,0:T(1,128)S(1)} %copy-done.7, f32[1,2,2]{2,1,0:T(2,128)S(1)} %copy-done.8, f32[1,768]{1,0:T(1,128)S(1)} %copy-done.5, f32[1,768]{1,0:T(1,128)S(1)} %copy-done.6, ...), custom_call_target="tpu_custom_call" | custom-call | flops 3623878 | bytes 18874 | tf_op jit(solution)/shard_map/backward_relay/pallas_call | solution.py:526
  50.2 1.6 collective-permute-start.1
  51.8 10.4 %collective-permute-done.4.refs_6_.refs_3_ = bf16[192,768]{1,0:T(8,128)(2,1)S(1)} collective-permute-done((bf16[192,768]{1,0:T(8,128)(2,1)S(1)}, bf16[192,768]{1,0:T(8,128)(2,1)S(1)}, u32[]{:S(2)}, u32[]{:S(2)}) %collective-permute-start.4) | collective-permute-done | bytes 294944 | tf_op jit(solution)/shard_map/ppermute | solution.py:682
  62.2 3.5 %collective-permute-done.1.refs_0_ = bf16[192,1536]{1,0:T(8,128)(2,1)S(1)} collective-permute-done((bf16[192,1536]{1,0:T(8,128)(2,1)S(1)}, bf16[192,1536]{1,0:T(8,128)(2,1)S(1)}, u32[]{:S(2)}, u32[]{:S(2)}) %collective-permute-start.1) | collective-permute-done | bytes 589856 | tf_op jit(solution)/shard_map/ppermute | solution.py:821
  65.7 0.8 backward_start.1
  66.9 5.3 %backward_ffn.1 = (bf16[192,768]{1,0:T(8,128)(2,1)S(1)}, bf16[192,768]{1,0:T(8,128)(2,1)S(1)}, bf16[192,768]{1,0:T(8,128)(2,1)S(1)}, bf16[192,768]{1,0:T(8,128)(...) custom-call(bf16[192,1536]{1,0:T(8,128)(2,1)S(1)} %get-tuple-element, ...), custom_call_target="tpu_custom_call" | custom-call | flops 2717908 | bytes 14155 | tf_op jit(solution)/shard_map/backward_ffn/pallas_call | solution.py:400
  72.2 2.7 %collective-permute-done.6.refs_6_ = bf16[192,768]{1,0:T(8,128)(2,1)S(1)} collective-permute-done((bf16[192,768]{1,0:T(8,128)(2,1)S(1)}, bf16[192,768]{1,0:T(8,128)(2,1)S(1)}, u32[]{:S(2)}, u32[]{:S(2)}) %collective-permute-start.6) | collective-permute-done | bytes 294944 | tf_op jit(solution)/shard_map/ppermute | solution.py:682
  74.9 1.6 collective-permute-done.7.refs_7_
  76.5 1.2 product_down.1
  77.7 1.6 collective-permute-start.13
  80.4 0.9 collective-permute-start.12
  81.4 8.2 %backward_attn.1 = (bf16[1,192,1536]{2,1,0:T(8,128)(2,1)}, bf16[208,3072]{1,0:T(8,128)(2,1)S(1)}, f32[8,768]{1,0:T(8,128)}) custom-call(bf16[192,768]{1,0:T(8,128)(2,1)S(1)} %get-tuple-element.116.datt_ref, bf16[192,768]{1,0:T(8,128)(2,1)S(1)} %get-tuple-element.106.q_ref, bf16[192,768]{1,0:T(8,128)(2,1)S(1)} %get-tuple-element.107.k_ref, ...), custom_call_target="tpu_custom_call" | custom-call | flops 1132462 | bytes 4718 | tf_op jit(solution)/shard_map/backward_attn/pallas_call | solution.py:480
  89.5 3.6 %collective-permute-done.13 = bf16[2,192,768]{2,1,0:T(8,128)(2,1)S(1)} collective-permute-done((bf16[2,192,768]{2,1,0:T(8,128)(2,1)S(1)}, bf16[2,192,768]{2,1,0:T(8,128)(2,1)S(1)}, u32[]{:S(2)}, u32[]{:S(2)}) %collective-permute-start.13) | collective-permute-done | bytes 589856 | tf_op jit(solution)/shard_map/ppermute | solution.py:682
  93.6 1.5 collective-permute-start.16
  95.2 1.2 product_gate.1
  96.4 1.6 collective-permute-start.19
  98.5 2.6 %collective-permute-start.21 = (bf16[192,768]{1,0:T(8,128)(2,1)S(1)}, bf16[192,768]{1,0:T(8,128)(2,1)S(1)}, u32[]{:S(2)}, u32[]{:S(2)}) collective-permute-start(bf16[192,768]{1,0:T(8,128)(2,1)S(1)} %fusion.4.refs_9_), channel_id=1, source_target_pairs={{0,8},{1,9},{2,10},{3,11},{4,12},{5,13},{6,14},{7,15},{8,0},{9,1},... | collective-permute-start | bytes 884744 | tf_op jit(solution)/shard_map/ppermute | solution.py:682
  101.1 2.0 %collective-permute-done.15.refs_6_ = bf16[192,768]{1,0:T(8,128)(2,1)S(1)} collective-permute-done((bf16[192,768]{1,0:T(8,128)(2,1)S(1)}, bf16[192,768]{1,0:T(8,128)(2,1)S(1)}, u32[]{:S(2)}, u32[]{:S(2)}) %collective-permute-start.15) | collective-permute-done | bytes 294944 | tf_op jit(solution)/shard_map/ppermute | solution.py:682
  103.1 5.5 %collective-permute-done.16.refs_7_ = bf16[192,768]{1,0:T(8,128)(2,1)S(1)} collective-permute-done((bf16[192,768]{1,0:T(8,128)(2,1)S(1)}, bf16[192,768]{1,0:T(8,128)(2,1)S(1)}, u32[]{:S(2)}, u32[]{:S(2)}) %collective-permute-start.16) | collective-permute-done | bytes 294944 | tf_op jit(solution)/shard_map/ppermute | solution.py:682
  109.0 3.6 %collective-permute-done.19 = bf16[192,768]{1,0:T(8,128)(2,1)S(1)} collective-permute-done((bf16[192,768]{1,0:T(8,128)(2,1)S(1)}, bf16[192,768]{1,0:T(8,128)(2,1)S(1)}, u32[]{:S(2)}, u32[]{:S(2)}) %collective-permute-start.19) | collective-permute-done | bytes 294944 | tf_op jit(solution)/shard_map/ppermute | solution.py:682
  112.6 5.7 %collective-permute-done.20 = bf16[192,768]{1,0:T(8,128)(2,1)S(1)} collective-permute-done((bf16[192,768]{1,0:T(8,128)(2,1)S(1)}, bf16[192,768]{1,0:T(8,128)(2,1)S(1)}, u32[]{:S(2)}, u32[]{:S(2)}) %collective-permute-start.20) | collective-permute-done | bytes 294944 | tf_op jit(solution)/shard_map/ppermute | solution.py:682
  118.5 1.2 product_up.1
  119.7 2.7 %collective-permute-start.22 = (bf16[2,192,768]{2,1,0:T(8,128)(2,1)S(1)}, bf16[2,192,768]{2,1,0:T(8,128)(2,1)S(1)}, u32[]{:S(2)}, u32[]{:S(2)}) collective-permute-start(bf16[2,192,768]{2,1,0:T(8,128)(2,1)S(1)} %get-tuple-element.150), channel_id=1, source_target_pairs={{0,4},{1,5},{2,6},{3,7},{4,0},{5,1},{6,2},{7,3},{8,12},{9,13},{10,... | collective-permute-start | bytes 1769480 | tf_op jit(solution)/shard_map/ppermute | solution.py:682
  122.4 1.7 collective-permute-start.23
  124.0 16.0 %collective-permute-done.22 = bf16[2,192,768]{2,1,0:T(8,128)(2,1)S(1)} collective-permute-done((bf16[2,192,768]{2,1,0:T(8,128)(2,1)S(1)}, bf16[2,192,768]{2,1,0:T(8,128)(2,1)S(1)}, u32[]{:S(2)}, u32[]{:S(2)}) %collective-permute-start.22) | collective-permute-done | bytes 589856 | tf_op jit(solution)/shard_map/ppermute | solution.py:682
  140.1 0.7 copy-done.12
  140.9 0.8 pad_maximum_fusion
  141.6 1.8 %collective-permute-start.26 = (bf16[240,768]{1,0:T(8,128)(2,1)}, bf16[240,768]{1,0:T(8,128)(2,1)}, u32[]{:S(2)}, u32[]{:S(2)}) collective-permute-start(bf16[240,768]{1,0:T(8,128)(2,1)} %pad_maximum_fusion), channel_id=1, source_target_pairs={{0,8},{1,9},{2,10},{3,11},{4,12},{5,13},{6,14},{7,15},{8,0},{9,1},... | collective-permute-start | bytes 1105928 | tf_op jit(solution)/shard_map/ppermute | solution.py:682
  143.8 1.5 product_attn.1
  146.1 1.2 collective-permute-start.25
  147.2 0.9 collective-permute-start.28
  148.1 13.7 %collective-permute-done.26 = bf16[240,768]{1,0:T(8,128)(2,1)} collective-permute-done((bf16[240,768]{1,0:T(8,128)(2,1)}, bf16[240,768]{1,0:T(8,128)(2,1)}, u32[]{:S(2)}, u32[]{:S(2)}) %collective-permute-start.26) | collective-permute-done | bytes 368672 | tf_op jit(solution)/shard_map/ppermute | solution.py:682
  161.8 2.7 %collective-permute-done.25.came_ref = bf16[112,1536]{1,0:T(8,128)(2,1)S(1)} collective-permute-done((bf16[112,1536]{1,0:T(8,128)(2,1)S(1)}, bf16[112,1536]{1,0:T(8,128)(2,1)S(1)}, u32[]{:S(2)}, u32[]{:S(2)}) %collective-permute-start.25) | collective-permute-done | bytes 344096 | tf_op jit(solution)/shard_map/ppermute | solution.py:682
  164.6 1.2 collective-permute-start.27
  165.8 0.9 slice.109
  166.7 1.7 fusion
  169.2 1.4 collective-permute-start.30
  171.2 1.3 collective-permute-start.29
  172.5 3.4 %collective-permute-done.27.came_ref = bf16[64,1536]{1,0:T(8,128)(2,1)S(1)} collective-permute-done((bf16[64,1536]{1,0:T(8,128)(2,1)S(1)}, bf16[64,1536]{1,0:T(8,128)(2,1)S(1)}, u32[]{:S(2)}, u32[]{:S(2)}) %collective-permute-start.27) | collective-permute-done | bytes 196640 | tf_op jit(solution)/shard_map/ppermute | solution.py:682
  175.9 0.7 first_end.1
  178.1 1.1 assemble.1
  179.7 1.7 collective-permute-done.29
  181.4 0.7 fusion.7
  (83 shorter events, 7.6 us)
Async XLA Ops:
  0.6 27.8 %copy-start.2 = (bf16[192,1536]{1,0:T(8,128)(2,1)S(1)}, bf16[192,1536]{1,0:T(8,128)(2,1)}, u32[]{:S(2)}) copy-start(bf16[192,1536]{1,0:T(8,128)(2,1)} %refs_0_.1) | copy-start | bytes 1769476
  0.7 27.8 %copy-start.9 = (s32[2,96]{1,0:T(2,128)S(1)}, s32[2,96]{1,0:T(2,128)}, u32[]{:S(2)}) copy-start(s32[2,96]{1,0:T(2,128)} %refs_2_.2) | copy-start | bytes 2308
  0.7 27.8 %copy-start.8 = (f32[1,2,2]{2,1,0:T(2,128)S(1)}, f32[1,2,2]{2,1,0:T(2,128)}, u32[]{:S(2)}) copy-start(f32[1,2,2]{2,1,0:T(2,128)} %mix_ref.3) | copy-start | bytes 52
  0.7 27.8 %copy-start.7 = (f32[1,2]{1,0:T(1,128)S(1)}, f32[1,2]{1,0:T(1,128)}, u32[]{:S(2)}) copy-start(f32[1,2]{1,0:T(1,128)} %cor_ref.5) | copy-start | bytes 28
  0.7 27.8 %copy-start.6 = (f32[1,768]{1,0:T(1,128)S(1)}, f32[1,768]{1,0:T(1,128)}, u32[]{:S(2)}) copy-start(f32[1,768]{1,0:T(1,128)} %ga_ref.3) | copy-start | bytes 9220
  0.7 27.8 %copy-start.5 = (f32[1,768]{1,0:T(1,128)S(1)}, f32[1,768]{1,0:T(1,128)}, u32[]{:S(2)}) copy-start(f32[1,768]{1,0:T(1,128)} %gf_ref.3) | copy-start | bytes 9220
  12.2 16.3 %collective-permute-start = (bf16[192,1536]{1,0:T(8,128)(2,1)S(1)}, bf16[192,1536]{1,0:T(8,128)(2,1)S(1)}, u32[]{:S(2)}, u32[]{:S(2)}) collective-permute-start(bf16[192,1536]{1,0:T(8,128)(2,1)S(1)} %get-tuple-element.94), channel_id=1, source_target_pairs={{0,16},{16,0},{1,17},{17,1},{2,18},{18,2},{3,19},{19,3},{4,20},{20... | collective-permute-start | bytes 1769480 | tf_op jit(solution)/shard_map/ppermute | solution.py:812
  28.5 10.5 %copy-start = (bf16[192,1536]{1,0:T(8,128)(2,1)S(1)}, bf16[192,1536]{1,0:T(8,128)(2,1)}, u32[]{:S(2)}) copy-start(bf16[192,1536]{1,0:T(8,128)(2,1)} %refs_1_.1) | copy-start | bytes 1769476
  28.5 10.5 %copy-start.10 = (s32[2]{0:T(128)S(1)}, s32[2]{0:T(128)}, u32[]{:S(2)}) copy-start(s32[2]{0:T(128)} %refs_2_.3) | copy-start | bytes 28
  37.2 28.5 %collective-permute-start.2 = (bf16[192,1920]{1,0:T(8,128)(2,1)S(1)}, bf16[192,1920]{1,0:T(8,128)(2,1)S(1)}, u32[]{:S(2)}, u32[]{:S(2)}) collective-permute-start(bf16[192,1920]{1,0:T(8,128)(2,1)S(1)} %get-tuple-element.111), channel_id=1, source_target_pairs={{0,1},{1,0},{2,3},{3,2},{4,5},{5,4},{6,7},{7,6},{8,9},{9,8},{10,11... | collective-permute-start | bytes 2211848 | tf_op jit(solution)/shard_map/ppermute | solution.py:682
  37.2 28.5 %collective-permute-start.3 = (bf16[192,1920]{1,0:T(8,128)(2,1)S(1)}, bf16[192,1920]{1,0:T(8,128)(2,1)S(1)}, u32[]{:S(2)}, u32[]{:S(2)}) collective-permute-start(bf16[192,1920]{1,0:T(8,128)(2,1)S(1)} %get-tuple-element.112), channel_id=1, source_target_pairs={{0,2},{1,3},{2,0},{3,1},{4,6},{5,7},{6,4},{7,5},{8,10},{9,11},{10,... | collective-permute-start | bytes 2211848 | tf_op jit(solution)/shard_map/ppermute | solution.py:682
  50.2 15.5 %collective-permute-start.1 = (bf16[192,1536]{1,0:T(8,128)(2,1)S(1)}, bf16[192,1536]{1,0:T(8,128)(2,1)S(1)}, u32[]{:S(2)}, u32[]{:S(2)}) collective-permute-start(bf16[192,1536]{1,0:T(8,128)(2,1)S(1)} %backward_relay.1), channel_id=1, source_target_pairs={{0,16},{16,0},{1,17},{17,1},{2,18},{18,2},{3,19},{19,3},{4,20},{20... | collective-permute-start | bytes 1769480 | tf_op jit(solution)/shard_map/ppermute | solution.py:821
  51.7 10.4 %collective-permute-start.4 = (bf16[192,768]{1,0:T(8,128)(2,1)S(1)}, bf16[192,768]{1,0:T(8,128)(2,1)S(1)}, u32[]{:S(2)}, u32[]{:S(2)}) collective-permute-start(bf16[192,768]{1,0:T(8,128)(2,1)S(1)} %get-tuple-element.113), channel_id=1, source_target_pairs={{0,3},{1,2},{2,1},{3,0},{4,7},{5,6},{6,5},{7,4},{8,11},{9,10},{10,... | collective-permute-start | bytes 884744 | tf_op jit(solution)/shard_map/ppermute | solution.py:682
  66.5 8.4 %collective-permute-start.6 = (bf16[192,768]{1,0:T(8,128)(2,1)S(1)}, bf16[192,768]{1,0:T(8,128)(2,1)S(1)}, u32[]{:S(2)}, u32[]{:S(2)}) collective-permute-start(bf16[192,768]{1,0:T(8,128)(2,1)S(1)} %get-tuple-element.115.low_ref.refs_4_), channel_id=1, source_target_pairs={{0,2},{1,3},{2,0},{3,1},{4,6},{5,7},{6,4},{7,5},{8,10},{9,11},{10,... | collective-permute-start | bytes 884744 | tf_op jit(solution)/shard_map/ppermute | solution.py:682
  66.9 8.0 %collective-permute-start.5 = (bf16[192,768]{1,0:T(8,128)(2,1)S(1)}, bf16[192,768]{1,0:T(8,128)(2,1)S(1)}, u32[]{:S(2)}, u32[]{:S(2)}) collective-permute-start(bf16[192,768]{1,0:T(8,128)(2,1)S(1)} %get-tuple-element.115.low_ref.refs_4_), channel_id=1, source_target_pairs={{0,1},{1,0},{2,3},{3,2},{4,5},{5,4},{6,7},{7,6},{8,9},{9,8},{10,11... | collective-permute-start | bytes 884744 | tf_op jit(solution)/shard_map/ppermute | solution.py:682
  74.9 1.6 collective-permute-start.7
  77.7 15.4 %collective-permute-start.13 = (bf16[2,192,768]{2,1,0:T(8,128)(2,1)S(1)}, bf16[2,192,768]{2,1,0:T(8,128)(2,1)S(1)}, u32[]{:S(2)}, u32[]{:S(2)}) collective-permute-start(bf16[2,192,768]{2,1,0:T(8,128)(2,1)S(1)} %get-tuple-element.124.before), channel_id=1, source_target_pairs={{0,4},{1,5},{2,6},{3,7},{4,0},{5,1},{6,2},{7,3},{8,12},{9,13},{10,... | collective-permute-start | bytes 1769480 | tf_op jit(solution)/shard_map/ppermute | solution.py:682
  79.4 13.9 %collective-permute-start.9 = (bf16[192,768]{1,0:T(8,128)(2,1)S(1)}, bf16[192,768]{1,0:T(8,128)(2,1)S(1)}, u32[]{:S(2)}, u32[]{:S(2)}) collective-permute-start(bf16[192,768]{1,0:T(8,128)(2,1)S(1)} %slice.117.refs_2_), channel_id=1, source_target_pairs={{0,1},{1,0},{2,3},{3,2},{4,5},{5,4},{6,7},{7,6},{8,9},{9,8},{10,11... | collective-permute-start | bytes 884744 | tf_op jit(solution)/shard_map/ppermute | solution.py:682
  79.4 14.2 %collective-permute-start.10 = (bf16[192,768]{1,0:T(8,128)(2,1)S(1)}, bf16[192,768]{1,0:T(8,128)(2,1)S(1)}, u32[]{:S(2)}, u32[]{:S(2)}) collective-permute-start(bf16[192,768]{1,0:T(8,128)(2,1)S(1)} %get-tuple-element.135), channel_id=1, source_target_pairs={{0,1},{1,0},{2,3},{3,2},{4,5},{5,4},{6,7},{7,6},{8,9},{9,8},{10,11... | collective-permute-start | bytes 884744 | tf_op jit(solution)/shard_map/ppermute | solution.py:682
  79.9 15.2 %collective-permute-start.11 = (bf16[192,768]{1,0:T(8,128)(2,1)S(1)}, bf16[192,768]{1,0:T(8,128)(2,1)S(1)}, u32[]{:S(2)}, u32[]{:S(2)}) collective-permute-start(bf16[192,768]{1,0:T(8,128)(2,1)S(1)} %get-tuple-element.136), channel_id=1, source_target_pairs={{0,2},{1,3},{2,0},{3,1},{4,6},{5,7},{6,4},{7,5},{8,10},{9,11},{10,... | collective-permute-start | bytes 884744 | tf_op jit(solution)/shard_map/ppermute | solution.py:682
  80.4 14.7 %collective-permute-start.12 = (bf16[192,768]{1,0:T(8,128)(2,1)S(1)}, bf16[192,768]{1,0:T(8,128)(2,1)S(1)}, u32[]{:S(2)}, u32[]{:S(2)}) collective-permute-start(bf16[192,768]{1,0:T(8,128)(2,1)S(1)} %get-tuple-element.137), channel_id=1, source_target_pairs={{0,3},{1,2},{2,1},{3,0},{4,7},{5,6},{6,5},{7,4},{8,11},{9,10},{10,... | collective-permute-start | bytes 884744 | tf_op jit(solution)/shard_map/ppermute | solution.py:682
  93.1 5.3 %collective-permute-start.14 = (bf16[192,768]{1,0:T(8,128)(2,1)S(1)}, bf16[192,768]{1,0:T(8,128)(2,1)S(1)}, u32[]{:S(2)}, u32[]{:S(2)}) collective-permute-start(bf16[192,768]{1,0:T(8,128)(2,1)S(1)} %get-tuple-element.141), channel_id=1, source_target_pairs={{0,1},{1,0},{2,3},{3,2},{4,5},{5,4},{6,7},{7,6},{8,9},{9,8},{10,11... | collective-permute-start | bytes 884744 | tf_op jit(solution)/shard_map/ppermute | solution.py:682
  93.2 9.9 %collective-permute-start.15 = (bf16[192,768]{1,0:T(8,128)(2,1)S(1)}, bf16[192,768]{1,0:T(8,128)(2,1)S(1)}, u32[]{:S(2)}, u32[]{:S(2)}) collective-permute-start(bf16[192,768]{1,0:T(8,128)(2,1)S(1)} %get-tuple-element.142), channel_id=1, source_target_pairs={{0,2},{1,3},{2,0},{3,1},{4,6},{5,7},{6,4},{7,5},{8,10},{9,11},{10,... | collective-permute-start | bytes 884744 | tf_op jit(solution)/shard_map/ppermute | solution.py:682
  93.6 15.0 %collective-permute-start.16 = (bf16[192,768]{1,0:T(8,128)(2,1)S(1)}, bf16[192,768]{1,0:T(8,128)(2,1)S(1)}, u32[]{:S(2)}, u32[]{:S(2)}) collective-permute-start(bf16[192,768]{1,0:T(8,128)(2,1)S(1)} %get-tuple-element.143), channel_id=1, source_target_pairs={{0,3},{1,2},{2,1},{3,0},{4,7},{5,6},{6,5},{7,4},{8,11},{9,10},{10,... | collective-permute-start | bytes 884744 | tf_op jit(solution)/shard_map/ppermute | solution.py:682
  96.4 47.1 %copy-start.3 = (f32[4,192,768]{2,1,0:T(8,128)}, f32[4,192,768]{2,1,0:T(8,128)S(1)}, u32[]{:S(2)}) copy-start(f32[4,192,768]{2,1,0:T(8,128)S(1)} %get-tuple-element.146) | copy-start | bytes 7077892
  96.4 16.2 %collective-permute-start.19 = (bf16[192,768]{1,0:T(8,128)(2,1)S(1)}, bf16[192,768]{1,0:T(8,128)(2,1)S(1)}, u32[]{:S(2)}, u32[]{:S(2)}) collective-permute-start(bf16[192,768]{1,0:T(8,128)(2,1)S(1)} %get-tuple-element.140), channel_id=1, source_target_pairs={{0,4},{1,5},{2,6},{3,7},{4,0},{5,1},{6,2},{7,3},{8,12},{9,13},{10,... | collective-permute-start | bytes 884744 | tf_op jit(solution)/shard_map/ppermute | solution.py:682
  98.0 20.3 %collective-permute-start.20 = (bf16[192,768]{1,0:T(8,128)(2,1)S(1)}, bf16[192,768]{1,0:T(8,128)(2,1)S(1)}, u32[]{:S(2)}, u32[]{:S(2)}) collective-permute-start(bf16[192,768]{1,0:T(8,128)(2,1)S(1)} %get-tuple-element.147), channel_id=1, source_target_pairs={{0,4},{1,5},{2,6},{3,7},{4,0},{5,1},{6,2},{7,3},{8,12},{9,13},{10,... | collective-permute-start | bytes 884744 | tf_op jit(solution)/shard_map/ppermute | solution.py:682
  98.5 19.8 %collective-permute-start.21 = (bf16[192,768]{1,0:T(8,128)(2,1)S(1)}, bf16[192,768]{1,0:T(8,128)(2,1)S(1)}, u32[]{:S(2)}, u32[]{:S(2)}) collective-permute-start(bf16[192,768]{1,0:T(8,128)(2,1)S(1)} %fusion.4.refs_9_), channel_id=1, source_target_pairs={{0,8},{1,9},{2,10},{3,11},{4,12},{5,13},{6,14},{7,15},{8,0},{9,1},... | collective-permute-start | bytes 884744 | tf_op jit(solution)/shard_map/ppermute | solution.py:682
  103.1 15.3 %collective-permute-start.8 = (bf16[192,384]{1,0:T(8,128)(2,1)S(1)}, bf16[192,384]{1,0:T(8,128)(2,1)S(1)}, u32[]{:S(2)}, u32[]{:S(2)}) collective-permute-start(bf16[192,384]{1,0:T(8,128)(2,1)S(1)} %get-tuple-element.132), channel_id=1, source_target_pairs={{0,3},{1,2},{2,1},{3,0},{4,7},{5,6},{6,5},{7,4},{8,11},{9,10},{10,... | collective-permute-start | bytes 442376 | tf_op jit(solution)/shard_map/ppermute | solution.py:682
  108.6 32.2 %collective-permute-start.18 = (bf16[208,3072]{1,0:T(8,128)(2,1)S(1)}, bf16[208,3072]{1,0:T(8,128)(2,1)S(1)}, u32[]{:S(2)}, u32[]{:S(2)}) collective-permute-start(bf16[208,3072]{1,0:T(8,128)(2,1)S(1)} %get-tuple-element.144.refs_8_.refs_4_), channel_id=1, source_target_pairs={{0,2},{1,3},{2,0},{3,1},{4,6},{5,7},{6,4},{7,5},{8,10},{9,11},{10,... | collective-permute-start | bytes 3833864 | tf_op jit(solution)/shard_map/ppermute | solution.py:682
  112.6 7.1 %copy-start.13 = (bf16[192,768]{1,0:T(8,128)(2,1)}, bf16[192,768]{1,0:T(8,128)(2,1)S(1)}, u32[]{:S(2)}) copy-start(bf16[192,768]{1,0:T(8,128)(2,1)S(1)} %collective-permute-done.19) | copy-start | bytes 884740
  118.4 4.0 %copy-start.1 = (f32[192,768]{1,0:T(8,128)}, f32[192,768]{1,0:T(8,128)S(1)}, u32[]{:S(2)}) copy-start(f32[192,768]{1,0:T(8,128)S(1)} %bitcast_add_fusion.2.refs_9_) | copy-start | bytes 1769476
  119.7 23.8 %copy-start.4 = (f32[4,192,768]{2,1,0:T(8,128)}, f32[4,192,768]{2,1,0:T(8,128)S(1)}, u32[]{:S(2)}) copy-start(f32[4,192,768]{2,1,0:T(8,128)S(1)} %get-tuple-element.149) | copy-start | bytes 7077892
  119.7 20.4 %collective-permute-start.22 = (bf16[2,192,768]{2,1,0:T(8,128)(2,1)S(1)}, bf16[2,192,768]{2,1,0:T(8,128)(2,1)S(1)}, u32[]{:S(2)}, u32[]{:S(2)}) collective-permute-start(bf16[2,192,768]{2,1,0:T(8,128)(2,1)S(1)} %get-tuple-element.150), channel_id=1, source_target_pairs={{0,4},{1,5},{2,6},{3,7},{4,0},{5,1},{6,2},{7,3},{8,12},{9,13},{10,... | collective-permute-start | bytes 1769480 | tf_op jit(solution)/shard_map/ppermute | solution.py:682
  122.3 21.1 %collective-permute-start.17 = (bf16[208,3072]{1,0:T(8,128)(2,1)S(1)}, bf16[208,3072]{1,0:T(8,128)(2,1)S(1)}, u32[]{:S(2)}, u32[]{:S(2)}) collective-permute-start(bf16[208,3072]{1,0:T(8,128)(2,1)S(1)} %get-tuple-element.144.refs_8_.refs_4_), channel_id=1, source_target_pairs={{0,1},{1,0},{2,3},{3,2},{4,5},{5,4},{6,7},{7,6},{8,9},{9,8},{10,11... | collective-permute-start | bytes 3833864 | tf_op jit(solution)/shard_map/ppermute | solution.py:682
  122.4 17.7 %collective-permute-start.23 = (bf16[144,768]{1,0:T(8,128)(2,1)S(1)}, bf16[144,768]{1,0:T(8,128)(2,1)S(1)}, u32[]{:S(2)}, u32[]{:S(2)}) collective-permute-start(bf16[144,768]{1,0:T(8,128)(2,1)S(1)} %slice.119), channel_id=1, source_target_pairs={{0,8},{1,9},{2,10},{3,11},{4,12},{5,13},{6,14},{7,15},{8,0},{9,1},... | collective-permute-start | bytes 663560 | tf_op jit(solution)/shard_map/ppermute | solution.py:682
  140.0 0.8 copy-start.12
  140.8 3.0 %collective-permute-start.24 = (bf16[208,3072]{1,0:T(8,128)(2,1)S(1)}, bf16[208,3072]{1,0:T(8,128)(2,1)S(1)}, u32[]{:S(2)}, u32[]{:S(2)}) collective-permute-start(bf16[208,3072]{1,0:T(8,128)(2,1)S(1)} %collective-permute-done.18.refs_6_), channel_id=1, source_target_pairs={{0,1},{1,0},{2,3},{3,2},{4,5},{5,4},{6,7},{7,6},{8,9},{9,8},{10,11... | collective-permute-start | bytes 3833864 | tf_op jit(solution)/shard_map/ppermute | solution.py:682
  141.6 20.2 %collective-permute-start.26 = (bf16[240,768]{1,0:T(8,128)(2,1)}, bf16[240,768]{1,0:T(8,128)(2,1)}, u32[]{:S(2)}, u32[]{:S(2)}) collective-permute-start(bf16[240,768]{1,0:T(8,128)(2,1)} %pad_maximum_fusion), channel_id=1, source_target_pairs={{0,8},{1,9},{2,10},{3,11},{4,12},{5,13},{6,14},{7,15},{8,0},{9,1},... | collective-permute-start | bytes 1105928 | tf_op jit(solution)/shard_map/ppermute | solution.py:682
  145.4 0.7 copy-start.11
  146.1 18.5 %collective-permute-start.25 = (bf16[112,1536]{1,0:T(8,128)(2,1)S(1)}, bf16[112,1536]{1,0:T(8,128)(2,1)S(1)}, u32[]{:S(2)}, u32[]{:S(2)}) collective-permute-start(bf16[112,1536]{1,0:T(8,128)(2,1)S(1)} %get-tuple-element.153), channel_id=1, source_target_pairs={{0,4},{1,5},{2,6},{3,7},{4,0},{5,1},{6,2},{7,3},{8,12},{9,13},{10,... | collective-permute-start | bytes 1032200 | tf_op jit(solution)/shard_map/ppermute | solution.py:682
  147.2 23.9 %collective-permute-start.28 = (bf16[2,48,1536]{2,1,0:T(8,128)(2,1)}, bf16[2,48,1536]{2,1,0:T(8,128)(2,1)S(1)}, u32[]{:S(2)}, u32[]{:S(2)}) collective-permute-start(bf16[2,48,1536]{2,1,0:T(8,128)(2,1)} %copy-done.11), channel_id=1, source_target_pairs={{0,4},{1,5},{2,6},{3,7},{4,0},{5,1},{6,2},{7,3},{8,12},{9,13},{10,... | collective-permute-start | bytes 884744 | tf_op jit(solution)/shard_map/ppermute | solution.py:682
  164.6 11.3 %collective-permute-start.27 = (bf16[64,1536]{1,0:T(8,128)(2,1)S(1)}, bf16[64,1536]{1,0:T(8,128)(2,1)S(1)}, u32[]{:S(2)}, u32[]{:S(2)}) collective-permute-start(bf16[64,1536]{1,0:T(8,128)(2,1)S(1)} %get-tuple-element.157), channel_id=1, source_target_pairs={{0,8},{1,9},{2,10},{3,11},{4,12},{5,13},{6,14},{7,15},{8,0},{9,1},... | collective-permute-start | bytes 589832 | tf_op jit(solution)/shard_map/ppermute | solution.py:682
  168.5 8.3 %collective-permute-start.32 = (bf16[48,1536]{1,0:T(8,128)(2,1)S(1)}, bf16[48,1536]{1,0:T(8,128)(2,1)S(1)}, u32[]{:S(2)}, u32[]{:S(2)}) collective-permute-start(bf16[48,1536]{1,0:T(8,128)(2,1)S(1)} %pad_maximum_fusion.4), channel_id=1, source_target_pairs={{0,3},{1,2},{2,1},{3,0},{4,7},{5,6},{6,5},{7,4},{8,11},{9,10},{10,... | collective-permute-start | bytes 442376 | tf_op jit(solution)/shard_map/ppermute | solution.py:682
  168.6 8.2 %collective-permute-start.31 = (bf16[48,1536]{1,0:T(8,128)(2,1)S(1)}, bf16[48,1536]{1,0:T(8,128)(2,1)S(1)}, u32[]{:S(2)}, u32[]{:S(2)}) collective-permute-start(bf16[48,1536]{1,0:T(8,128)(2,1)S(1)} %pad_maximum_fusion.3), channel_id=1, source_target_pairs={{0,2},{1,3},{2,0},{3,1},{4,6},{5,7},{6,4},{7,5},{8,10},{9,11},{10,... | collective-permute-start | bytes 442376 | tf_op jit(solution)/shard_map/ppermute | solution.py:682
  169.2 7.7 %collective-permute-start.30 = (bf16[48,1536]{1,0:T(8,128)(2,1)S(1)}, bf16[48,1536]{1,0:T(8,128)(2,1)S(1)}, u32[]{:S(2)}, u32[]{:S(2)}) collective-permute-start(bf16[48,1536]{1,0:T(8,128)(2,1)S(1)} %pad_maximum_fusion.2), channel_id=1, source_target_pairs={{0,1},{1,0},{2,3},{3,2},{4,5},{5,4},{6,7},{7,6},{8,9},{9,8},{10,11... | collective-permute-start | bytes 442376 | tf_op jit(solution)/shard_map/ppermute | solution.py:682
  171.2 10.2 %collective-permute-start.29 = (bf16[48,1536]{1,0:T(8,128)(2,1)S(1)}, bf16[48,1536]{1,0:T(8,128)(2,1)S(1)}, u32[]{:S(2)}, u32[]{:S(2)}) collective-permute-start(bf16[48,1536]{1,0:T(8,128)(2,1)S(1)} %get-tuple-element.175), channel_id=1, source_target_pairs={{0,8},{1,9},{2,10},{3,11},{4,12},{5,13},{6,14},{7,15},{8,0},{9,1},... | collective-permute-start | bytes 442376 | tf_op jit(solution)/shard_map/ppermute | solution.py:682

commit v3 on v2

--- a/solution.py
+++ b/solution.py
@@ -785,7 +785,8 @@
     before = [up_sums[1], gate_came]
     first_send, first_keep, small, *second_pair = attn_product(kept[:3] + [nearby], rights, halves, share, before)
     held, first_passed, small = first_sum(first_keep, after(exchange(first_send, 4), up_came), small)
-    gate_came, up_came = after((gate_came, up_came), first_passed)
+    second_sums = sum_once(second_pair, first_passed)
+    gate_came, up_came = after((gate_came, up_came), second_sums[1])
     gate_tile = (gate_sums[0] + jnp.concatenate([gate_came, up_came[block:]], axis=0).astype(floating)).astype(bfloat)
     up_tile = (up_sums[0] + up_came[:block].astype(floating)).astype(bfloat)
     quarter = index & 3
@@ -796,7 +797,6 @@
     ]
     pieces = swapped(pieces)
     grad_out, grad_query, small = first_end(held, exchange(first_passed, 8), small)
-    second_sums = sum_once(second_pair, first_passed)
     grad_gate, grad_up = assemble(list(after(pieces, second_sums[1], small)))
     return [grad_down[None], grad_gate, grad_up, grad_out, grad_query], (second_sums[0], exchange(second_sums[1], 8)), small
 

time: 182 us -> 188 us (1.033)
  waiting for transfers between devices: 90.5 us -> 94.6 us
    ppermute x31, waiting for transfers between devices: 73.6 us -> 77.6 us  [exchange(): lax.ppermute(value, 'dp', [(source, source ^ flips) for source in range(c...]
  transfers between devices with their start and end apart: 33 -> 33, of which waited for: 17 -> 16; matrix products, arithmetic and copies ran while one was open for 3% -> 4% of each run, Pallas kernels for 17% -> 17%
where the time goes in v3:
time: 188 us
  waiting for transfers between devices  94.6 us (50%)
  Pallas kernels  54 us (29%)
  starting transfers between devices  30.4 us (16%)
  other arithmetic  4.54 us (2%)
  local copies, waits for them, and re-layouts  2.91 us (2%)
    ppermute x31, waiting for transfers between devices, exchange(): lax.ppermute(value, 'dp', [(source, source ^ flips) for source in range(c...  77.6 us
    ppermute x31, starting transfers between devices, exchange(): lax.ppermute(value, 'dp', [(source, source ^ flips) for source in range(c...  25.9 us
    ppermute x2, waiting for transfers between devices, local(): message = lax.ppermute(message, 'section', [(0, 1), (1, 0)])  17 us
    pallas_call x1, Pallas kernels, forward_lite(): pl.pallas_call(forward_lite_kernel, out_shape=[jax.ShapeDtypeStruct((toke...  11.4 us
    pallas_call x1, Pallas kernels, relay_backward(): pl.pallas_call(relay_kernel, out_shape=shape((tokens, 2 * width), bfloat)...  11.2 us
    pallas_call x1, Pallas kernels, forward(): pl.pallas_call(lambda *refs: forward_kernel(fast, *refs), out_shape=[shap...  9.1 us
    pallas_call x1, Pallas kernels, attn_backward(): pl.pallas_call(attn_kernel, out_shape=[shape((1, tokens, 2 * width), bflo...  8.26 us
    pallas_call x1, Pallas kernels, ffn_backward(): pl.pallas_call(ffn_kernel, out_shape=[shape((tokens, width), bfloat)] * 8...  5.38 us
  transfers between devices with their start and end apart: 33, of which 16 were waited for; matrix products, arithmetic and copies ran while one was open for 4% of the time, Pallas kernels for 17%

profile of v3, /device:TPU:0, one launch (start us, length us, event | category | flops | bytes accessed | tf_op | source)
XLA Modules:
  0.0 187.5 jit_solution(15991968204772000474)
XLA Ops:
  0.7 11.4 %forward_lite.1 = (bf16[192,1536]{1,0:T(8,128)(2,1)S(1)}, bf16[1,768,768]{2,1,0:T(8,128)(2,1)S(1)}, bf16[1,768,768]{2,1,0:T(8,128)(2,1)S(1)}, bf16[1,768,768]{2,...) custom-call(bf16[192,1536]{1,0:T(8,128)(2,1)} %refs_0_.1, ...), custom_call_target="tpu_custom_call" | custom-call | flops 3623878 | bytes 18874 | tf_op jit(solution)/shard_map/forward_lite/pallas_call | solution.py:202
  12.2 3.0 %collective-permute-start = (bf16[192,1536]{1,0:T(8,128)(2,1)S(1)}, bf16[192,1536]{1,0:T(8,128)(2,1)S(1)}, u32[]{:S(2)}, u32[]{:S(2)}) collective-permute-start(bf16[192,1536]{1,0:T(8,128)(2,1)S(1)} %get-tuple-element.94), channel_id=1, source_target_pairs={{0,16},{16,0},{1,17},{17,1},{2,18},{18,2},{3,19},{19,3},{4,20},{20... | collective-permute-start | bytes 1769480 | tf_op jit(solution)/shard_map/ppermute | solution.py:812
  15.2 13.3 %collective-permute-done.refs_1_ = bf16[192,1536]{1,0:T(8,128)(2,1)S(1)} collective-permute-done((bf16[192,1536]{1,0:T(8,128)(2,1)S(1)}, bf16[192,1536]{1,0:T(8,128)(2,1)S(1)}, u32[]{:S(2)}, u32[]{:S(2)}) %collective-permute-start) | collective-permute-done | bytes 589856 | tf_op jit(solution)/shard_map/ppermute | solution.py:812
  28.6 9.1 %forward_full.1 = (bf16[192,1536]{1,0:T(8,128)(2,1)S(1)}, bf16[1,192,1536]{2,1,0:T(8,128)(2,1)}, bf16[192,768]{1,0:T(8,128)(2,1)S(1)}, bf16[192,768]{1,0:T(8,128...) custom-call(bf16[192,1536]{1,0:T(8,128)(2,1)S(1)} %copy-done.2, ...), custom_call_target="tpu_custom_call" | custom-call | flops 3623878 | bytes 18874 | tf_op jit(solution)/shard_map/forward_full/pallas_call | solution.py:307
  37.7 1.8 collective-permute-start.3
  39.4 11.2 %backward_relay.1 = bf16[192,1536]{1,0:T(8,128)(2,1)S(1)} custom-call(bf16[192,1536]{1,0:T(8,128)(2,1)S(1)} %copy-done, s32[2]{0:T(128)S(1)} %copy-done.10, f32[1,2]{1,0:T(1,128)S(1)} %copy-done.7, f32[1,2,2]{2,1,0:T(2,128)S(1)} %copy-done.8, f32[1,768]{1,0:T(1,128)S(1)} %copy-done.5, f32[1,768]{1,0:T(1,128)S(1)} %copy-done.6, ...), custom_call_target="tpu_custom_call" | custom-call | flops 3623878 | bytes 18874 | tf_op jit(solution)/shard_map/backward_relay/pallas_call | solution.py:526
  50.7 1.6 collective-permute-start.1
  52.3 10.2 %collective-permute-done.4.refs_6_.refs_3_ = bf16[192,768]{1,0:T(8,128)(2,1)S(1)} collective-permute-done((bf16[192,768]{1,0:T(8,128)(2,1)S(1)}, bf16[192,768]{1,0:T(8,128)(2,1)S(1)}, u32[]{:S(2)}, u32[]{:S(2)}) %collective-permute-start.4) | collective-permute-done | bytes 294944 | tf_op jit(solution)/shard_map/ppermute | solution.py:682
  62.5 3.7 %collective-permute-done.1.refs_0_ = bf16[192,1536]{1,0:T(8,128)(2,1)S(1)} collective-permute-done((bf16[192,1536]{1,0:T(8,128)(2,1)S(1)}, bf16[192,1536]{1,0:T(8,128)(2,1)S(1)}, u32[]{:S(2)}, u32[]{:S(2)}) %collective-permute-start.1) | collective-permute-done | bytes 589856 | tf_op jit(solution)/shard_map/ppermute | solution.py:821
  66.2 0.8 backward_start.1
  67.4 5.4 %backward_ffn.1 = (bf16[192,768]{1,0:T(8,128)(2,1)S(1)}, bf16[192,768]{1,0:T(8,128)(2,1)S(1)}, bf16[192,768]{1,0:T(8,128)(2,1)S(1)}, bf16[192,768]{1,0:T(8,128)(...) custom-call(bf16[192,1536]{1,0:T(8,128)(2,1)S(1)} %get-tuple-element, ...), custom_call_target="tpu_custom_call" | custom-call | flops 2717908 | bytes 14155 | tf_op jit(solution)/shard_map/backward_ffn/pallas_call | solution.py:400
  72.8 2.6 %collective-permute-done.6.refs_6_ = bf16[192,768]{1,0:T(8,128)(2,1)S(1)} collective-permute-done((bf16[192,768]{1,0:T(8,128)(2,1)S(1)}, bf16[192,768]{1,0:T(8,128)(2,1)S(1)}, u32[]{:S(2)}, u32[]{:S(2)}) %collective-permute-start.6) | collective-permute-done | bytes 294944 | tf_op jit(solution)/shard_map/ppermute | solution.py:682
  75.4 1.6 collective-permute-done.7.refs_7_
  77.0 1.2 product_down.1
  78.2 1.6 collective-permute-start.13
  81.0 0.9 collective-permute-start.12
  81.9 8.3 %backward_attn.1 = (bf16[1,192,1536]{2,1,0:T(8,128)(2,1)}, bf16[208,3072]{1,0:T(8,128)(2,1)S(1)}, f32[8,768]{1,0:T(8,128)}) custom-call(bf16[192,768]{1,0:T(8,128)(2,1)S(1)} %get-tuple-element.116.datt_ref, bf16[192,768]{1,0:T(8,128)(2,1)S(1)} %get-tuple-element.106.q_ref, bf16[192,768]{1,0:T(8,128)(2,1)S(1)} %get-tuple-element.107.k_ref, ...), custom_call_target="tpu_custom_call" | custom-call | flops 1132462 | bytes 4718 | tf_op jit(solution)/shard_map/backward_attn/pallas_call | solution.py:480
  90.2 3.5 %collective-permute-done.13 = bf16[2,192,768]{2,1,0:T(8,128)(2,1)S(1)} collective-permute-done((bf16[2,192,768]{2,1,0:T(8,128)(2,1)S(1)}, bf16[2,192,768]{2,1,0:T(8,128)(2,1)S(1)}, u32[]{:S(2)}, u32[]{:S(2)}) %collective-permute-start.13) | collective-permute-done | bytes 589856 | tf_op jit(solution)/shard_map/ppermute | solution.py:682
  94.2 1.5 collective-permute-start.16
  95.7 1.2 product_gate.1
  96.9 1.6 collective-permute-start.19
  99.0 2.6 %collective-permute-start.21 = (bf16[192,768]{1,0:T(8,128)(2,1)S(1)}, bf16[192,768]{1,0:T(8,128)(2,1)S(1)}, u32[]{:S(2)}, u32[]{:S(2)}) collective-permute-start(bf16[192,768]{1,0:T(8,128)(2,1)S(1)} %fusion.4.refs_9_), channel_id=1, source_target_pairs={{0,8},{1,9},{2,10},{3,11},{4,12},{5,13},{6,14},{7,15},{8,0},{9,1},... | collective-permute-start | bytes 884744 | tf_op jit(solution)/shard_map/ppermute | solution.py:682
  101.6 2.0 %collective-permute-done.15.refs_6_ = bf16[192,768]{1,0:T(8,128)(2,1)S(1)} collective-permute-done((bf16[192,768]{1,0:T(8,128)(2,1)S(1)}, bf16[192,768]{1,0:T(8,128)(2,1)S(1)}, u32[]{:S(2)}, u32[]{:S(2)}) %collective-permute-start.15) | collective-permute-done | bytes 294944 | tf_op jit(solution)/shard_map/ppermute | solution.py:682
  103.6 5.5 %collective-permute-done.16.refs_7_ = bf16[192,768]{1,0:T(8,128)(2,1)S(1)} collective-permute-done((bf16[192,768]{1,0:T(8,128)(2,1)S(1)}, bf16[192,768]{1,0:T(8,128)(2,1)S(1)}, u32[]{:S(2)}, u32[]{:S(2)}) %collective-permute-start.16) | collective-permute-done | bytes 294944 | tf_op jit(solution)/shard_map/ppermute | solution.py:682
  109.5 3.6 %collective-permute-done.19 = bf16[192,768]{1,0:T(8,128)(2,1)S(1)} collective-permute-done((bf16[192,768]{1,0:T(8,128)(2,1)S(1)}, bf16[192,768]{1,0:T(8,128)(2,1)S(1)}, u32[]{:S(2)}, u32[]{:S(2)}) %collective-permute-start.19) | collective-permute-done | bytes 294944 | tf_op jit(solution)/shard_map/ppermute | solution.py:682
  113.1 5.7 %collective-permute-done.20 = bf16[192,768]{1,0:T(8,128)(2,1)S(1)} collective-permute-done((bf16[192,768]{1,0:T(8,128)(2,1)S(1)}, bf16[192,768]{1,0:T(8,128)(2,1)S(1)}, u32[]{:S(2)}, u32[]{:S(2)}) %collective-permute-start.20) | collective-permute-done | bytes 294944 | tf_op jit(solution)/shard_map/ppermute | solution.py:682
  119.0 1.2 product_up.1
  120.2 2.7 %collective-permute-start.22 = (bf16[2,192,768]{2,1,0:T(8,128)(2,1)S(1)}, bf16[2,192,768]{2,1,0:T(8,128)(2,1)S(1)}, u32[]{:S(2)}, u32[]{:S(2)}) collective-permute-start(bf16[2,192,768]{2,1,0:T(8,128)(2,1)S(1)} %get-tuple-element.150), channel_id=1, source_target_pairs={{0,4},{1,5},{2,6},{3,7},{4,0},{5,1},{6,2},{7,3},{8,12},{9,13},{10,... | collective-permute-start | bytes 1769480 | tf_op jit(solution)/shard_map/ppermute | solution.py:682
  122.9 1.6 collective-permute-start.23
  124.6 16.0 %collective-permute-done.22 = bf16[2,192,768]{2,1,0:T(8,128)(2,1)S(1)} collective-permute-done((bf16[2,192,768]{2,1,0:T(8,128)(2,1)S(1)}, bf16[2,192,768]{2,1,0:T(8,128)(2,1)S(1)}, u32[]{:S(2)}, u32[]{:S(2)}) %collective-permute-start.22) | collective-permute-done | bytes 589856 | tf_op jit(solution)/shard_map/ppermute | solution.py:682
  140.7 0.8 pad_maximum_fusion
  141.5 2.5 %collective-permute-start.26 = (bf16[240,768]{1,0:T(8,128)(2,1)}, bf16[240,768]{1,0:T(8,128)(2,1)}, u32[]{:S(2)}, u32[]{:S(2)}) collective-permute-start(bf16[240,768]{1,0:T(8,128)(2,1)} %pad_maximum_fusion), channel_id=1, source_target_pairs={{0,8},{1,9},{2,10},{3,11},{4,12},{5,13},{6,14},{7,15},{8,0},{9,1},... | collective-permute-start | bytes 1105928 | tf_op jit(solution)/shard_map/ppermute | solution.py:682
  144.0 2.3 %product_attn.1 = (bf16[112,1536]{1,0:T(8,128)(2,1)S(1)}, f32[4,48,1536]{2,1,0:T(8,128)S(1)}, f32[8,768]{1,0:T(8,128)S(1)}, bf16[2,48,1536]{2,1,0:T(8,128)(2,1)}, f32[4,48,1536]{2,1,0:T(8,128)S(1)}) custom-call(bf16[192,1152]{1,0:T(8,128)(2,1)S(1)} %get-tuple-element.121.refs_0_, bf16[192,1920]{1,0:T(8,128)(2,1)S(1)} %collective-permute-done.2.refs_4_.refs_1_, ...), custom_call_target="tpu_custom_call" | custom-call | flops 1 | bytes 1 | tf_op jit(solution)/shard_map/product_attn/pallas_call | solution.py:598
  146.3 1.2 collective-permute-start.25
  147.5 0.8 collective-permute-start.28
  148.3 13.4 %collective-permute-done.26 = bf16[240,768]{1,0:T(8,128)(2,1)} collective-permute-done((bf16[240,768]{1,0:T(8,128)(2,1)}, bf16[240,768]{1,0:T(8,128)(2,1)}, u32[]{:S(2)}, u32[]{:S(2)}) %collective-permute-start.26) | collective-permute-done | bytes 368672 | tf_op jit(solution)/shard_map/ppermute | solution.py:682
  161.7 2.4 %collective-permute-done.25.came_ref = bf16[112,1536]{1,0:T(8,128)(2,1)S(1)} collective-permute-done((bf16[112,1536]{1,0:T(8,128)(2,1)S(1)}, bf16[112,1536]{1,0:T(8,128)(2,1)S(1)}, u32[]{:S(2)}, u32[]{:S(2)}) %collective-permute-start.25) | collective-permute-done | bytes 344096 | tf_op jit(solution)/shard_map/ppermute | solution.py:682
  164.2 1.4 collective-permute-start.27
  165.6 6.1 %collective-permute-done.28 = bf16[2,48,1536]{2,1,0:T(8,128)(2,1)} collective-permute-done((bf16[2,48,1536]{2,1,0:T(8,128)(2,1)}, bf16[2,48,1536]{2,1,0:T(8,128)(2,1)}, u32[]{:S(2)}, u32[]{:S(2)}) %collective-permute-start.28) | collective-permute-done | bytes 294944 | tf_op jit(solution)/shard_map/ppermute | solution.py:682
  171.7 1.0 fusion.6
  172.7 0.8 collective-permute-start.29
  173.5 0.9 slice.109
  174.4 1.6 fusion
  176.9 1.3 collective-permute-start.30
  178.2 0.7 first_end.1
  179.0 3.2 %collective-permute-done.32.three = bf16[48,1536]{1,0:T(8,128)(2,1)S(1)} collective-permute-done((bf16[48,1536]{1,0:T(8,128)(2,1)S(1)}, bf16[48,1536]{1,0:T(8,128)(2,1)S(1)}, u32[]{:S(2)}, u32[]{:S(2)}) %collective-permute-start.32) | collective-permute-done | bytes 147488 | tf_op jit(solution)/shard_map/ppermute | solution.py:682
  182.2 1.6 collective-permute-done.31.two
  185.1 1.1 assemble.1
  (85 shorter events, 6.9 us)
Async XLA Ops:
  0.7 27.8 %copy-start.2 = (bf16[192,1536]{1,0:T(8,128)(2,1)S(1)}, bf16[192,1536]{1,0:T(8,128)(2,1)}, u32[]{:S(2)}) copy-start(bf16[192,1536]{1,0:T(8,128)(2,1)} %refs_0_.1) | copy-start | bytes 1769476
  0.7 27.8 %copy-start.9 = (s32[2,96]{1,0:T(2,128)S(1)}, s32[2,96]{1,0:T(2,128)}, u32[]{:S(2)}) copy-start(s32[2,96]{1,0:T(2,128)} %refs_2_.2) | copy-start | bytes 2308
  0.7 27.8 %copy-start.8 = (f32[1,2,2]{2,1,0:T(2,128)S(1)}, f32[1,2,2]{2,1,0:T(2,128)}, u32[]{:S(2)}) copy-start(f32[1,2,2]{2,1,0:T(2,128)} %mix_ref.3) | copy-start | bytes 52
  0.7 27.8 %copy-start.7 = (f32[1,2]{1,0:T(1,128)S(1)}, f32[1,2]{1,0:T(1,128)}, u32[]{:S(2)}) copy-start(f32[1,2]{1,0:T(1,128)} %cor_ref.5) | copy-start | bytes 28
  0.7 27.8 %copy-start.6 = (f32[1,768]{1,0:T(1,128)S(1)}, f32[1,768]{1,0:T(1,128)}, u32[]{:S(2)}) copy-start(f32[1,768]{1,0:T(1,128)} %ga_ref.3) | copy-start | bytes 9220
  0.7 27.8 %copy-start.5 = (f32[1,768]{1,0:T(1,128)S(1)}, f32[1,768]{1,0:T(1,128)}, u32[]{:S(2)}) copy-start(f32[1,768]{1,0:T(1,128)} %gf_ref.3) | copy-start | bytes 9220
  12.2 16.3 %collective-permute-start = (bf16[192,1536]{1,0:T(8,128)(2,1)S(1)}, bf16[192,1536]{1,0:T(8,128)(2,1)S(1)}, u32[]{:S(2)}, u32[]{:S(2)}) collective-permute-start(bf16[192,1536]{1,0:T(8,128)(2,1)S(1)} %get-tuple-element.94), channel_id=1, source_target_pairs={{0,16},{16,0},{1,17},{17,1},{2,18},{18,2},{3,19},{19,3},{4,20},{20... | collective-permute-start | bytes 1769480 | tf_op jit(solution)/shard_map/ppermute | solution.py:812
  28.5 10.9 %copy-start = (bf16[192,1536]{1,0:T(8,128)(2,1)S(1)}, bf16[192,1536]{1,0:T(8,128)(2,1)}, u32[]{:S(2)}) copy-start(bf16[192,1536]{1,0:T(8,128)(2,1)} %refs_1_.1) | copy-start | bytes 1769476
  28.5 10.9 %copy-start.10 = (s32[2]{0:T(128)S(1)}, s32[2]{0:T(128)}, u32[]{:S(2)}) copy-start(s32[2]{0:T(128)} %refs_2_.3) | copy-start | bytes 28
  37.7 28.6 %collective-permute-start.2 = (bf16[192,1920]{1,0:T(8,128)(2,1)S(1)}, bf16[192,1920]{1,0:T(8,128)(2,1)S(1)}, u32[]{:S(2)}, u32[]{:S(2)}) collective-permute-start(bf16[192,1920]{1,0:T(8,128)(2,1)S(1)} %get-tuple-element.111), channel_id=1, source_target_pairs={{0,1},{1,0},{2,3},{3,2},{4,5},{5,4},{6,7},{7,6},{8,9},{9,8},{10,11... | collective-permute-start | bytes 2211848 | tf_op jit(solution)/shard_map/ppermute | solution.py:682
  37.7 28.6 %collective-permute-start.3 = (bf16[192,1920]{1,0:T(8,128)(2,1)S(1)}, bf16[192,1920]{1,0:T(8,128)(2,1)S(1)}, u32[]{:S(2)}, u32[]{:S(2)}) collective-permute-start(bf16[192,1920]{1,0:T(8,128)(2,1)S(1)} %get-tuple-element.112), channel_id=1, source_target_pairs={{0,2},{1,3},{2,0},{3,1},{4,6},{5,7},{6,4},{7,5},{8,10},{9,11},{10,... | collective-permute-start | bytes 2211848 | tf_op jit(solution)/shard_map/ppermute | solution.py:682
  50.7 15.5 %collective-permute-start.1 = (bf16[192,1536]{1,0:T(8,128)(2,1)S(1)}, bf16[192,1536]{1,0:T(8,128)(2,1)S(1)}, u32[]{:S(2)}, u32[]{:S(2)}) collective-permute-start(bf16[192,1536]{1,0:T(8,128)(2,1)S(1)} %backward_relay.1), channel_id=1, source_target_pairs={{0,16},{16,0},{1,17},{17,1},{2,18},{18,2},{3,19},{19,3},{4,20},{20... | collective-permute-start | bytes 1769480 | tf_op jit(solution)/shard_map/ppermute | solution.py:821
  52.2 10.3 %collective-permute-start.4 = (bf16[192,768]{1,0:T(8,128)(2,1)S(1)}, bf16[192,768]{1,0:T(8,128)(2,1)S(1)}, u32[]{:S(2)}, u32[]{:S(2)}) collective-permute-start(bf16[192,768]{1,0:T(8,128)(2,1)S(1)} %get-tuple-element.113), channel_id=1, source_target_pairs={{0,3},{1,2},{2,1},{3,0},{4,7},{5,6},{6,5},{7,4},{8,11},{9,10},{10,... | collective-permute-start | bytes 884744 | tf_op jit(solution)/shard_map/ppermute | solution.py:682
  67.0 8.4 %collective-permute-start.6 = (bf16[192,768]{1,0:T(8,128)(2,1)S(1)}, bf16[192,768]{1,0:T(8,128)(2,1)S(1)}, u32[]{:S(2)}, u32[]{:S(2)}) collective-permute-start(bf16[192,768]{1,0:T(8,128)(2,1)S(1)} %get-tuple-element.115.low_ref.refs_4_), channel_id=1, source_target_pairs={{0,2},{1,3},{2,0},{3,1},{4,6},{5,7},{6,4},{7,5},{8,10},{9,11},{10,... | collective-permute-start | bytes 884744 | tf_op jit(solution)/shard_map/ppermute | solution.py:682
  67.4 8.0 %collective-permute-start.5 = (bf16[192,768]{1,0:T(8,128)(2,1)S(1)}, bf16[192,768]{1,0:T(8,128)(2,1)S(1)}, u32[]{:S(2)}, u32[]{:S(2)}) collective-permute-start(bf16[192,768]{1,0:T(8,128)(2,1)S(1)} %get-tuple-element.115.low_ref.refs_4_), channel_id=1, source_target_pairs={{0,1},{1,0},{2,3},{3,2},{4,5},{5,4},{6,7},{7,6},{8,9},{9,8},{10,11... | collective-permute-start | bytes 884744 | tf_op jit(solution)/shard_map/ppermute | solution.py:682
  75.4 1.6 collective-permute-start.7
  78.2 15.4 %collective-permute-start.13 = (bf16[2,192,768]{2,1,0:T(8,128)(2,1)S(1)}, bf16[2,192,768]{2,1,0:T(8,128)(2,1)S(1)}, u32[]{:S(2)}, u32[]{:S(2)}) collective-permute-start(bf16[2,192,768]{2,1,0:T(8,128)(2,1)S(1)} %get-tuple-element.124.before), channel_id=1, source_target_pairs={{0,4},{1,5},{2,6},{3,7},{4,0},{5,1},{6,2},{7,3},{8,12},{9,13},{10,... | collective-permute-start | bytes 1769480 | tf_op jit(solution)/shard_map/ppermute | solution.py:682
  79.9 13.9 %collective-permute-start.9 = (bf16[192,768]{1,0:T(8,128)(2,1)S(1)}, bf16[192,768]{1,0:T(8,128)(2,1)S(1)}, u32[]{:S(2)}, u32[]{:S(2)}) collective-permute-start(bf16[192,768]{1,0:T(8,128)(2,1)S(1)} %slice.117.refs_2_), channel_id=1, source_target_pairs={{0,1},{1,0},{2,3},{3,2},{4,5},{5,4},{6,7},{7,6},{8,9},{9,8},{10,11... | collective-permute-start | bytes 884744 | tf_op jit(solution)/shard_map/ppermute | solution.py:682
  80.0 14.2 %collective-permute-start.10 = (bf16[192,768]{1,0:T(8,128)(2,1)S(1)}, bf16[192,768]{1,0:T(8,128)(2,1)S(1)}, u32[]{:S(2)}, u32[]{:S(2)}) collective-permute-start(bf16[192,768]{1,0:T(8,128)(2,1)S(1)} %get-tuple-element.135), channel_id=1, source_target_pairs={{0,1},{1,0},{2,3},{3,2},{4,5},{5,4},{6,7},{7,6},{8,9},{9,8},{10,11... | collective-permute-start | bytes 884744 | tf_op jit(solution)/shard_map/ppermute | solution.py:682
  80.5 15.2 %collective-permute-start.11 = (bf16[192,768]{1,0:T(8,128)(2,1)S(1)}, bf16[192,768]{1,0:T(8,128)(2,1)S(1)}, u32[]{:S(2)}, u32[]{:S(2)}) collective-permute-start(bf16[192,768]{1,0:T(8,128)(2,1)S(1)} %get-tuple-element.136), channel_id=1, source_target_pairs={{0,2},{1,3},{2,0},{3,1},{4,6},{5,7},{6,4},{7,5},{8,10},{9,11},{10,... | collective-permute-start | bytes 884744 | tf_op jit(solution)/shard_map/ppermute | solution.py:682
  81.0 14.7 %collective-permute-start.12 = (bf16[192,768]{1,0:T(8,128)(2,1)S(1)}, bf16[192,768]{1,0:T(8,128)(2,1)S(1)}, u32[]{:S(2)}, u32[]{:S(2)}) collective-permute-start(bf16[192,768]{1,0:T(8,128)(2,1)S(1)} %get-tuple-element.137), channel_id=1, source_target_pairs={{0,3},{1,2},{2,1},{3,0},{4,7},{5,6},{6,5},{7,4},{8,11},{9,10},{10,... | collective-permute-start | bytes 884744 | tf_op jit(solution)/shard_map/ppermute | solution.py:682
  93.7 5.3 %collective-permute-start.14 = (bf16[192,768]{1,0:T(8,128)(2,1)S(1)}, bf16[192,768]{1,0:T(8,128)(2,1)S(1)}, u32[]{:S(2)}, u32[]{:S(2)}) collective-permute-start(bf16[192,768]{1,0:T(8,128)(2,1)S(1)} %get-tuple-element.141), channel_id=1, source_target_pairs={{0,1},{1,0},{2,3},{3,2},{4,5},{5,4},{6,7},{7,6},{8,9},{9,8},{10,11... | collective-permute-start | bytes 884744 | tf_op jit(solution)/shard_map/ppermute | solution.py:682
  93.8 9.9 %collective-permute-start.15 = (bf16[192,768]{1,0:T(8,128)(2,1)S(1)}, bf16[192,768]{1,0:T(8,128)(2,1)S(1)}, u32[]{:S(2)}, u32[]{:S(2)}) collective-permute-start(bf16[192,768]{1,0:T(8,128)(2,1)S(1)} %get-tuple-element.142), channel_id=1, source_target_pairs={{0,2},{1,3},{2,0},{3,1},{4,6},{5,7},{6,4},{7,5},{8,10},{9,11},{10,... | collective-permute-start | bytes 884744 | tf_op jit(solution)/shard_map/ppermute | solution.py:682
  94.2 15.0 %collective-permute-start.16 = (bf16[192,768]{1,0:T(8,128)(2,1)S(1)}, bf16[192,768]{1,0:T(8,128)(2,1)S(1)}, u32[]{:S(2)}, u32[]{:S(2)}) collective-permute-start(bf16[192,768]{1,0:T(8,128)(2,1)S(1)} %get-tuple-element.143), channel_id=1, source_target_pairs={{0,3},{1,2},{2,1},{3,0},{4,7},{5,6},{6,5},{7,4},{8,11},{9,10},{10,... | collective-permute-start | bytes 884744 | tf_op jit(solution)/shard_map/ppermute | solution.py:682
  96.9 22.0 %copy-start.3 = (f32[4,192,768]{2,1,0:T(8,128)}, f32[4,192,768]{2,1,0:T(8,128)S(1)}, u32[]{:S(2)}) copy-start(f32[4,192,768]{2,1,0:T(8,128)S(1)} %get-tuple-element.146) | copy-start | bytes 7077892
  96.9 16.2 %collective-permute-start.19 = (bf16[192,768]{1,0:T(8,128)(2,1)S(1)}, bf16[192,768]{1,0:T(8,128)(2,1)S(1)}, u32[]{:S(2)}, u32[]{:S(2)}) collective-permute-start(bf16[192,768]{1,0:T(8,128)(2,1)S(1)} %get-tuple-element.140), channel_id=1, source_target_pairs={{0,4},{1,5},{2,6},{3,7},{4,0},{5,1},{6,2},{7,3},{8,12},{9,13},{10,... | collective-permute-start | bytes 884744 | tf_op jit(solution)/shard_map/ppermute | solution.py:682
  98.5 20.3 %collective-permute-start.20 = (bf16[192,768]{1,0:T(8,128)(2,1)S(1)}, bf16[192,768]{1,0:T(8,128)(2,1)S(1)}, u32[]{:S(2)}, u32[]{:S(2)}) collective-permute-start(bf16[192,768]{1,0:T(8,128)(2,1)S(1)} %get-tuple-element.147), channel_id=1, source_target_pairs={{0,4},{1,5},{2,6},{3,7},{4,0},{5,1},{6,2},{7,3},{8,12},{9,13},{10,... | collective-permute-start | bytes 884744 | tf_op jit(solution)/shard_map/ppermute | solution.py:682
  99.0 19.8 %collective-permute-start.21 = (bf16[192,768]{1,0:T(8,128)(2,1)S(1)}, bf16[192,768]{1,0:T(8,128)(2,1)S(1)}, u32[]{:S(2)}, u32[]{:S(2)}) collective-permute-start(bf16[192,768]{1,0:T(8,128)(2,1)S(1)} %fusion.4.refs_9_), channel_id=1, source_target_pairs={{0,8},{1,9},{2,10},{3,11},{4,12},{5,13},{6,14},{7,15},{8,0},{9,1},... | collective-permute-start | bytes 884744 | tf_op jit(solution)/shard_map/ppermute | solution.py:682
  103.6 15.4 %collective-permute-start.8 = (bf16[192,384]{1,0:T(8,128)(2,1)S(1)}, bf16[192,384]{1,0:T(8,128)(2,1)S(1)}, u32[]{:S(2)}, u32[]{:S(2)}) collective-permute-start(bf16[192,384]{1,0:T(8,128)(2,1)S(1)} %get-tuple-element.132), channel_id=1, source_target_pairs={{0,3},{1,2},{2,1},{3,0},{4,7},{5,6},{6,5},{7,4},{8,11},{9,10},{10,... | collective-permute-start | bytes 442376 | tf_op jit(solution)/shard_map/ppermute | solution.py:682
  109.2 31.5 %collective-permute-start.18 = (bf16[208,3072]{1,0:T(8,128)(2,1)S(1)}, bf16[208,3072]{1,0:T(8,128)(2,1)S(1)}, u32[]{:S(2)}, u32[]{:S(2)}) collective-permute-start(bf16[208,3072]{1,0:T(8,128)(2,1)S(1)} %get-tuple-element.144.refs_8_.refs_4_), channel_id=1, source_target_pairs={{0,2},{1,3},{2,0},{3,1},{4,6},{5,7},{6,4},{7,5},{8,10},{9,11},{10,... | collective-permute-start | bytes 3833864 | tf_op jit(solution)/shard_map/ppermute | solution.py:682
  113.1 7.1 %copy-start.13 = (bf16[192,768]{1,0:T(8,128)(2,1)}, bf16[192,768]{1,0:T(8,128)(2,1)S(1)}, u32[]{:S(2)}) copy-start(bf16[192,768]{1,0:T(8,128)(2,1)S(1)} %collective-permute-done.19) | copy-start | bytes 884740
  118.9 4.0 %copy-start.1 = (f32[192,768]{1,0:T(8,128)}, f32[192,768]{1,0:T(8,128)S(1)}, u32[]{:S(2)}) copy-start(f32[192,768]{1,0:T(8,128)S(1)} %bitcast_add_fusion.2.refs_9_) | copy-start | bytes 1769476
  120.2 23.8 %copy-start.4 = (f32[4,192,768]{2,1,0:T(8,128)}, f32[4,192,768]{2,1,0:T(8,128)S(1)}, u32[]{:S(2)}) copy-start(f32[4,192,768]{2,1,0:T(8,128)S(1)} %get-tuple-element.149) | copy-start | bytes 7077892
  120.2 20.4 %collective-permute-start.22 = (bf16[2,192,768]{2,1,0:T(8,128)(2,1)S(1)}, bf16[2,192,768]{2,1,0:T(8,128)(2,1)S(1)}, u32[]{:S(2)}, u32[]{:S(2)}) collective-permute-start(bf16[2,192,768]{2,1,0:T(8,128)(2,1)S(1)} %get-tuple-element.150), channel_id=1, source_target_pairs={{0,4},{1,5},{2,6},{3,7},{4,0},{5,1},{6,2},{7,3},{8,12},{9,13},{10,... | collective-permute-start | bytes 1769480 | tf_op jit(solution)/shard_map/ppermute | solution.py:682
  122.9 21.1 %collective-permute-start.17 = (bf16[208,3072]{1,0:T(8,128)(2,1)S(1)}, bf16[208,3072]{1,0:T(8,128)(2,1)S(1)}, u32[]{:S(2)}, u32[]{:S(2)}) collective-permute-start(bf16[208,3072]{1,0:T(8,128)(2,1)S(1)} %get-tuple-element.144.refs_8_.refs_4_), channel_id=1, source_target_pairs={{0,1},{1,0},{2,3},{3,2},{4,5},{5,4},{6,7},{7,6},{8,9},{9,8},{10,11... | collective-permute-start | bytes 3833864 | tf_op jit(solution)/shard_map/ppermute | solution.py:682
  122.9 17.7 %collective-permute-start.23 = (bf16[144,768]{1,0:T(8,128)(2,1)S(1)}, bf16[144,768]{1,0:T(8,128)(2,1)S(1)}, u32[]{:S(2)}, u32[]{:S(2)}) collective-permute-start(bf16[144,768]{1,0:T(8,128)(2,1)S(1)} %slice.119), channel_id=1, source_target_pairs={{0,8},{1,9},{2,10},{3,11},{4,12},{5,13},{6,14},{7,15},{8,0},{9,1},... | collective-permute-start | bytes 663560 | tf_op jit(solution)/shard_map/ppermute | solution.py:682
  140.6 5.7 %copy-start.11 = (bf16[2,192,768]{2,1,0:T(8,128)(2,1)}, bf16[2,192,768]{2,1,0:T(8,128)(2,1)S(1)}, u32[]{:S(2)}) copy-start(bf16[2,192,768]{2,1,0:T(8,128)(2,1)S(1)} %collective-permute-done.22) | copy-start | bytes 1769476
  140.7 3.4 %collective-permute-start.24 = (bf16[208,3072]{1,0:T(8,128)(2,1)S(1)}, bf16[208,3072]{1,0:T(8,128)(2,1)S(1)}, u32[]{:S(2)}, u32[]{:S(2)}) collective-permute-start(bf16[208,3072]{1,0:T(8,128)(2,1)S(1)} %collective-permute-done.18.refs_6_), channel_id=1, source_target_pairs={{0,1},{1,0},{2,3},{3,2},{4,5},{5,4},{6,7},{7,6},{8,9},{9,8},{10,11... | collective-permute-start | bytes 3833864 | tf_op jit(solution)/shard_map/ppermute | solution.py:682
  141.5 20.2 %collective-permute-start.26 = (bf16[240,768]{1,0:T(8,128)(2,1)}, bf16[240,768]{1,0:T(8,128)(2,1)}, u32[]{:S(2)}, u32[]{:S(2)}) collective-permute-start(bf16[240,768]{1,0:T(8,128)(2,1)} %pad_maximum_fusion), channel_id=1, source_target_pairs={{0,8},{1,9},{2,10},{3,11},{4,12},{5,13},{6,14},{7,15},{8,0},{9,1},... | collective-permute-start | bytes 1105928 | tf_op jit(solution)/shard_map/ppermute | solution.py:682
  146.3 17.8 %collective-permute-start.25 = (bf16[112,1536]{1,0:T(8,128)(2,1)S(1)}, bf16[112,1536]{1,0:T(8,128)(2,1)S(1)}, u32[]{:S(2)}, u32[]{:S(2)}) collective-permute-start(bf16[112,1536]{1,0:T(8,128)(2,1)S(1)} %get-tuple-element.153), channel_id=1, source_target_pairs={{0,4},{1,5},{2,6},{3,7},{4,0},{5,1},{6,2},{7,3},{8,12},{9,13},{10,... | collective-permute-start | bytes 1032200 | tf_op jit(solution)/shard_map/ppermute | solution.py:682
  147.5 24.2 %collective-permute-start.28 = (bf16[2,48,1536]{2,1,0:T(8,128)(2,1)}, bf16[2,48,1536]{2,1,0:T(8,128)(2,1)}, u32[]{:S(2)}, u32[]{:S(2)}) collective-permute-start(bf16[2,48,1536]{2,1,0:T(8,128)(2,1)} %get-tuple-element.162), channel_id=1, source_target_pairs={{0,4},{1,5},{2,6},{3,7},{4,0},{5,1},{6,2},{7,3},{8,12},{9,13},{10,... | collective-permute-start | bytes 884744 | tf_op jit(solution)/shard_map/ppermute | solution.py:682
  148.3 26.1 %copy-start.12 = (bf16[2,192,768]{2,1,0:T(8,128)(2,1)S(1)}, bf16[2,192,768]{2,1,0:T(8,128)(2,1)}, u32[]{:S(2)}) copy-start(bf16[2,192,768]{2,1,0:T(8,128)(2,1)} %copy-done.11) | copy-start | bytes 1769476
  148.3 26.1 %copy-start.14 = (bf16[192,768]{1,0:T(8,128)(2,1)S(1)}, bf16[192,768]{1,0:T(8,128)(2,1)}, u32[]{:S(2)}) copy-start(bf16[192,768]{1,0:T(8,128)(2,1)} %copy-done.13) | copy-start | bytes 884740
  164.2 14.0 %collective-permute-start.27 = (bf16[64,1536]{1,0:T(8,128)(2,1)S(1)}, bf16[64,1536]{1,0:T(8,128)(2,1)S(1)}, u32[]{:S(2)}, u32[]{:S(2)}) collective-permute-start(bf16[64,1536]{1,0:T(8,128)(2,1)S(1)} %get-tuple-element.157), channel_id=1, source_target_pairs={{0,8},{1,9},{2,10},{3,11},{4,12},{5,13},{6,14},{7,15},{8,0},{9,1},... | collective-permute-start | bytes 589832 | tf_op jit(solution)/shard_map/ppermute | solution.py:682
  172.7 14.0 %collective-permute-start.29 = (bf16[48,1536]{1,0:T(8,128)(2,1)S(1)}, bf16[48,1536]{1,0:T(8,128)(2,1)S(1)}, u32[]{:S(2)}, u32[]{:S(2)}) collective-permute-start(bf16[48,1536]{1,0:T(8,128)(2,1)S(1)} %get-tuple-element.175), channel_id=1, source_target_pairs={{0,8},{1,9},{2,10},{3,11},{4,12},{5,13},{6,14},{7,15},{8,0},{9,1},... | collective-permute-start | bytes 442376 | tf_op jit(solution)/shard_map/ppermute | solution.py:682
  176.1 6.2 %collective-permute-start.32 = (bf16[48,1536]{1,0:T(8,128)(2,1)S(1)}, bf16[48,1536]{1,0:T(8,128)(2,1)S(1)}, u32[]{:S(2)}, u32[]{:S(2)}) collective-permute-start(bf16[48,1536]{1,0:T(8,128)(2,1)S(1)} %pad_maximum_fusion.4), channel_id=1, source_target_pairs={{0,3},{1,2},{2,1},{3,0},{4,7},{5,6},{6,5},{7,4},{8,11},{9,10},{10,... | collective-permute-start | bytes 442376 | tf_op jit(solution)/shard_map/ppermute | solution.py:682
  176.2 7.7 %collective-permute-start.31 = (bf16[48,1536]{1,0:T(8,128)(2,1)S(1)}, bf16[48,1536]{1,0:T(8,128)(2,1)S(1)}, u32[]{:S(2)}, u32[]{:S(2)}) collective-permute-start(bf16[48,1536]{1,0:T(8,128)(2,1)S(1)} %pad_maximum_fusion.3), channel_id=1, source_target_pairs={{0,2},{1,3},{2,0},{3,1},{4,6},{5,7},{6,4},{7,5},{8,10},{9,11},{10,... | collective-permute-start | bytes 442376 | tf_op jit(solution)/shard_map/ppermute | solution.py:682
  176.9 7.0 %collective-permute-start.30 = (bf16[48,1536]{1,0:T(8,128)(2,1)S(1)}, bf16[48,1536]{1,0:T(8,128)(2,1)S(1)}, u32[]{:S(2)}, u32[]{:S(2)}) collective-permute-start(bf16[48,1536]{1,0:T(8,128)(2,1)S(1)} %pad_maximum_fusion.2), channel_id=1, source_target_pairs={{0,1},{1,0},{2,3},{3,2},{4,5},{5,4},{6,7},{7,6},{8,9},{9,8},{10,11... | collective-permute-start | bytes 442376 | tf_op jit(solution)/shard_map/ppermute | solution.py:682

commit v4 on v2

--- a/solution.py
+++ b/solution.py
@@ -773,7 +773,7 @@
     gate_pair = quarter_product(normed_ffn, gates, block, [right, down_sums[1]], "product_gate", True)
     grad_down = sum_twice(*down_sums)
     rights = gather_start(after(right, gate_pair[0], ups[1:]))
-    gate_sums = parts_once(gate_pair)
+    gate_sums = parts_once(gate_pair, grad_down)
     up_pair = quarter_product(normed_ffn, ups, block, [gate_sums[1], grad_down, nearby], "product_up", False)
     up_sums = sum_once(up_pair)
     part = block * 3 // 4

time: 182 us -> 181 us (level)
  transfers between devices with their start and end apart: 33 -> 33, of which waited for: 17 -> 19; matrix products, arithmetic and copies ran while one was open for 3% -> 3% of each run, Pallas kernels for 17% -> 17%
where the time goes in v4:
time: 181 us
  waiting for transfers between devices  91.3 us (50%)
  Pallas kernels  52.6 us (29%)
  starting transfers between devices  28.9 us (16%)
  other arithmetic  3.67 us (2%)
  local copies, waits for them, and re-layouts  3.6 us (2%)
    ppermute x31, waiting for transfers between devices, exchange(): lax.ppermute(value, 'dp', [(source, source ^ flips) for source in range(c...  74.4 us
    ppermute x31, starting transfers between devices, exchange(): lax.ppermute(value, 'dp', [(source, source ^ flips) for source in range(c...  24.4 us
    ppermute x2, waiting for transfers between devices, local(): message = lax.ppermute(message, 'section', [(0, 1), (1, 0)])  16.9 us
    pallas_call x1, Pallas kernels, forward_lite(): pl.pallas_call(forward_lite_kernel, out_shape=[jax.ShapeDtypeStruct((toke...  11.4 us
    pallas_call x1, Pallas kernels, relay_backward(): pl.pallas_call(relay_kernel, out_shape=shape((tokens, 2 * width), bfloat)...  11.1 us
    pallas_call x1, Pallas kernels, forward(): pl.pallas_call(lambda *refs: forward_kernel(fast, *refs), out_shape=[shap...  8.71 us
    pallas_call x1, Pallas kernels, attn_backward(): pl.pallas_call(attn_kernel, out_shape=[shape((1, tokens, 2 * width), bflo...  8.17 us
    pallas_call x1, Pallas kernels, ffn_backward(): pl.pallas_call(ffn_kernel, out_shape=[shape((tokens, width), bfloat)] * 8...  5.33 us
  transfers between devices with their start and end apart: 33, of which 19 were waited for; matrix products, arithmetic and copies ran while one was open for 3% of the time, Pallas kernels for 17%

profile of v4, /device:TPU:0, one launch (start us, length us, event | category | flops | bytes accessed | tf_op | source)
XLA Modules:
  0.0 181.1 jit_solution(4820425927269498301)
XLA Ops:
  0.7 11.4 %forward_lite.1 = (bf16[192,1536]{1,0:T(8,128)(2,1)S(1)}, bf16[1,768,768]{2,1,0:T(8,128)(2,1)S(1)}, bf16[1,768,768]{2,1,0:T(8,128)(2,1)S(1)}, bf16[1,768,768]{2,...) custom-call(bf16[192,1536]{1,0:T(8,128)(2,1)} %refs_0_.1, ...), custom_call_target="tpu_custom_call" | custom-call | flops 3623878 | bytes 18874 | tf_op jit(solution)/shard_map/forward_lite/pallas_call | solution.py:202
  12.2 3.0 %collective-permute-start = (bf16[192,1536]{1,0:T(8,128)(2,1)S(1)}, bf16[192,1536]{1,0:T(8,128)(2,1)S(1)}, u32[]{:S(2)}, u32[]{:S(2)}) collective-permute-start(bf16[192,1536]{1,0:T(8,128)(2,1)S(1)} %get-tuple-element.94), channel_id=1, source_target_pairs={{0,16},{16,0},{1,17},{17,1},{2,18},{18,2},{3,19},{19,3},{4,20},{20... | collective-permute-start | bytes 1769480 | tf_op jit(solution)/shard_map/ppermute | solution.py:812
  15.1 13.3 %collective-permute-done.refs_1_ = bf16[192,1536]{1,0:T(8,128)(2,1)S(1)} collective-permute-done((bf16[192,1536]{1,0:T(8,128)(2,1)S(1)}, bf16[192,1536]{1,0:T(8,128)(2,1)S(1)}, u32[]{:S(2)}, u32[]{:S(2)}) %collective-permute-start) | collective-permute-done | bytes 589856 | tf_op jit(solution)/shard_map/ppermute | solution.py:812
  28.5 8.7 %forward_full.1 = (bf16[192,1536]{1,0:T(8,128)(2,1)S(1)}, bf16[1,192,1536]{2,1,0:T(8,128)(2,1)}, bf16[192,768]{1,0:T(8,128)(2,1)S(1)}, bf16[192,768]{1,0:T(8,128...) custom-call(bf16[192,1536]{1,0:T(8,128)(2,1)S(1)} %copy-done.2, ...), custom_call_target="tpu_custom_call" | custom-call | flops 3623878 | bytes 18874 | tf_op jit(solution)/shard_map/forward_full/pallas_call | solution.py:307
  37.2 1.8 collective-permute-start.3
  39.0 11.1 %backward_relay.1 = bf16[192,1536]{1,0:T(8,128)(2,1)S(1)} custom-call(bf16[192,1536]{1,0:T(8,128)(2,1)S(1)} %copy-done, s32[2]{0:T(128)S(1)} %copy-done.10, f32[1,2]{1,0:T(1,128)S(1)} %copy-done.7, f32[1,2,2]{2,1,0:T(2,128)S(1)} %copy-done.8, f32[1,768]{1,0:T(1,128)S(1)} %copy-done.5, f32[1,768]{1,0:T(1,128)S(1)} %copy-done.6, ...), custom_call_target="tpu_custom_call" | custom-call | flops 3623878 | bytes 18874 | tf_op jit(solution)/shard_map/backward_relay/pallas_call | solution.py:526
  50.2 1.6 collective-permute-start.1
  51.8 10.4 %collective-permute-done.4.refs_6_.refs_3_ = bf16[192,768]{1,0:T(8,128)(2,1)S(1)} collective-permute-done((bf16[192,768]{1,0:T(8,128)(2,1)S(1)}, bf16[192,768]{1,0:T(8,128)(2,1)S(1)}, u32[]{:S(2)}, u32[]{:S(2)}) %collective-permute-start.4) | collective-permute-done | bytes 294944 | tf_op jit(solution)/shard_map/ppermute | solution.py:682
  62.2 3.5 %collective-permute-done.1.refs_0_ = bf16[192,1536]{1,0:T(8,128)(2,1)S(1)} collective-permute-done((bf16[192,1536]{1,0:T(8,128)(2,1)S(1)}, bf16[192,1536]{1,0:T(8,128)(2,1)S(1)}, u32[]{:S(2)}, u32[]{:S(2)}) %collective-permute-start.1) | collective-permute-done | bytes 589856 | tf_op jit(solution)/shard_map/ppermute | solution.py:821
  65.7 0.8 backward_start.1
  66.9 5.3 %backward_ffn.1 = (bf16[192,768]{1,0:T(8,128)(2,1)S(1)}, bf16[192,768]{1,0:T(8,128)(2,1)S(1)}, bf16[192,768]{1,0:T(8,128)(2,1)S(1)}, bf16[192,768]{1,0:T(8,128)(...) custom-call(bf16[192,1536]{1,0:T(8,128)(2,1)S(1)} %get-tuple-element, ...), custom_call_target="tpu_custom_call" | custom-call | flops 2717908 | bytes 14155 | tf_op jit(solution)/shard_map/backward_ffn/pallas_call | solution.py:400
  72.2 2.7 %collective-permute-done.6.refs_6_ = bf16[192,768]{1,0:T(8,128)(2,1)S(1)} collective-permute-done((bf16[192,768]{1,0:T(8,128)(2,1)S(1)}, bf16[192,768]{1,0:T(8,128)(2,1)S(1)}, u32[]{:S(2)}, u32[]{:S(2)}) %collective-permute-start.6) | collective-permute-done | bytes 294944 | tf_op jit(solution)/shard_map/ppermute | solution.py:682
  74.9 1.6 collective-permute-done.7.refs_7_
  76.5 1.2 product_down.1
  77.7 1.6 collective-permute-start.13
  80.4 0.9 collective-permute-start.12
  81.4 8.2 %backward_attn.1 = (bf16[1,192,1536]{2,1,0:T(8,128)(2,1)}, bf16[208,3072]{1,0:T(8,128)(2,1)S(1)}, f32[8,768]{1,0:T(8,128)}) custom-call(bf16[192,768]{1,0:T(8,128)(2,1)S(1)} %get-tuple-element.116.datt_ref, bf16[192,768]{1,0:T(8,128)(2,1)S(1)} %get-tuple-element.106.q_ref, bf16[192,768]{1,0:T(8,128)(2,1)S(1)} %get-tuple-element.107.k_ref, ...), custom_call_target="tpu_custom_call" | custom-call | flops 1132462 | bytes 4718 | tf_op jit(solution)/shard_map/backward_attn/pallas_call | solution.py:480
  89.5 3.6 %collective-permute-done.13 = bf16[2,192,768]{2,1,0:T(8,128)(2,1)S(1)} collective-permute-done((bf16[2,192,768]{2,1,0:T(8,128)(2,1)S(1)}, bf16[2,192,768]{2,1,0:T(8,128)(2,1)S(1)}, u32[]{:S(2)}, u32[]{:S(2)}) %collective-permute-start.13) | collective-permute-done | bytes 589856 | tf_op jit(solution)/shard_map/ppermute | solution.py:682
  93.5 1.5 collective-permute-start.16
  95.1 2.7 %collective-permute-start.21 = (bf16[192,768]{1,0:T(8,128)(2,1)S(1)}, bf16[192,768]{1,0:T(8,128)(2,1)S(1)}, u32[]{:S(2)}, u32[]{:S(2)}) collective-permute-start(bf16[192,768]{1,0:T(8,128)(2,1)S(1)} %fusion.4.refs_9_), channel_id=1, source_target_pairs={{0,8},{1,9},{2,10},{3,11},{4,12},{5,13},{6,14},{7,15},{8,0},{9,1},... | collective-permute-start | bytes 884744 | tf_op jit(solution)/shard_map/ppermute | solution.py:682
  97.7 1.2 product_gate.1
  99.0 1.7 collective-permute-start.19
  101.0 1.9 %collective-permute-done.15.refs_6_ = bf16[192,768]{1,0:T(8,128)(2,1)S(1)} collective-permute-done((bf16[192,768]{1,0:T(8,128)(2,1)S(1)}, bf16[192,768]{1,0:T(8,128)(2,1)S(1)}, u32[]{:S(2)}, u32[]{:S(2)}) %collective-permute-start.15) | collective-permute-done | bytes 294944 | tf_op jit(solution)/shard_map/ppermute | solution.py:682
  102.9 5.5 %collective-permute-done.16.refs_7_ = bf16[192,768]{1,0:T(8,128)(2,1)S(1)} collective-permute-done((bf16[192,768]{1,0:T(8,128)(2,1)S(1)}, bf16[192,768]{1,0:T(8,128)(2,1)S(1)}, u32[]{:S(2)}, u32[]{:S(2)}) %collective-permute-start.16) | collective-permute-done | bytes 294944 | tf_op jit(solution)/shard_map/ppermute | solution.py:682
  108.8 2.8 %collective-permute-done.21 = bf16[192,768]{1,0:T(8,128)(2,1)S(1)} collective-permute-done((bf16[192,768]{1,0:T(8,128)(2,1)S(1)}, bf16[192,768]{1,0:T(8,128)(2,1)S(1)}, u32[]{:S(2)}, u32[]{:S(2)}) %collective-permute-start.21) | collective-permute-done | bytes 294944 | tf_op jit(solution)/shard_map/ppermute | solution.py:682
  111.7 2.4 %collective-permute-done.19 = bf16[192,768]{1,0:T(8,128)(2,1)S(1)} collective-permute-done((bf16[192,768]{1,0:T(8,128)(2,1)S(1)}, bf16[192,768]{1,0:T(8,128)(2,1)S(1)}, u32[]{:S(2)}, u32[]{:S(2)}) %collective-permute-start.19) | collective-permute-done | bytes 294944 | tf_op jit(solution)/shard_map/ppermute | solution.py:682
  114.1 5.4 %collective-permute-done.20 = bf16[192,768]{1,0:T(8,128)(2,1)S(1)} collective-permute-done((bf16[192,768]{1,0:T(8,128)(2,1)S(1)}, bf16[192,768]{1,0:T(8,128)(2,1)S(1)}, u32[]{:S(2)}, u32[]{:S(2)}) %collective-permute-start.20) | collective-permute-done | bytes 294944 | tf_op jit(solution)/shard_map/ppermute | solution.py:682
  119.5 1.2 product_up.1
  121.0 2.9 %collective-permute-start.23 = (bf16[144,768]{1,0:T(8,128)(2,1)S(1)}, bf16[144,768]{1,0:T(8,128)(2,1)S(1)}, u32[]{:S(2)}, u32[]{:S(2)}) collective-permute-start(bf16[144,768]{1,0:T(8,128)(2,1)S(1)} %slice.119), channel_id=1, source_target_pairs={{0,8},{1,9},{2,10},{3,11},{4,12},{5,13},{6,14},{7,15},{8,0},{9,1},... | collective-permute-start | bytes 663560 | tf_op jit(solution)/shard_map/ppermute | solution.py:682
  123.9 16.0 %collective-permute-done.22 = bf16[2,192,768]{2,1,0:T(8,128)(2,1)S(1)} collective-permute-done((bf16[2,192,768]{2,1,0:T(8,128)(2,1)S(1)}, bf16[2,192,768]{2,1,0:T(8,128)(2,1)S(1)}, u32[]{:S(2)}, u32[]{:S(2)}) %collective-permute-start.22) | collective-permute-done | bytes 589856 | tf_op jit(solution)/shard_map/ppermute | solution.py:682
  140.1 0.8 pad_maximum_fusion
  140.9 2.0 %collective-permute-start.26 = (bf16[240,768]{1,0:T(8,128)(2,1)}, bf16[240,768]{1,0:T(8,128)(2,1)}, u32[]{:S(2)}, u32[]{:S(2)}) collective-permute-start(bf16[240,768]{1,0:T(8,128)(2,1)} %pad_maximum_fusion), channel_id=1, source_target_pairs={{0,8},{1,9},{2,10},{3,11},{4,12},{5,13},{6,14},{7,15},{8,0},{9,1},... | collective-permute-start | bytes 1105928 | tf_op jit(solution)/shard_map/ppermute | solution.py:682
  143.1 1.5 product_attn.1
  144.6 0.7 copy-done.11
  145.3 1.4 collective-permute-start.25
  147.4 13.7 %collective-permute-done.26 = bf16[240,768]{1,0:T(8,128)(2,1)} collective-permute-done((bf16[240,768]{1,0:T(8,128)(2,1)}, bf16[240,768]{1,0:T(8,128)(2,1)}, u32[]{:S(2)}, u32[]{:S(2)}) %collective-permute-start.26) | collective-permute-done | bytes 368672 | tf_op jit(solution)/shard_map/ppermute | solution.py:682
  161.1 2.4 %collective-permute-done.25.came_ref = bf16[112,1536]{1,0:T(8,128)(2,1)S(1)} collective-permute-done((bf16[112,1536]{1,0:T(8,128)(2,1)S(1)}, bf16[112,1536]{1,0:T(8,128)(2,1)S(1)}, u32[]{:S(2)}, u32[]{:S(2)}) %collective-permute-start.25) | collective-permute-done | bytes 344096 | tf_op jit(solution)/shard_map/ppermute | solution.py:682
  163.5 1.7 collective-permute-start.27
  165.2 0.9 slice.109
  166.1 1.7 fusion
  168.6 1.4 collective-permute-start.30
  170.0 0.7 collective-permute-done.28
  170.8 0.7 collective-permute-start.29
  171.5 3.0 %collective-permute-done.27.came_ref = bf16[64,1536]{1,0:T(8,128)(2,1)S(1)} collective-permute-done((bf16[64,1536]{1,0:T(8,128)(2,1)S(1)}, bf16[64,1536]{1,0:T(8,128)(2,1)S(1)}, u32[]{:S(2)}, u32[]{:S(2)}) %collective-permute-start.27) | collective-permute-done | bytes 196640 | tf_op jit(solution)/shard_map/ppermute | solution.py:682
  174.4 0.7 first_end.1
  176.6 1.1 assemble.1
  178.3 2.1 %collective-permute-done.29 = bf16[48,1536]{1,0:T(8,128)(2,1)S(1)} collective-permute-done((bf16[48,1536]{1,0:T(8,128)(2,1)S(1)}, bf16[48,1536]{1,0:T(8,128)(2,1)S(1)}, u32[]{:S(2)}, u32[]{:S(2)}) %collective-permute-start.29) | collective-permute-done | bytes 147488 | tf_op jit(solution)/shard_map/ppermute | solution.py:682
  180.4 0.7 fusion.7
  (83 shorter events, 7.0 us)
Async XLA Ops:
  0.6 27.8 %copy-start.2 = (bf16[192,1536]{1,0:T(8,128)(2,1)S(1)}, bf16[192,1536]{1,0:T(8,128)(2,1)}, u32[]{:S(2)}) copy-start(bf16[192,1536]{1,0:T(8,128)(2,1)} %refs_0_.1) | copy-start | bytes 1769476
  0.7 27.8 %copy-start.9 = (s32[2,96]{1,0:T(2,128)S(1)}, s32[2,96]{1,0:T(2,128)}, u32[]{:S(2)}) copy-start(s32[2,96]{1,0:T(2,128)} %refs_2_.2) | copy-start | bytes 2308
  0.7 27.8 %copy-start.8 = (f32[1,2,2]{2,1,0:T(2,128)S(1)}, f32[1,2,2]{2,1,0:T(2,128)}, u32[]{:S(2)}) copy-start(f32[1,2,2]{2,1,0:T(2,128)} %mix_ref.3) | copy-start | bytes 52
  0.7 27.8 %copy-start.7 = (f32[1,2]{1,0:T(1,128)S(1)}, f32[1,2]{1,0:T(1,128)}, u32[]{:S(2)}) copy-start(f32[1,2]{1,0:T(1,128)} %cor_ref.5) | copy-start | bytes 28
  0.7 27.8 %copy-start.6 = (f32[1,768]{1,0:T(1,128)S(1)}, f32[1,768]{1,0:T(1,128)}, u32[]{:S(2)}) copy-start(f32[1,768]{1,0:T(1,128)} %ga_ref.3) | copy-start | bytes 9220
  0.7 27.8 %copy-start.5 = (f32[1,768]{1,0:T(1,128)S(1)}, f32[1,768]{1,0:T(1,128)}, u32[]{:S(2)}) copy-start(f32[1,768]{1,0:T(1,128)} %gf_ref.3) | copy-start | bytes 9220
  12.2 16.3 %collective-permute-start = (bf16[192,1536]{1,0:T(8,128)(2,1)S(1)}, bf16[192,1536]{1,0:T(8,128)(2,1)S(1)}, u32[]{:S(2)}, u32[]{:S(2)}) collective-permute-start(bf16[192,1536]{1,0:T(8,128)(2,1)S(1)} %get-tuple-element.94), channel_id=1, source_target_pairs={{0,16},{16,0},{1,17},{17,1},{2,18},{18,2},{3,19},{19,3},{4,20},{20... | collective-permute-start | bytes 1769480 | tf_op jit(solution)/shard_map/ppermute | solution.py:812
  28.5 10.5 %copy-start = (bf16[192,1536]{1,0:T(8,128)(2,1)S(1)}, bf16[192,1536]{1,0:T(8,128)(2,1)}, u32[]{:S(2)}) copy-start(bf16[192,1536]{1,0:T(8,128)(2,1)} %refs_1_.1) | copy-start | bytes 1769476
  28.5 10.5 %copy-start.10 = (s32[2]{0:T(128)S(1)}, s32[2]{0:T(128)}, u32[]{:S(2)}) copy-start(s32[2]{0:T(128)} %refs_2_.3) | copy-start | bytes 28
  37.2 28.5 %collective-permute-start.2 = (bf16[192,1920]{1,0:T(8,128)(2,1)S(1)}, bf16[192,1920]{1,0:T(8,128)(2,1)S(1)}, u32[]{:S(2)}, u32[]{:S(2)}) collective-permute-start(bf16[192,1920]{1,0:T(8,128)(2,1)S(1)} %get-tuple-element.111), channel_id=1, source_target_pairs={{0,1},{1,0},{2,3},{3,2},{4,5},{5,4},{6,7},{7,6},{8,9},{9,8},{10,11... | collective-permute-start | bytes 2211848 | tf_op jit(solution)/shard_map/ppermute | solution.py:682
  37.2 28.5 %collective-permute-start.3 = (bf16[192,1920]{1,0:T(8,128)(2,1)S(1)}, bf16[192,1920]{1,0:T(8,128)(2,1)S(1)}, u32[]{:S(2)}, u32[]{:S(2)}) collective-permute-start(bf16[192,1920]{1,0:T(8,128)(2,1)S(1)} %get-tuple-element.112), channel_id=1, source_target_pairs={{0,2},{1,3},{2,0},{3,1},{4,6},{5,7},{6,4},{7,5},{8,10},{9,11},{10,... | collective-permute-start | bytes 2211848 | tf_op jit(solution)/shard_map/ppermute | solution.py:682
  50.2 15.5 %collective-permute-start.1 = (bf16[192,1536]{1,0:T(8,128)(2,1)S(1)}, bf16[192,1536]{1,0:T(8,128)(2,1)S(1)}, u32[]{:S(2)}, u32[]{:S(2)}) collective-permute-start(bf16[192,1536]{1,0:T(8,128)(2,1)S(1)} %backward_relay.1), channel_id=1, source_target_pairs={{0,16},{16,0},{1,17},{17,1},{2,18},{18,2},{3,19},{19,3},{4,20},{20... | collective-permute-start | bytes 1769480 | tf_op jit(solution)/shard_map/ppermute | solution.py:821
  51.7 10.4 %collective-permute-start.4 = (bf16[192,768]{1,0:T(8,128)(2,1)S(1)}, bf16[192,768]{1,0:T(8,128)(2,1)S(1)}, u32[]{:S(2)}, u32[]{:S(2)}) collective-permute-start(bf16[192,768]{1,0:T(8,128)(2,1)S(1)} %get-tuple-element.113), channel_id=1, source_target_pairs={{0,3},{1,2},{2,1},{3,0},{4,7},{5,6},{6,5},{7,4},{8,11},{9,10},{10,... | collective-permute-start | bytes 884744 | tf_op jit(solution)/shard_map/ppermute | solution.py:682
  66.5 8.4 %collective-permute-start.6 = (bf16[192,768]{1,0:T(8,128)(2,1)S(1)}, bf16[192,768]{1,0:T(8,128)(2,1)S(1)}, u32[]{:S(2)}, u32[]{:S(2)}) collective-permute-start(bf16[192,768]{1,0:T(8,128)(2,1)S(1)} %get-tuple-element.115.low_ref.refs_4_), channel_id=1, source_target_pairs={{0,2},{1,3},{2,0},{3,1},{4,6},{5,7},{6,4},{7,5},{8,10},{9,11},{10,... | collective-permute-start | bytes 884744 | tf_op jit(solution)/shard_map/ppermute | solution.py:682
  66.9 8.0 %collective-permute-start.5 = (bf16[192,768]{1,0:T(8,128)(2,1)S(1)}, bf16[192,768]{1,0:T(8,128)(2,1)S(1)}, u32[]{:S(2)}, u32[]{:S(2)}) collective-permute-start(bf16[192,768]{1,0:T(8,128)(2,1)S(1)} %get-tuple-element.115.low_ref.refs_4_), channel_id=1, source_target_pairs={{0,1},{1,0},{2,3},{3,2},{4,5},{5,4},{6,7},{7,6},{8,9},{9,8},{10,11... | collective-permute-start | bytes 884744 | tf_op jit(solution)/shard_map/ppermute | solution.py:682
  74.9 1.6 collective-permute-start.7
  77.7 15.4 %collective-permute-start.13 = (bf16[2,192,768]{2,1,0:T(8,128)(2,1)S(1)}, bf16[2,192,768]{2,1,0:T(8,128)(2,1)S(1)}, u32[]{:S(2)}, u32[]{:S(2)}) collective-permute-start(bf16[2,192,768]{2,1,0:T(8,128)(2,1)S(1)} %get-tuple-element.124.before), channel_id=1, source_target_pairs={{0,4},{1,5},{2,6},{3,7},{4,0},{5,1},{6,2},{7,3},{8,12},{9,13},{10,... | collective-permute-start | bytes 1769480 | tf_op jit(solution)/shard_map/ppermute | solution.py:682
  79.4 13.8 %collective-permute-start.9 = (bf16[192,768]{1,0:T(8,128)(2,1)S(1)}, bf16[192,768]{1,0:T(8,128)(2,1)S(1)}, u32[]{:S(2)}, u32[]{:S(2)}) collective-permute-start(bf16[192,768]{1,0:T(8,128)(2,1)S(1)} %slice.117.refs_2_), channel_id=1, source_target_pairs={{0,1},{1,0},{2,3},{3,2},{4,5},{5,4},{6,7},{7,6},{8,9},{9,8},{10,11... | collective-permute-start | bytes 884744 | tf_op jit(solution)/shard_map/ppermute | solution.py:682
  79.4 14.0 %collective-permute-start.10 = (bf16[192,768]{1,0:T(8,128)(2,1)S(1)}, bf16[192,768]{1,0:T(8,128)(2,1)S(1)}, u32[]{:S(2)}, u32[]{:S(2)}) collective-permute-start(bf16[192,768]{1,0:T(8,128)(2,1)S(1)} %get-tuple-element.135), channel_id=1, source_target_pairs={{0,1},{1,0},{2,3},{3,2},{4,5},{5,4},{6,7},{7,6},{8,9},{9,8},{10,11... | collective-permute-start | bytes 884744 | tf_op jit(solution)/shard_map/ppermute | solution.py:682
  79.9 15.1 %collective-permute-start.11 = (bf16[192,768]{1,0:T(8,128)(2,1)S(1)}, bf16[192,768]{1,0:T(8,128)(2,1)S(1)}, u32[]{:S(2)}, u32[]{:S(2)}) collective-permute-start(bf16[192,768]{1,0:T(8,128)(2,1)S(1)} %get-tuple-element.136), channel_id=1, source_target_pairs={{0,2},{1,3},{2,0},{3,1},{4,6},{5,7},{6,4},{7,5},{8,10},{9,11},{10,... | collective-permute-start | bytes 884744 | tf_op jit(solution)/shard_map/ppermute | solution.py:682
  80.4 17.3 %collective-permute-start.12 = (bf16[192,768]{1,0:T(8,128)(2,1)S(1)}, bf16[192,768]{1,0:T(8,128)(2,1)S(1)}, u32[]{:S(2)}, u32[]{:S(2)}) collective-permute-start(bf16[192,768]{1,0:T(8,128)(2,1)S(1)} %get-tuple-element.137), channel_id=1, source_target_pairs={{0,3},{1,2},{2,1},{3,0},{4,7},{5,6},{6,5},{7,4},{8,11},{9,10},{10,... | collective-permute-start | bytes 884744 | tf_op jit(solution)/shard_map/ppermute | solution.py:682
  93.1 7.5 %collective-permute-start.14 = (bf16[192,768]{1,0:T(8,128)(2,1)S(1)}, bf16[192,768]{1,0:T(8,128)(2,1)S(1)}, u32[]{:S(2)}, u32[]{:S(2)}) collective-permute-start(bf16[192,768]{1,0:T(8,128)(2,1)S(1)} %get-tuple-element.141), channel_id=1, source_target_pairs={{0,1},{1,0},{2,3},{3,2},{4,5},{5,4},{6,7},{7,6},{8,9},{9,8},{10,11... | collective-permute-start | bytes 884744 | tf_op jit(solution)/shard_map/ppermute | solution.py:682
  93.1 9.8 %collective-permute-start.15 = (bf16[192,768]{1,0:T(8,128)(2,1)S(1)}, bf16[192,768]{1,0:T(8,128)(2,1)S(1)}, u32[]{:S(2)}, u32[]{:S(2)}) collective-permute-start(bf16[192,768]{1,0:T(8,128)(2,1)S(1)} %get-tuple-element.142), channel_id=1, source_target_pairs={{0,2},{1,3},{2,0},{3,1},{4,6},{5,7},{6,4},{7,5},{8,10},{9,11},{10,... | collective-permute-start | bytes 884744 | tf_op jit(solution)/shard_map/ppermute | solution.py:682
  93.5 15.0 %collective-permute-start.16 = (bf16[192,768]{1,0:T(8,128)(2,1)S(1)}, bf16[192,768]{1,0:T(8,128)(2,1)S(1)}, u32[]{:S(2)}, u32[]{:S(2)}) collective-permute-start(bf16[192,768]{1,0:T(8,128)(2,1)S(1)} %get-tuple-element.143), channel_id=1, source_target_pairs={{0,3},{1,2},{2,1},{3,0},{4,7},{5,6},{6,5},{7,4},{8,11},{9,10},{10,... | collective-permute-start | bytes 884744 | tf_op jit(solution)/shard_map/ppermute | solution.py:682
  95.1 16.6 %collective-permute-start.21 = (bf16[192,768]{1,0:T(8,128)(2,1)S(1)}, bf16[192,768]{1,0:T(8,128)(2,1)S(1)}, u32[]{:S(2)}, u32[]{:S(2)}) collective-permute-start(bf16[192,768]{1,0:T(8,128)(2,1)S(1)} %fusion.4.refs_9_), channel_id=1, source_target_pairs={{0,8},{1,9},{2,10},{3,11},{4,12},{5,13},{6,14},{7,15},{8,0},{9,1},... | collective-permute-start | bytes 884744 | tf_op jit(solution)/shard_map/ppermute | solution.py:682
  98.9 20.5 %copy-start.3 = (f32[4,192,768]{2,1,0:T(8,128)}, f32[4,192,768]{2,1,0:T(8,128)S(1)}, u32[]{:S(2)}) copy-start(f32[4,192,768]{2,1,0:T(8,128)S(1)} %get-tuple-element.146) | copy-start | bytes 7077892
  99.0 15.1 %collective-permute-start.19 = (bf16[192,768]{1,0:T(8,128)(2,1)S(1)}, bf16[192,768]{1,0:T(8,128)(2,1)S(1)}, u32[]{:S(2)}, u32[]{:S(2)}) collective-permute-start(bf16[192,768]{1,0:T(8,128)(2,1)S(1)} %get-tuple-element.140), channel_id=1, source_target_pairs={{0,4},{1,5},{2,6},{3,7},{4,0},{5,1},{6,2},{7,3},{8,12},{9,13},{10,... | collective-permute-start | bytes 884744 | tf_op jit(solution)/shard_map/ppermute | solution.py:682
  100.6 18.8 %collective-permute-start.20 = (bf16[192,768]{1,0:T(8,128)(2,1)S(1)}, bf16[192,768]{1,0:T(8,128)(2,1)S(1)}, u32[]{:S(2)}, u32[]{:S(2)}) collective-permute-start(bf16[192,768]{1,0:T(8,128)(2,1)S(1)} %get-tuple-element.147), channel_id=1, source_target_pairs={{0,4},{1,5},{2,6},{3,7},{4,0},{5,1},{6,2},{7,3},{8,12},{9,13},{10,... | collective-permute-start | bytes 884744 | tf_op jit(solution)/shard_map/ppermute | solution.py:682
  102.9 16.6 %collective-permute-start.8 = (bf16[192,384]{1,0:T(8,128)(2,1)S(1)}, bf16[192,384]{1,0:T(8,128)(2,1)S(1)}, u32[]{:S(2)}, u32[]{:S(2)}) collective-permute-start(bf16[192,384]{1,0:T(8,128)(2,1)S(1)} %get-tuple-element.132), channel_id=1, source_target_pairs={{0,3},{1,2},{2,1},{3,0},{4,7},{5,6},{6,5},{7,4},{8,11},{9,10},{10,... | collective-permute-start | bytes 442376 | tf_op jit(solution)/shard_map/ppermute | solution.py:682
  108.5 31.5 %collective-permute-start.18 = (bf16[208,3072]{1,0:T(8,128)(2,1)S(1)}, bf16[208,3072]{1,0:T(8,128)(2,1)S(1)}, u32[]{:S(2)}, u32[]{:S(2)}) collective-permute-start(bf16[208,3072]{1,0:T(8,128)(2,1)S(1)} %get-tuple-element.144.refs_8_.refs_4_), channel_id=1, source_target_pairs={{0,2},{1,3},{2,0},{3,1},{4,6},{5,7},{6,4},{7,5},{8,10},{9,11},{10,... | collective-permute-start | bytes 3833864 | tf_op jit(solution)/shard_map/ppermute | solution.py:682
  111.7 9.2 %copy-start.1 = (f32[192,768]{1,0:T(8,128)}, f32[192,768]{1,0:T(8,128)S(1)}, u32[]{:S(2)}) copy-start(f32[192,768]{1,0:T(8,128)S(1)} %bitcast_add_fusion.2.refs_9_) | copy-start | bytes 1769476
  114.1 6.9 %copy-start.13 = (bf16[192,768]{1,0:T(8,128)(2,1)}, bf16[192,768]{1,0:T(8,128)(2,1)S(1)}, u32[]{:S(2)}) copy-start(bf16[192,768]{1,0:T(8,128)(2,1)S(1)} %collective-permute-done.19) | copy-start | bytes 884740
  120.7 19.3 %copy-start.4 = (f32[4,192,768]{2,1,0:T(8,128)}, f32[4,192,768]{2,1,0:T(8,128)S(1)}, u32[]{:S(2)}) copy-start(f32[4,192,768]{2,1,0:T(8,128)S(1)} %get-tuple-element.149) | copy-start | bytes 7077892
  120.7 19.2 %collective-permute-start.22 = (bf16[2,192,768]{2,1,0:T(8,128)(2,1)S(1)}, bf16[2,192,768]{2,1,0:T(8,128)(2,1)S(1)}, u32[]{:S(2)}, u32[]{:S(2)}) collective-permute-start(bf16[2,192,768]{2,1,0:T(8,128)(2,1)S(1)} %get-tuple-element.150), channel_id=1, source_target_pairs={{0,4},{1,5},{2,6},{3,7},{4,0},{5,1},{6,2},{7,3},{8,12},{9,13},{10,... | collective-permute-start | bytes 1769480 | tf_op jit(solution)/shard_map/ppermute | solution.py:682
  120.9 21.9 %collective-permute-start.17 = (bf16[208,3072]{1,0:T(8,128)(2,1)S(1)}, bf16[208,3072]{1,0:T(8,128)(2,1)S(1)}, u32[]{:S(2)}, u32[]{:S(2)}) collective-permute-start(bf16[208,3072]{1,0:T(8,128)(2,1)S(1)} %get-tuple-element.144.refs_8_.refs_4_), channel_id=1, source_target_pairs={{0,1},{1,0},{2,3},{3,2},{4,5},{5,4},{6,7},{7,6},{8,9},{9,8},{10,11... | collective-permute-start | bytes 3833864 | tf_op jit(solution)/shard_map/ppermute | solution.py:682
  121.0 19.0 %collective-permute-start.23 = (bf16[144,768]{1,0:T(8,128)(2,1)S(1)}, bf16[144,768]{1,0:T(8,128)(2,1)S(1)}, u32[]{:S(2)}, u32[]{:S(2)}) collective-permute-start(bf16[144,768]{1,0:T(8,128)(2,1)S(1)} %slice.119), channel_id=1, source_target_pairs={{0,8},{1,9},{2,10},{3,11},{4,12},{5,13},{6,14},{7,15},{8,0},{9,1},... | collective-permute-start | bytes 663560 | tf_op jit(solution)/shard_map/ppermute | solution.py:682
  139.9 3.0 %copy-start.12 = (bf16[2,192,768]{2,1,0:T(8,128)(2,1)}, bf16[2,192,768]{2,1,0:T(8,128)(2,1)S(1)}, u32[]{:S(2)}) copy-start(bf16[2,192,768]{2,1,0:T(8,128)(2,1)S(1)} %collective-permute-done.22) | copy-start | bytes 1769476
  140.0 3.1 %collective-permute-start.24 = (bf16[208,3072]{1,0:T(8,128)(2,1)S(1)}, bf16[208,3072]{1,0:T(8,128)(2,1)S(1)}, u32[]{:S(2)}, u32[]{:S(2)}) collective-permute-start(bf16[208,3072]{1,0:T(8,128)(2,1)S(1)} %collective-permute-done.18.refs_6_), channel_id=1, source_target_pairs={{0,1},{1,0},{2,3},{3,2},{4,5},{5,4},{6,7},{7,6},{8,9},{9,8},{10,11... | collective-permute-start | bytes 3833864 | tf_op jit(solution)/shard_map/ppermute | solution.py:682
  140.9 20.2 %collective-permute-start.26 = (bf16[240,768]{1,0:T(8,128)(2,1)}, bf16[240,768]{1,0:T(8,128)(2,1)}, u32[]{:S(2)}, u32[]{:S(2)}) collective-permute-start(bf16[240,768]{1,0:T(8,128)(2,1)} %pad_maximum_fusion), channel_id=1, source_target_pairs={{0,8},{1,9},{2,10},{3,11},{4,12},{5,13},{6,14},{7,15},{8,0},{9,1},... | collective-permute-start | bytes 1105928 | tf_op jit(solution)/shard_map/ppermute | solution.py:682
  144.6 0.7 copy-start.11
  145.3 18.1 %collective-permute-start.25 = (bf16[112,1536]{1,0:T(8,128)(2,1)S(1)}, bf16[112,1536]{1,0:T(8,128)(2,1)S(1)}, u32[]{:S(2)}, u32[]{:S(2)}) collective-permute-start(bf16[112,1536]{1,0:T(8,128)(2,1)S(1)} %get-tuple-element.153), channel_id=1, source_target_pairs={{0,4},{1,5},{2,6},{3,7},{4,0},{5,1},{6,2},{7,3},{8,12},{9,13},{10,... | collective-permute-start | bytes 1032200 | tf_op jit(solution)/shard_map/ppermute | solution.py:682
  146.8 24.0 %collective-permute-start.28 = (bf16[2,48,1536]{2,1,0:T(8,128)(2,1)}, bf16[2,48,1536]{2,1,0:T(8,128)(2,1)S(1)}, u32[]{:S(2)}, u32[]{:S(2)}) collective-permute-start(bf16[2,48,1536]{2,1,0:T(8,128)(2,1)} %copy-done.11), channel_id=1, source_target_pairs={{0,4},{1,5},{2,6},{3,7},{4,0},{5,1},{6,2},{7,3},{8,12},{9,13},{10,... | collective-permute-start | bytes 884744 | tf_op jit(solution)/shard_map/ppermute | solution.py:682
  163.5 10.9 %collective-permute-start.27 = (bf16[64,1536]{1,0:T(8,128)(2,1)S(1)}, bf16[64,1536]{1,0:T(8,128)(2,1)S(1)}, u32[]{:S(2)}, u32[]{:S(2)}) collective-permute-start(bf16[64,1536]{1,0:T(8,128)(2,1)S(1)} %get-tuple-element.157), channel_id=1, source_target_pairs={{0,8},{1,9},{2,10},{3,11},{4,12},{5,13},{6,14},{7,15},{8,0},{9,1},... | collective-permute-start | bytes 589832 | tf_op jit(solution)/shard_map/ppermute | solution.py:682
  167.9 7.4 %collective-permute-start.32 = (bf16[48,1536]{1,0:T(8,128)(2,1)S(1)}, bf16[48,1536]{1,0:T(8,128)(2,1)S(1)}, u32[]{:S(2)}, u32[]{:S(2)}) collective-permute-start(bf16[48,1536]{1,0:T(8,128)(2,1)S(1)} %pad_maximum_fusion.4), channel_id=1, source_target_pairs={{0,3},{1,2},{2,1},{3,0},{4,7},{5,6},{6,5},{7,4},{8,11},{9,10},{10,... | collective-permute-start | bytes 442376 | tf_op jit(solution)/shard_map/ppermute | solution.py:682
  168.0 7.4 %collective-permute-start.31 = (bf16[48,1536]{1,0:T(8,128)(2,1)S(1)}, bf16[48,1536]{1,0:T(8,128)(2,1)S(1)}, u32[]{:S(2)}, u32[]{:S(2)}) collective-permute-start(bf16[48,1536]{1,0:T(8,128)(2,1)S(1)} %pad_maximum_fusion.3), channel_id=1, source_target_pairs={{0,2},{1,3},{2,0},{3,1},{4,6},{5,7},{6,4},{7,5},{8,10},{9,11},{10,... | collective-permute-start | bytes 442376 | tf_op jit(solution)/shard_map/ppermute | solution.py:682
  168.6 6.8 %collective-permute-start.30 = (bf16[48,1536]{1,0:T(8,128)(2,1)S(1)}, bf16[48,1536]{1,0:T(8,128)(2,1)S(1)}, u32[]{:S(2)}, u32[]{:S(2)}) collective-permute-start(bf16[48,1536]{1,0:T(8,128)(2,1)S(1)} %pad_maximum_fusion.2), channel_id=1, source_target_pairs={{0,1},{1,0},{2,3},{3,2},{4,5},{5,4},{6,7},{7,6},{8,9},{9,8},{10,11... | collective-permute-start | bytes 442376 | tf_op jit(solution)/shard_map/ppermute | solution.py:682
  170.8 9.6 %collective-permute-start.29 = (bf16[48,1536]{1,0:T(8,128)(2,1)S(1)}, bf16[48,1536]{1,0:T(8,128)(2,1)S(1)}, u32[]{:S(2)}, u32[]{:S(2)}) collective-permute-start(bf16[48,1536]{1,0:T(8,128)(2,1)S(1)} %get-tuple-element.175), channel_id=1, source_target_pairs={{0,8},{1,9},{2,10},{3,11},{4,12},{5,13},{6,14},{7,15},{8,0},{9,1},... | collective-permute-start | bytes 442376 | tf_op jit(solution)/shard_map/ppermute | solution.py:682

commit v5 on v4

--- a/solution.py
+++ b/solution.py
@@ -156,8 +156,8 @@
     nrm_ref[...] = (active * rms_scale(active) * ga_ref[...]).astype(bfloat)
     for place, (copy, weight, target) in enumerate(zip(queue, (wq_s, wk_s, wv_s), (q_ref, k_ref, v_ref))):
         copy.wait()
-        if place != 1:
-            start_group(place // 2)
+        if place < 2:
+            start_group(place)
         target[...] = dot(nrm_ref[...], weight[0]).astype(bfloat)
     attention(q_ref, k_ref, v_ref, seg_ref, att_ref, None)
     for piece in range(2, pieces):

time: 181 us -> 181 us (level)
  no operation moved by 1% of the time
where the time goes in v5:
time: 181 us
  waiting for transfers between devices  91.2 us (50%)
  Pallas kernels  52.6 us (29%)
  starting transfers between devices  29 us (16%)
  other arithmetic  3.67 us (2%)
  local copies, waits for them, and re-layouts  3.6 us (2%)
    ppermute x31, waiting for transfers between devices, exchange(): lax.ppermute(value, 'dp', [(source, source ^ flips) for source in range(c...  74.3 us
    ppermute x31, starting transfers between devices, exchange(): lax.ppermute(value, 'dp', [(source, source ^ flips) for source in range(c...  24.5 us
    ppermute x2, waiting for transfers between devices, local(): message = lax.ppermute(message, 'section', [(0, 1), (1, 0)])  16.9 us
    pallas_call x1, Pallas kernels, forward_lite(): pl.pallas_call(forward_lite_kernel, out_shape=[jax.ShapeDtypeStruct((toke...  11.4 us
    pallas_call x1, Pallas kernels, relay_backward(): pl.pallas_call(relay_kernel, out_shape=shape((tokens, 2 * width), bfloat)...  11.1 us
    pallas_call x1, Pallas kernels, forward(): pl.pallas_call(lambda *refs: forward_kernel(fast, *refs), out_shape=[shap...  8.71 us
    pallas_call x1, Pallas kernels, attn_backward(): pl.pallas_call(attn_kernel, out_shape=[shape((1, tokens, 2 * width), bflo...  8.17 us
    pallas_call x1, Pallas kernels, ffn_backward(): pl.pallas_call(ffn_kernel, out_shape=[shape((tokens, width), bfloat)] * 8...  5.33 us
  transfers between devices with their start and end apart: 33, of which 19 were waited for; matrix products, arithmetic and copies ran while one was open for 3% of the time, Pallas kernels for 17%

profile of v5, /device:TPU:0, one launch (start us, length us, event | category | flops | bytes accessed | tf_op | source)
XLA Modules:
  0.0 181.1 jit_solution(14103641373502837172)
XLA Ops:
  0.7 11.4 %forward_lite.1 = (bf16[192,1536]{1,0:T(8,128)(2,1)S(1)}, bf16[1,768,768]{2,1,0:T(8,128)(2,1)S(1)}, bf16[1,768,768]{2,1,0:T(8,128)(2,1)S(1)}, bf16[1,768,768]{2,...) custom-call(bf16[192,1536]{1,0:T(8,128)(2,1)} %refs_0_.1, ...), custom_call_target="tpu_custom_call" | custom-call | flops 3623878 | bytes 18874 | tf_op jit(solution)/shard_map/forward_lite/pallas_call | solution.py:202
  12.2 3.0 %collective-permute-start = (bf16[192,1536]{1,0:T(8,128)(2,1)S(1)}, bf16[192,1536]{1,0:T(8,128)(2,1)S(1)}, u32[]{:S(2)}, u32[]{:S(2)}) collective-permute-start(bf16[192,1536]{1,0:T(8,128)(2,1)S(1)} %get-tuple-element.94), channel_id=1, source_target_pairs={{0,16},{16,0},{1,17},{17,1},{2,18},{18,2},{3,19},{19,3},{4,20},{20... | collective-permute-start | bytes 1769480 | tf_op jit(solution)/shard_map/ppermute | solution.py:812
  15.1 13.3 %collective-permute-done.refs_1_ = bf16[192,1536]{1,0:T(8,128)(2,1)S(1)} collective-permute-done((bf16[192,1536]{1,0:T(8,128)(2,1)S(1)}, bf16[192,1536]{1,0:T(8,128)(2,1)S(1)}, u32[]{:S(2)}, u32[]{:S(2)}) %collective-permute-start) | collective-permute-done | bytes 589856 | tf_op jit(solution)/shard_map/ppermute | solution.py:812
  28.5 8.7 %forward_full.1 = (bf16[192,1536]{1,0:T(8,128)(2,1)S(1)}, bf16[1,192,1536]{2,1,0:T(8,128)(2,1)}, bf16[192,768]{1,0:T(8,128)(2,1)S(1)}, bf16[192,768]{1,0:T(8,128...) custom-call(bf16[192,1536]{1,0:T(8,128)(2,1)S(1)} %copy-done.2, ...), custom_call_target="tpu_custom_call" | custom-call | flops 3623878 | bytes 18874 | tf_op jit(solution)/shard_map/forward_full/pallas_call | solution.py:307
  37.2 1.8 collective-permute-start.3
  39.0 11.1 %backward_relay.1 = bf16[192,1536]{1,0:T(8,128)(2,1)S(1)} custom-call(bf16[192,1536]{1,0:T(8,128)(2,1)S(1)} %copy-done, s32[2]{0:T(128)S(1)} %copy-done.10, f32[1,2]{1,0:T(1,128)S(1)} %copy-done.7, f32[1,2,2]{2,1,0:T(2,128)S(1)} %copy-done.8, f32[1,768]{1,0:T(1,128)S(1)} %copy-done.5, f32[1,768]{1,0:T(1,128)S(1)} %copy-done.6, ...), custom_call_target="tpu_custom_call" | custom-call | flops 3623878 | bytes 18874 | tf_op jit(solution)/shard_map/backward_relay/pallas_call | solution.py:526
  50.2 1.6 collective-permute-start.1
  51.8 10.4 %collective-permute-done.4.refs_6_.refs_3_ = bf16[192,768]{1,0:T(8,128)(2,1)S(1)} collective-permute-done((bf16[192,768]{1,0:T(8,128)(2,1)S(1)}, bf16[192,768]{1,0:T(8,128)(2,1)S(1)}, u32[]{:S(2)}, u32[]{:S(2)}) %collective-permute-start.4) | collective-permute-done | bytes 294944 | tf_op jit(solution)/shard_map/ppermute | solution.py:682
  62.2 3.5 %collective-permute-done.1.refs_0_ = bf16[192,1536]{1,0:T(8,128)(2,1)S(1)} collective-permute-done((bf16[192,1536]{1,0:T(8,128)(2,1)S(1)}, bf16[192,1536]{1,0:T(8,128)(2,1)S(1)}, u32[]{:S(2)}, u32[]{:S(2)}) %collective-permute-start.1) | collective-permute-done | bytes 589856 | tf_op jit(solution)/shard_map/ppermute | solution.py:821
  65.7 0.8 backward_start.1
  66.9 5.3 %backward_ffn.1 = (bf16[192,768]{1,0:T(8,128)(2,1)S(1)}, bf16[192,768]{1,0:T(8,128)(2,1)S(1)}, bf16[192,768]{1,0:T(8,128)(2,1)S(1)}, bf16[192,768]{1,0:T(8,128)(...) custom-call(bf16[192,1536]{1,0:T(8,128)(2,1)S(1)} %get-tuple-element, ...), custom_call_target="tpu_custom_call" | custom-call | flops 2717908 | bytes 14155 | tf_op jit(solution)/shard_map/backward_ffn/pallas_call | solution.py:400
  72.2 2.7 %collective-permute-done.6.refs_6_ = bf16[192,768]{1,0:T(8,128)(2,1)S(1)} collective-permute-done((bf16[192,768]{1,0:T(8,128)(2,1)S(1)}, bf16[192,768]{1,0:T(8,128)(2,1)S(1)}, u32[]{:S(2)}, u32[]{:S(2)}) %collective-permute-start.6) | collective-permute-done | bytes 294944 | tf_op jit(solution)/shard_map/ppermute | solution.py:682
  74.9 1.6 collective-permute-done.7.refs_7_
  76.5 1.2 product_down.1
  77.7 1.7 collective-permute-start.13
  80.4 0.9 collective-permute-start.12
  81.4 8.2 %backward_attn.1 = (bf16[1,192,1536]{2,1,0:T(8,128)(2,1)}, bf16[208,3072]{1,0:T(8,128)(2,1)S(1)}, f32[8,768]{1,0:T(8,128)}) custom-call(bf16[192,768]{1,0:T(8,128)(2,1)S(1)} %get-tuple-element.116.datt_ref, bf16[192,768]{1,0:T(8,128)(2,1)S(1)} %get-tuple-element.106.q_ref, bf16[192,768]{1,0:T(8,128)(2,1)S(1)} %get-tuple-element.107.k_ref, ...), custom_call_target="tpu_custom_call" | custom-call | flops 1132462 | bytes 4718 | tf_op jit(solution)/shard_map/backward_attn/pallas_call | solution.py:480
  89.6 3.6 %collective-permute-done.13 = bf16[2,192,768]{2,1,0:T(8,128)(2,1)S(1)} collective-permute-done((bf16[2,192,768]{2,1,0:T(8,128)(2,1)S(1)}, bf16[2,192,768]{2,1,0:T(8,128)(2,1)S(1)}, u32[]{:S(2)}, u32[]{:S(2)}) %collective-permute-start.13) | collective-permute-done | bytes 589856 | tf_op jit(solution)/shard_map/ppermute | solution.py:682
  93.5 1.5 collective-permute-start.16
  95.1 2.7 %collective-permute-start.21 = (bf16[192,768]{1,0:T(8,128)(2,1)S(1)}, bf16[192,768]{1,0:T(8,128)(2,1)S(1)}, u32[]{:S(2)}, u32[]{:S(2)}) collective-permute-start(bf16[192,768]{1,0:T(8,128)(2,1)S(1)} %fusion.4.refs_9_), channel_id=1, source_target_pairs={{0,8},{1,9},{2,10},{3,11},{4,12},{5,13},{6,14},{7,15},{8,0},{9,1},... | collective-permute-start | bytes 884744 | tf_op jit(solution)/shard_map/ppermute | solution.py:682
  97.7 1.2 product_gate.1
  99.0 1.7 collective-permute-start.19
  101.0 1.9 %collective-permute-done.15.refs_6_ = bf16[192,768]{1,0:T(8,128)(2,1)S(1)} collective-permute-done((bf16[192,768]{1,0:T(8,128)(2,1)S(1)}, bf16[192,768]{1,0:T(8,128)(2,1)S(1)}, u32[]{:S(2)}, u32[]{:S(2)}) %collective-permute-start.15) | collective-permute-done | bytes 294944 | tf_op jit(solution)/shard_map/ppermute | solution.py:682
  102.9 5.5 %collective-permute-done.16.refs_7_ = bf16[192,768]{1,0:T(8,128)(2,1)S(1)} collective-permute-done((bf16[192,768]{1,0:T(8,128)(2,1)S(1)}, bf16[192,768]{1,0:T(8,128)(2,1)S(1)}, u32[]{:S(2)}, u32[]{:S(2)}) %collective-permute-start.16) | collective-permute-done | bytes 294944 | tf_op jit(solution)/shard_map/ppermute | solution.py:682
  108.8 2.8 %collective-permute-done.21 = bf16[192,768]{1,0:T(8,128)(2,1)S(1)} collective-permute-done((bf16[192,768]{1,0:T(8,128)(2,1)S(1)}, bf16[192,768]{1,0:T(8,128)(2,1)S(1)}, u32[]{:S(2)}, u32[]{:S(2)}) %collective-permute-start.21) | collective-permute-done | bytes 294944 | tf_op jit(solution)/shard_map/ppermute | solution.py:682
  111.7 2.3 %collective-permute-done.19 = bf16[192,768]{1,0:T(8,128)(2,1)S(1)} collective-permute-done((bf16[192,768]{1,0:T(8,128)(2,1)S(1)}, bf16[192,768]{1,0:T(8,128)(2,1)S(1)}, u32[]{:S(2)}, u32[]{:S(2)}) %collective-permute-start.19) | collective-permute-done | bytes 294944 | tf_op jit(solution)/shard_map/ppermute | solution.py:682
  114.1 5.4 %collective-permute-done.20 = bf16[192,768]{1,0:T(8,128)(2,1)S(1)} collective-permute-done((bf16[192,768]{1,0:T(8,128)(2,1)S(1)}, bf16[192,768]{1,0:T(8,128)(2,1)S(1)}, u32[]{:S(2)}, u32[]{:S(2)}) %collective-permute-start.20) | collective-permute-done | bytes 294944 | tf_op jit(solution)/shard_map/ppermute | solution.py:682
  119.5 1.2 product_up.1
  121.0 2.9 %collective-permute-start.23 = (bf16[144,768]{1,0:T(8,128)(2,1)S(1)}, bf16[144,768]{1,0:T(8,128)(2,1)S(1)}, u32[]{:S(2)}, u32[]{:S(2)}) collective-permute-start(bf16[144,768]{1,0:T(8,128)(2,1)S(1)} %slice.119), channel_id=1, source_target_pairs={{0,8},{1,9},{2,10},{3,11},{4,12},{5,13},{6,14},{7,15},{8,0},{9,1},... | collective-permute-start | bytes 663560 | tf_op jit(solution)/shard_map/ppermute | solution.py:682
  123.9 16.0 %collective-permute-done.22 = bf16[2,192,768]{2,1,0:T(8,128)(2,1)S(1)} collective-permute-done((bf16[2,192,768]{2,1,0:T(8,128)(2,1)S(1)}, bf16[2,192,768]{2,1,0:T(8,128)(2,1)S(1)}, u32[]{:S(2)}, u32[]{:S(2)}) %collective-permute-start.22) | collective-permute-done | bytes 589856 | tf_op jit(solution)/shard_map/ppermute | solution.py:682
  140.1 0.8 pad_maximum_fusion
  140.9 2.0 %collective-permute-start.26 = (bf16[240,768]{1,0:T(8,128)(2,1)}, bf16[240,768]{1,0:T(8,128)(2,1)}, u32[]{:S(2)}, u32[]{:S(2)}) collective-permute-start(bf16[240,768]{1,0:T(8,128)(2,1)} %pad_maximum_fusion), channel_id=1, source_target_pairs={{0,8},{1,9},{2,10},{3,11},{4,12},{5,13},{6,14},{7,15},{8,0},{9,1},... | collective-permute-start | bytes 1105928 | tf_op jit(solution)/shard_map/ppermute | solution.py:682
  143.1 1.5 product_attn.1
  144.6 0.7 copy-done.11
  145.3 1.4 collective-permute-start.25
  147.3 13.7 %collective-permute-done.26 = bf16[240,768]{1,0:T(8,128)(2,1)} collective-permute-done((bf16[240,768]{1,0:T(8,128)(2,1)}, bf16[240,768]{1,0:T(8,128)(2,1)}, u32[]{:S(2)}, u32[]{:S(2)}) %collective-permute-start.26) | collective-permute-done | bytes 368672 | tf_op jit(solution)/shard_map/ppermute | solution.py:682
  161.1 2.4 %collective-permute-done.25.came_ref = bf16[112,1536]{1,0:T(8,128)(2,1)S(1)} collective-permute-done((bf16[112,1536]{1,0:T(8,128)(2,1)S(1)}, bf16[112,1536]{1,0:T(8,128)(2,1)S(1)}, u32[]{:S(2)}, u32[]{:S(2)}) %collective-permute-start.25) | collective-permute-done | bytes 344096 | tf_op jit(solution)/shard_map/ppermute | solution.py:682
  163.5 1.7 collective-permute-start.27
  165.2 0.9 slice.109
  166.1 1.7 fusion
  168.6 1.4 collective-permute-start.30
  170.0 0.7 collective-permute-done.28
  171.4 3.0 %collective-permute-done.27.came_ref = bf16[64,1536]{1,0:T(8,128)(2,1)S(1)} collective-permute-done((bf16[64,1536]{1,0:T(8,128)(2,1)S(1)}, bf16[64,1536]{1,0:T(8,128)(2,1)S(1)}, u32[]{:S(2)}, u32[]{:S(2)}) %collective-permute-start.27) | collective-permute-done | bytes 196640 | tf_op jit(solution)/shard_map/ppermute | solution.py:682
  174.4 0.7 first_end.1
  176.0 0.6 reshape.47
  176.6 1.1 assemble.1
  178.3 2.1 %collective-permute-done.29 = bf16[48,1536]{1,0:T(8,128)(2,1)S(1)} collective-permute-done((bf16[48,1536]{1,0:T(8,128)(2,1)S(1)}, bf16[48,1536]{1,0:T(8,128)(2,1)S(1)}, u32[]{:S(2)}, u32[]{:S(2)}) %collective-permute-start.29) | collective-permute-done | bytes 147488 | tf_op jit(solution)/shard_map/ppermute | solution.py:682
  180.4 0.7 fusion.7
  (83 shorter events, 7.0 us)
Async XLA Ops:
  0.6 27.8 %copy-start.2 = (bf16[192,1536]{1,0:T(8,128)(2,1)S(1)}, bf16[192,1536]{1,0:T(8,128)(2,1)}, u32[]{:S(2)}) copy-start(bf16[192,1536]{1,0:T(8,128)(2,1)} %refs_0_.1) | copy-start | bytes 1769476
  0.7 27.8 %copy-start.9 = (s32[2,96]{1,0:T(2,128)S(1)}, s32[2,96]{1,0:T(2,128)}, u32[]{:S(2)}) copy-start(s32[2,96]{1,0:T(2,128)} %refs_2_.2) | copy-start | bytes 2308
  0.7 27.8 %copy-start.8 = (f32[1,2,2]{2,1,0:T(2,128)S(1)}, f32[1,2,2]{2,1,0:T(2,128)}, u32[]{:S(2)}) copy-start(f32[1,2,2]{2,1,0:T(2,128)} %mix_ref.3) | copy-start | bytes 52
  0.7 27.8 %copy-start.7 = (f32[1,2]{1,0:T(1,128)S(1)}, f32[1,2]{1,0:T(1,128)}, u32[]{:S(2)}) copy-start(f32[1,2]{1,0:T(1,128)} %cor_ref.5) | copy-start | bytes 28
  0.7 27.8 %copy-start.6 = (f32[1,768]{1,0:T(1,128)S(1)}, f32[1,768]{1,0:T(1,128)}, u32[]{:S(2)}) copy-start(f32[1,768]{1,0:T(1,128)} %ga_ref.3) | copy-start | bytes 9220
  0.7 27.8 %copy-start.5 = (f32[1,768]{1,0:T(1,128)S(1)}, f32[1,768]{1,0:T(1,128)}, u32[]{:S(2)}) copy-start(f32[1,768]{1,0:T(1,128)} %gf_ref.3) | copy-start | bytes 9220
  12.2 16.3 %collective-permute-start = (bf16[192,1536]{1,0:T(8,128)(2,1)S(1)}, bf16[192,1536]{1,0:T(8,128)(2,1)S(1)}, u32[]{:S(2)}, u32[]{:S(2)}) collective-permute-start(bf16[192,1536]{1,0:T(8,128)(2,1)S(1)} %get-tuple-element.94), channel_id=1, source_target_pairs={{0,16},{16,0},{1,17},{17,1},{2,18},{18,2},{3,19},{19,3},{4,20},{20... | collective-permute-start | bytes 1769480 | tf_op jit(solution)/shard_map/ppermute | solution.py:812
  28.5 10.5 %copy-start = (bf16[192,1536]{1,0:T(8,128)(2,1)S(1)}, bf16[192,1536]{1,0:T(8,128)(2,1)}, u32[]{:S(2)}) copy-start(bf16[192,1536]{1,0:T(8,128)(2,1)} %refs_1_.1) | copy-start | bytes 1769476
  28.5 10.5 %copy-start.10 = (s32[2]{0:T(128)S(1)}, s32[2]{0:T(128)}, u32[]{:S(2)}) copy-start(s32[2]{0:T(128)} %refs_2_.3) | copy-start | bytes 28
  37.2 28.5 %collective-permute-start.2 = (bf16[192,1920]{1,0:T(8,128)(2,1)S(1)}, bf16[192,1920]{1,0:T(8,128)(2,1)S(1)}, u32[]{:S(2)}, u32[]{:S(2)}) collective-permute-start(bf16[192,1920]{1,0:T(8,128)(2,1)S(1)} %get-tuple-element.111), channel_id=1, source_target_pairs={{0,1},{1,0},{2,3},{3,2},{4,5},{5,4},{6,7},{7,6},{8,9},{9,8},{10,11... | collective-permute-start | bytes 2211848 | tf_op jit(solution)/shard_map/ppermute | solution.py:682
  37.2 28.5 %collective-permute-start.3 = (bf16[192,1920]{1,0:T(8,128)(2,1)S(1)}, bf16[192,1920]{1,0:T(8,128)(2,1)S(1)}, u32[]{:S(2)}, u32[]{:S(2)}) collective-permute-start(bf16[192,1920]{1,0:T(8,128)(2,1)S(1)} %get-tuple-element.112), channel_id=1, source_target_pairs={{0,2},{1,3},{2,0},{3,1},{4,6},{5,7},{6,4},{7,5},{8,10},{9,11},{10,... | collective-permute-start | bytes 2211848 | tf_op jit(solution)/shard_map/ppermute | solution.py:682
  50.2 15.5 %collective-permute-start.1 = (bf16[192,1536]{1,0:T(8,128)(2,1)S(1)}, bf16[192,1536]{1,0:T(8,128)(2,1)S(1)}, u32[]{:S(2)}, u32[]{:S(2)}) collective-permute-start(bf16[192,1536]{1,0:T(8,128)(2,1)S(1)} %backward_relay.1), channel_id=1, source_target_pairs={{0,16},{16,0},{1,17},{17,1},{2,18},{18,2},{3,19},{19,3},{4,20},{20... | collective-permute-start | bytes 1769480 | tf_op jit(solution)/shard_map/ppermute | solution.py:821
  51.7 10.4 %collective-permute-start.4 = (bf16[192,768]{1,0:T(8,128)(2,1)S(1)}, bf16[192,768]{1,0:T(8,128)(2,1)S(1)}, u32[]{:S(2)}, u32[]{:S(2)}) collective-permute-start(bf16[192,768]{1,0:T(8,128)(2,1)S(1)} %get-tuple-element.113), channel_id=1, source_target_pairs={{0,3},{1,2},{2,1},{3,0},{4,7},{5,6},{6,5},{7,4},{8,11},{9,10},{10,... | collective-permute-start | bytes 884744 | tf_op jit(solution)/shard_map/ppermute | solution.py:682
  66.5 8.4 %collective-permute-start.6 = (bf16[192,768]{1,0:T(8,128)(2,1)S(1)}, bf16[192,768]{1,0:T(8,128)(2,1)S(1)}, u32[]{:S(2)}, u32[]{:S(2)}) collective-permute-start(bf16[192,768]{1,0:T(8,128)(2,1)S(1)} %get-tuple-element.115.low_ref.refs_4_), channel_id=1, source_target_pairs={{0,2},{1,3},{2,0},{3,1},{4,6},{5,7},{6,4},{7,5},{8,10},{9,11},{10,... | collective-permute-start | bytes 884744 | tf_op jit(solution)/shard_map/ppermute | solution.py:682
  66.9 8.0 %collective-permute-start.5 = (bf16[192,768]{1,0:T(8,128)(2,1)S(1)}, bf16[192,768]{1,0:T(8,128)(2,1)S(1)}, u32[]{:S(2)}, u32[]{:S(2)}) collective-permute-start(bf16[192,768]{1,0:T(8,128)(2,1)S(1)} %get-tuple-element.115.low_ref.refs_4_), channel_id=1, source_target_pairs={{0,1},{1,0},{2,3},{3,2},{4,5},{5,4},{6,7},{7,6},{8,9},{9,8},{10,11... | collective-permute-start | bytes 884744 | tf_op jit(solution)/shard_map/ppermute | solution.py:682
  74.9 1.6 collective-permute-start.7
  77.7 15.4 %collective-permute-start.13 = (bf16[2,192,768]{2,1,0:T(8,128)(2,1)S(1)}, bf16[2,192,768]{2,1,0:T(8,128)(2,1)S(1)}, u32[]{:S(2)}, u32[]{:S(2)}) collective-permute-start(bf16[2,192,768]{2,1,0:T(8,128)(2,1)S(1)} %get-tuple-element.124.before), channel_id=1, source_target_pairs={{0,4},{1,5},{2,6},{3,7},{4,0},{5,1},{6,2},{7,3},{8,12},{9,13},{10,... | collective-permute-start | bytes 1769480 | tf_op jit(solution)/shard_map/ppermute | solution.py:682
  79.4 13.8 %collective-permute-start.9 = (bf16[192,768]{1,0:T(8,128)(2,1)S(1)}, bf16[192,768]{1,0:T(8,128)(2,1)S(1)}, u32[]{:S(2)}, u32[]{:S(2)}) collective-permute-start(bf16[192,768]{1,0:T(8,128)(2,1)S(1)} %slice.117.refs_2_), channel_id=1, source_target_pairs={{0,1},{1,0},{2,3},{3,2},{4,5},{5,4},{6,7},{7,6},{8,9},{9,8},{10,11... | collective-permute-start | bytes 884744 | tf_op jit(solution)/shard_map/ppermute | solution.py:682
  79.5 14.0 %collective-permute-start.10 = (bf16[192,768]{1,0:T(8,128)(2,1)S(1)}, bf16[192,768]{1,0:T(8,128)(2,1)S(1)}, u32[]{:S(2)}, u32[]{:S(2)}) collective-permute-start(bf16[192,768]{1,0:T(8,128)(2,1)S(1)} %get-tuple-element.135), channel_id=1, source_target_pairs={{0,1},{1,0},{2,3},{3,2},{4,5},{5,4},{6,7},{7,6},{8,9},{9,8},{10,11... | collective-permute-start | bytes 884744 | tf_op jit(solution)/shard_map/ppermute | solution.py:682
  80.0 15.1 %collective-permute-start.11 = (bf16[192,768]{1,0:T(8,128)(2,1)S(1)}, bf16[192,768]{1,0:T(8,128)(2,1)S(1)}, u32[]{:S(2)}, u32[]{:S(2)}) collective-permute-start(bf16[192,768]{1,0:T(8,128)(2,1)S(1)} %get-tuple-element.136), channel_id=1, source_target_pairs={{0,2},{1,3},{2,0},{3,1},{4,6},{5,7},{6,4},{7,5},{8,10},{9,11},{10,... | collective-permute-start | bytes 884744 | tf_op jit(solution)/shard_map/ppermute | solution.py:682
  80.4 17.3 %collective-permute-start.12 = (bf16[192,768]{1,0:T(8,128)(2,1)S(1)}, bf16[192,768]{1,0:T(8,128)(2,1)S(1)}, u32[]{:S(2)}, u32[]{:S(2)}) collective-permute-start(bf16[192,768]{1,0:T(8,128)(2,1)S(1)} %get-tuple-element.137), channel_id=1, source_target_pairs={{0,3},{1,2},{2,1},{3,0},{4,7},{5,6},{6,5},{7,4},{8,11},{9,10},{10,... | collective-permute-start | bytes 884744 | tf_op jit(solution)/shard_map/ppermute | solution.py:682
  93.1 7.5 %collective-permute-start.14 = (bf16[192,768]{1,0:T(8,128)(2,1)S(1)}, bf16[192,768]{1,0:T(8,128)(2,1)S(1)}, u32[]{:S(2)}, u32[]{:S(2)}) collective-permute-start(bf16[192,768]{1,0:T(8,128)(2,1)S(1)} %get-tuple-element.141), channel_id=1, source_target_pairs={{0,1},{1,0},{2,3},{3,2},{4,5},{5,4},{6,7},{7,6},{8,9},{9,8},{10,11... | collective-permute-start | bytes 884744 | tf_op jit(solution)/shard_map/ppermute | solution.py:682
  93.1 9.8 %collective-permute-start.15 = (bf16[192,768]{1,0:T(8,128)(2,1)S(1)}, bf16[192,768]{1,0:T(8,128)(2,1)S(1)}, u32[]{:S(2)}, u32[]{:S(2)}) collective-permute-start(bf16[192,768]{1,0:T(8,128)(2,1)S(1)} %get-tuple-element.142), channel_id=1, source_target_pairs={{0,2},{1,3},{2,0},{3,1},{4,6},{5,7},{6,4},{7,5},{8,10},{9,11},{10,... | collective-permute-start | bytes 884744 | tf_op jit(solution)/shard_map/ppermute | solution.py:682
  93.5 15.0 %collective-permute-start.16 = (bf16[192,768]{1,0:T(8,128)(2,1)S(1)}, bf16[192,768]{1,0:T(8,128)(2,1)S(1)}, u32[]{:S(2)}, u32[]{:S(2)}) collective-permute-start(bf16[192,768]{1,0:T(8,128)(2,1)S(1)} %get-tuple-element.143), channel_id=1, source_target_pairs={{0,3},{1,2},{2,1},{3,0},{4,7},{5,6},{6,5},{7,4},{8,11},{9,10},{10,... | collective-permute-start | bytes 884744 | tf_op jit(solution)/shard_map/ppermute | solution.py:682
  95.1 16.6 %collective-permute-start.21 = (bf16[192,768]{1,0:T(8,128)(2,1)S(1)}, bf16[192,768]{1,0:T(8,128)(2,1)S(1)}, u32[]{:S(2)}, u32[]{:S(2)}) collective-permute-start(bf16[192,768]{1,0:T(8,128)(2,1)S(1)} %fusion.4.refs_9_), channel_id=1, source_target_pairs={{0,8},{1,9},{2,10},{3,11},{4,12},{5,13},{6,14},{7,15},{8,0},{9,1},... | collective-permute-start | bytes 884744 | tf_op jit(solution)/shard_map/ppermute | solution.py:682
  98.9 20.5 %copy-start.3 = (f32[4,192,768]{2,1,0:T(8,128)}, f32[4,192,768]{2,1,0:T(8,128)S(1)}, u32[]{:S(2)}) copy-start(f32[4,192,768]{2,1,0:T(8,128)S(1)} %get-tuple-element.146) | copy-start | bytes 7077892
  99.0 15.1 %collective-permute-start.19 = (bf16[192,768]{1,0:T(8,128)(2,1)S(1)}, bf16[192,768]{1,0:T(8,128)(2,1)S(1)}, u32[]{:S(2)}, u32[]{:S(2)}) collective-permute-start(bf16[192,768]{1,0:T(8,128)(2,1)S(1)} %get-tuple-element.140), channel_id=1, source_target_pairs={{0,4},{1,5},{2,6},{3,7},{4,0},{5,1},{6,2},{7,3},{8,12},{9,13},{10,... | collective-permute-start | bytes 884744 | tf_op jit(solution)/shard_map/ppermute | solution.py:682
  100.6 18.8 %collective-permute-start.20 = (bf16[192,768]{1,0:T(8,128)(2,1)S(1)}, bf16[192,768]{1,0:T(8,128)(2,1)S(1)}, u32[]{:S(2)}, u32[]{:S(2)}) collective-permute-start(bf16[192,768]{1,0:T(8,128)(2,1)S(1)} %get-tuple-element.147), channel_id=1, source_target_pairs={{0,4},{1,5},{2,6},{3,7},{4,0},{5,1},{6,2},{7,3},{8,12},{9,13},{10,... | collective-permute-start | bytes 884744 | tf_op jit(solution)/shard_map/ppermute | solution.py:682
  102.9 16.6 %collective-permute-start.8 = (bf16[192,384]{1,0:T(8,128)(2,1)S(1)}, bf16[192,384]{1,0:T(8,128)(2,1)S(1)}, u32[]{:S(2)}, u32[]{:S(2)}) collective-permute-start(bf16[192,384]{1,0:T(8,128)(2,1)S(1)} %get-tuple-element.132), channel_id=1, source_target_pairs={{0,3},{1,2},{2,1},{3,0},{4,7},{5,6},{6,5},{7,4},{8,11},{9,10},{10,... | collective-permute-start | bytes 442376 | tf_op jit(solution)/shard_map/ppermute | solution.py:682
  108.5 31.5 %collective-permute-start.18 = (bf16[208,3072]{1,0:T(8,128)(2,1)S(1)}, bf16[208,3072]{1,0:T(8,128)(2,1)S(1)}, u32[]{:S(2)}, u32[]{:S(2)}) collective-permute-start(bf16[208,3072]{1,0:T(8,128)(2,1)S(1)} %get-tuple-element.144.refs_8_.refs_4_), channel_id=1, source_target_pairs={{0,2},{1,3},{2,0},{3,1},{4,6},{5,7},{6,4},{7,5},{8,10},{9,11},{10,... | collective-permute-start | bytes 3833864 | tf_op jit(solution)/shard_map/ppermute | solution.py:682
  111.7 9.2 %copy-start.1 = (f32[192,768]{1,0:T(8,128)}, f32[192,768]{1,0:T(8,128)S(1)}, u32[]{:S(2)}) copy-start(f32[192,768]{1,0:T(8,128)S(1)} %bitcast_add_fusion.2.refs_9_) | copy-start | bytes 1769476
  114.1 6.9 %copy-start.13 = (bf16[192,768]{1,0:T(8,128)(2,1)}, bf16[192,768]{1,0:T(8,128)(2,1)S(1)}, u32[]{:S(2)}) copy-start(bf16[192,768]{1,0:T(8,128)(2,1)S(1)} %collective-permute-done.19) | copy-start | bytes 884740
  120.7 19.3 %copy-start.4 = (f32[4,192,768]{2,1,0:T(8,128)}, f32[4,192,768]{2,1,0:T(8,128)S(1)}, u32[]{:S(2)}) copy-start(f32[4,192,768]{2,1,0:T(8,128)S(1)} %get-tuple-element.149) | copy-start | bytes 7077892
  120.7 19.2 %collective-permute-start.22 = (bf16[2,192,768]{2,1,0:T(8,128)(2,1)S(1)}, bf16[2,192,768]{2,1,0:T(8,128)(2,1)S(1)}, u32[]{:S(2)}, u32[]{:S(2)}) collective-permute-start(bf16[2,192,768]{2,1,0:T(8,128)(2,1)S(1)} %get-tuple-element.150), channel_id=1, source_target_pairs={{0,4},{1,5},{2,6},{3,7},{4,0},{5,1},{6,2},{7,3},{8,12},{9,13},{10,... | collective-permute-start | bytes 1769480 | tf_op jit(solution)/shard_map/ppermute | solution.py:682
  120.9 21.9 %collective-permute-start.17 = (bf16[208,3072]{1,0:T(8,128)(2,1)S(1)}, bf16[208,3072]{1,0:T(8,128)(2,1)S(1)}, u32[]{:S(2)}, u32[]{:S(2)}) collective-permute-start(bf16[208,3072]{1,0:T(8,128)(2,1)S(1)} %get-tuple-element.144.refs_8_.refs_4_), channel_id=1, source_target_pairs={{0,1},{1,0},{2,3},{3,2},{4,5},{5,4},{6,7},{7,6},{8,9},{9,8},{10,11... | collective-permute-start | bytes 3833864 | tf_op jit(solution)/shard_map/ppermute | solution.py:682
  121.0 19.0 %collective-permute-start.23 = (bf16[144,768]{1,0:T(8,128)(2,1)S(1)}, bf16[144,768]{1,0:T(8,128)(2,1)S(1)}, u32[]{:S(2)}, u32[]{:S(2)}) collective-permute-start(bf16[144,768]{1,0:T(8,128)(2,1)S(1)} %slice.119), channel_id=1, source_target_pairs={{0,8},{1,9},{2,10},{3,11},{4,12},{5,13},{6,14},{7,15},{8,0},{9,1},... | collective-permute-start | bytes 663560 | tf_op jit(solution)/shard_map/ppermute | solution.py:682
  139.9 3.0 %copy-start.12 = (bf16[2,192,768]{2,1,0:T(8,128)(2,1)}, bf16[2,192,768]{2,1,0:T(8,128)(2,1)S(1)}, u32[]{:S(2)}) copy-start(bf16[2,192,768]{2,1,0:T(8,128)(2,1)S(1)} %collective-permute-done.22) | copy-start | bytes 1769476
  140.0 3.1 %collective-permute-start.24 = (bf16[208,3072]{1,0:T(8,128)(2,1)S(1)}, bf16[208,3072]{1,0:T(8,128)(2,1)S(1)}, u32[]{:S(2)}, u32[]{:S(2)}) collective-permute-start(bf16[208,3072]{1,0:T(8,128)(2,1)S(1)} %collective-permute-done.18.refs_6_), channel_id=1, source_target_pairs={{0,1},{1,0},{2,3},{3,2},{4,5},{5,4},{6,7},{7,6},{8,9},{9,8},{10,11... | collective-permute-start | bytes 3833864 | tf_op jit(solution)/shard_map/ppermute | solution.py:682
  140.9 20.2 %collective-permute-start.26 = (bf16[240,768]{1,0:T(8,128)(2,1)}, bf16[240,768]{1,0:T(8,128)(2,1)}, u32[]{:S(2)}, u32[]{:S(2)}) collective-permute-start(bf16[240,768]{1,0:T(8,128)(2,1)} %pad_maximum_fusion), channel_id=1, source_target_pairs={{0,8},{1,9},{2,10},{3,11},{4,12},{5,13},{6,14},{7,15},{8,0},{9,1},... | collective-permute-start | bytes 1105928 | tf_op jit(solution)/shard_map/ppermute | solution.py:682
  144.6 0.7 copy-start.11
  145.3 18.1 %collective-permute-start.25 = (bf16[112,1536]{1,0:T(8,128)(2,1)S(1)}, bf16[112,1536]{1,0:T(8,128)(2,1)S(1)}, u32[]{:S(2)}, u32[]{:S(2)}) collective-permute-start(bf16[112,1536]{1,0:T(8,128)(2,1)S(1)} %get-tuple-element.153), channel_id=1, source_target_pairs={{0,4},{1,5},{2,6},{3,7},{4,0},{5,1},{6,2},{7,3},{8,12},{9,13},{10,... | collective-permute-start | bytes 1032200 | tf_op jit(solution)/shard_map/ppermute | solution.py:682
  146.8 24.0 %collective-permute-start.28 = (bf16[2,48,1536]{2,1,0:T(8,128)(2,1)}, bf16[2,48,1536]{2,1,0:T(8,128)(2,1)S(1)}, u32[]{:S(2)}, u32[]{:S(2)}) collective-permute-start(bf16[2,48,1536]{2,1,0:T(8,128)(2,1)} %copy-done.11), channel_id=1, source_target_pairs={{0,4},{1,5},{2,6},{3,7},{4,0},{5,1},{6,2},{7,3},{8,12},{9,13},{10,... | collective-permute-start | bytes 884744 | tf_op jit(solution)/shard_map/ppermute | solution.py:682
  163.5 10.9 %collective-permute-start.27 = (bf16[64,1536]{1,0:T(8,128)(2,1)S(1)}, bf16[64,1536]{1,0:T(8,128)(2,1)S(1)}, u32[]{:S(2)}, u32[]{:S(2)}) collective-permute-start(bf16[64,1536]{1,0:T(8,128)(2,1)S(1)} %get-tuple-element.157), channel_id=1, source_target_pairs={{0,8},{1,9},{2,10},{3,11},{4,12},{5,13},{6,14},{7,15},{8,0},{9,1},... | collective-permute-start | bytes 589832 | tf_op jit(solution)/shard_map/ppermute | solution.py:682
  167.9 7.3 %collective-permute-start.32 = (bf16[48,1536]{1,0:T(8,128)(2,1)S(1)}, bf16[48,1536]{1,0:T(8,128)(2,1)S(1)}, u32[]{:S(2)}, u32[]{:S(2)}) collective-permute-start(bf16[48,1536]{1,0:T(8,128)(2,1)S(1)} %pad_maximum_fusion.4), channel_id=1, source_target_pairs={{0,3},{1,2},{2,1},{3,0},{4,7},{5,6},{6,5},{7,4},{8,11},{9,10},{10,... | collective-permute-start | bytes 442376 | tf_op jit(solution)/shard_map/ppermute | solution.py:682
  168.0 7.4 %collective-permute-start.31 = (bf16[48,1536]{1,0:T(8,128)(2,1)S(1)}, bf16[48,1536]{1,0:T(8,128)(2,1)S(1)}, u32[]{:S(2)}, u32[]{:S(2)}) collective-permute-start(bf16[48,1536]{1,0:T(8,128)(2,1)S(1)} %pad_maximum_fusion.3), channel_id=1, source_target_pairs={{0,2},{1,3},{2,0},{3,1},{4,6},{5,7},{6,4},{7,5},{8,10},{9,11},{10,... | collective-permute-start | bytes 442376 | tf_op jit(solution)/shard_map/ppermute | solution.py:682
  168.6 6.8 %collective-permute-start.30 = (bf16[48,1536]{1,0:T(8,128)(2,1)S(1)}, bf16[48,1536]{1,0:T(8,128)(2,1)S(1)}, u32[]{:S(2)}, u32[]{:S(2)}) collective-permute-start(bf16[48,1536]{1,0:T(8,128)(2,1)S(1)} %pad_maximum_fusion.2), channel_id=1, source_target_pairs={{0,1},{1,0},{2,3},{3,2},{4,5},{5,4},{6,7},{7,6},{8,9},{9,8},{10,11... | collective-permute-start | bytes 442376 | tf_op jit(solution)/shard_map/ppermute | solution.py:682
  170.8 9.6 %collective-permute-start.29 = (bf16[48,1536]{1,0:T(8,128)(2,1)S(1)}, bf16[48,1536]{1,0:T(8,128)(2,1)S(1)}, u32[]{:S(2)}, u32[]{:S(2)}) collective-permute-start(bf16[48,1536]{1,0:T(8,128)(2,1)S(1)} %get-tuple-element.175), channel_id=1, source_target_pairs={{0,8},{1,9},{2,10},{3,11},{4,12},{5,13},{6,14},{7,15},{8,0},{9,1},... | collective-permute-start | bytes 442376 | tf_op jit(solution)/shard_map/ppermute | solution.py:682
